TPU v7x, 512 devices: a whole 4x4x16 slice. The times are simulated.
512 devices in a mesh: mem: 8 (over y, core), space: 64 (over z, x).
Axes of the slice: x: 4, y: 4, z: 16, core: 2. Of those that a mesh axis runs over, the one named last changes fastest.
Arguments:
- ensemble: bfloat16 [64, 160, 128, 128], P('mem', None, 'space'), may hold values from -6 to 6
- obs_value: float32 [64, 256], P('space'), may hold values from -6 to 6
- obs_error: float32 [64, 256], P('space'), may hold values from 0.3 to 3
- obs_cell: int32 [64, 256], P('space'), may hold values from 0 to 255
- obs_species: int32 [64, 256], P('space'), may hold values from 0 to 39
- patch_index: int32 [64, 256, 32], P('space', 'mem'), may hold values from 0 to 767, as said below
- patch_count: int32 [64, 256], P('space', 'mem'), may hold values from 1 to 32, as said below
- courant_x: float32 [4, 128, 128], P(None, 'space'), may hold values from -0.7 to 0.7
- courant_y: float32 [4, 128, 128], P(None, 'space'), may hold values from -0.7 to 0.7
- dep_velocity: float32 [40], replicated, may hold values from 0.05 to 0.5
- surface_factor: float32 [128, 128], P('space'), may hold values from 0.5 to 2
Outputs:
- forecast: bfloat16 [64, 160, 128, 128], P('mem', None, 'space')
Inputs may be any that keep to these rules, and one draw needn't show every extreme that they name: `patch_index`: each cell's list names distinct pool observations of existing tiles, nearest to the cell first; those within 3 cells of the cell come first. `patch_count`: the number of listed observations used for the cell, at least 1 and at most 32; the most is reached in every draw.
All inputs are finite; a program needn't handle non-finite values.
Results may differ from a plain program's by a relative error of at most 0.0049.
Values may be sent and summed in bfloat16 or wider, within the bound.
No kernel may reach another device: no remote copies, remote signals or barrier semaphores. Data moves between devices by JAX's collectives and lax.ppermute only.
A program may use at most 64 MiB of HBM per device.

v0:
```python
import functools
import math

import jax
import jax.numpy as jnp
from jax import lax
from jax.experimental import pallas as pl
from jax.experimental.pallas import tpu as pltpu
from jax.sharding import PartitionSpec as P

NEWTON = 8
SUBSTEPS = 2
LOC = 1
F32 = jnp.float32
BF16 = jnp.bfloat16
VMEM = pl.BlockSpec(memory_space=pltpu.VMEM)


def iota(shape, dim):
    return lax.broadcasted_iota(jnp.int32, shape, dim)


def split2(x):
    hi = x.astype(BF16)
    return hi, (x - hi.astype(F32)).astype(BF16)


def split3(x):
    hi = x.astype(BF16).astype(F32)
    mid = (x - hi).astype(BF16).astype(F32)
    return hi, mid, x - hi - mid


def mm(a, b):
    return jnp.dot(a, b, preferred_element_type=F32)


def mm_nt(a, b):
    return lax.dot_general(a, b, (((1,), (1,)), ((), ())), preferred_element_type=F32)


def block_rows(x, width):
    lane = iota(x.shape, 1) // width
    zero = jnp.zeros_like(x)
    return jnp.concatenate([jnp.where(lane == b, x, zero) for b in range(4)], axis=0)


def product(a2, b2, dot=mm):
    rows = a2[0].shape[0]
    first = dot(jnp.concatenate(a2, axis=0), b2[0])
    return first[:rows] + first[rows:] + dot(a2[0], b2[1])


def blocks2(x, width=64):
    hi, lo = split2(x)
    return block_rows(hi, width), block_rows(lo, width)


def weights_kernel(left, own, right, idx_ref, pos_ref, hi_ref, lo_ref, p_ref, z_ref, q_ref, tr_ref):
    members, maxobs, cells_g = 64, 32, 4
    groups = hi_ref.shape[0]
    parts = [left[...], own[...], right[...]]
    equiv = jnp.concatenate([p[:members] for p in parts], axis=1)
    info = jnp.concatenate([p[members : members + 8] for p in parts], axis=1)
    n_obs = info.shape[1]
    tile = n_obs // 3
    row_obs = info[2:3] + ((iota((1, n_obs), 1) // tile).astype(F32) - 1.0) * 2.0
    sub = iota((8, n_obs), 0)
    rows = [*split3(info[0:1]), *split3(info[1:2]), row_obs, info[3:4]]
    table = jnp.zeros((8, n_obs), F32)
    for r, line in enumerate(rows):
        table = jnp.where(sub == r, line, table)
    lhs = jnp.concatenate([equiv, table, jnp.zeros((8, n_obs), F32)], axis=0).astype(BF16)

    eye = (iota((members, 256), 0) == iota((members, 256), 1) % 64).astype(F32)
    spread = (iota((128, 256), 0) // maxobs == iota((128, 256), 1) // 64).astype(BF16)
    for half in range(groups // 2):
        sl = slice(half * 256, half * 256 + 256)
        idx = idx_ref[:, sl]
        onehot = (iota((n_obs, 256), 0) == idx).astype(F32).astype(BF16)
        got = mm(lhs, onehot)
        raw = got[:members]
        mean = jnp.sum(raw, axis=0, keepdims=True) * (1.0 / members)
        dev = raw - mean
        value = got[64:65] + got[65:66] + got[66:67]
        error = got[67:68] + got[68:69] + got[69:70]
        active = idx >= 0
        d2 = (got[70:71] - pos_ref[0:1, sl]) ** 2 + (got[71:72] - pos_ref[1:2, sl]) ** 2
        rho = jnp.where(
            active, jnp.exp(-d2 / (2.0 * LOC * LOC)) / jnp.where(active, error, 1.0), 0.0
        )
        scaled = dev * rho
        pull = rho * (value - mean)
        power = jnp.sum(dev * scaled, axis=0, keepdims=True)
        for part in range(2):
            g = half * 2 + part
            gs = slice(part * 128, part * 128 + 128)
            dev_g = dev[:, gs]
            lhs_g = jnp.concatenate(
                [scaled[:, gs], jnp.broadcast_to(pull[:, gs], (16, 128))], axis=0
            )
            both = product(split2(lhs_g), blocks2(dev_g, maxobs), mm_nt)
            sub16 = iota((16, 128), 0)
            p_hi, p_mid, p_lo = split3(power[:, gs])
            power3 = jnp.where(
                sub16 == 0, p_hi, jnp.where(sub16 == 1, p_mid, jnp.where(sub16 == 2, p_lo, 0.0))
            )
            trace = (members - 1.0) * members + jnp.sum(
                mm(power3.astype(BF16), spread), axis=0, keepdims=True
            )
            pmat = (both[:members] + (members - 1.0) * eye) / trace
            middle = 1.5 * eye - 0.5 * pmat
            p_ref[g] = product(split2(pmat), blocks2(middle))
            z_ref[g] = middle
            q_ref[g] = both[members : members + 8]
            tr_ref[g] = jnp.broadcast_to(trace, (8, 256))

    def step(_, carry):
        for g in range(groups):
            pmat, zmat = p_ref[g], z_ref[g]
            zs = split2(zmat)
            ps = split2(pmat)
            middle = 1.5 * eye - 0.5 * product(zs, tuple(block_rows(x, 64) for x in ps))
            ms = split2(middle)
            p_ref[g] = product(ps, tuple(block_rows(x, 64) for x in ms))
            z_ref[g] = product(ms, tuple(block_rows(x, 64) for x in zs))
        return carry

    lax.fori_loop(0, NEWTON - 2, step, 0)
    for g in range(groups):
        pmat, zmat = p_ref[g], z_ref[g]
        middle = 1.5 * eye - 0.5 * product(split2(zmat), blocks2(pmat))
        root = product(split2(middle), blocks2(zmat))
        trace = tr_ref[g][:1]
        blocks = blocks2(root)
        q16 = jnp.concatenate([q_ref[g], q_ref[g]], axis=0)
        pulled = product(split2(product(split2(q16), blocks)), blocks)[:1] / trace
        scale = math.sqrt(members - 1.0) / jnp.sqrt(trace)
        p0 = (members - 1.0) / trace
        z0 = jnp.ones_like(p0)
        for _ in range(NEWTON):
            m0 = 1.5 - 0.5 * z0 * p0
            p0 = p0 * m0
            z0 = m0 * z0
        full = scale * root + (pulled + (1.0 - scale * z0) * (1.0 / members))
        hi, lo = split2(full)
        hi_ref[g] = hi
        lo_ref[g] = lo


def transform_kernel(hi_ref, lo_ref, x_ref, *refs):
    outs, scr = refs[:-1], refs[-1]
    groups = hi_ref.shape[0]
    per = 32
    for g in range(groups):
        lhs = jnp.concatenate([block_rows(hi_ref[g], 64), block_rows(lo_ref[g], 64)], axis=0)
        x = jnp.concatenate(
            [x_ref[:, g * 4 + c].astype(F32).reshape(64, 256) for c in range(4)], axis=0
        ).astype(BF16)
        out = mm(lhs, x)
        for c in range(4):
            scr_val = out[c * 64 : c * 64 + 64] + out[256 + c * 64 : 256 + c * 64 + 64]
            scr[0, pl.ds(g * 4 + c, 64, stride=per), :] = scr_val[:, :128]
            scr[1, pl.ds(g * 4 + c, 64, stride=per), :] = scr_val[:, 128:]
    lane = iota((8, 128), 1) // 32
    chunk = 8 // len(outs)
    for dest in range(8):
        for ml in range(8):
            base = (dest * 8 + ml) * per
            main = scr[0, base : base + per, :]
            rest = jnp.zeros((8, 128), F32)
            for cc in range(4):
                piece = scr[1, base + cc * 8 : base + cc * 8 + 8, :]
                piece = pltpu.roll(piece, 32 * cc, 1) if cc else piece
                rest = jnp.where(lane == cc, piece, rest)
            outs[ml // chunk][dest, ml % chunk] = jnp.concatenate([main, rest, jnp.zeros_like(rest)], axis=0)[:48].astype(BF16)[:40]


def relayout_kernel(x_ref, o_ref):
    fields = o_ref.shape[2]
    ident = (iota((fields, 256), 0) == iota((fields, 256), 1)).astype(F32).astype(BF16)
    for row in range(2):
        for ml in range(x_ref.shape[1]):
            mains, rests = [], []
            for q in range(4):
                block = x_ref[row * 4 + q, ml].astype(F32)
                mains.append(block[:32])
                tail = block[32:40]
                for cc in range(4):
                    rests.append(pltpu.roll(tail, 128 - 32 * cc, 1) if cc else tail)
            full = jnp.concatenate(
                [jnp.concatenate(mains, axis=0), jnp.concatenate(rests, axis=0)], axis=1
            ).astype(BF16)
            o_ref[row, ml] = mm_nt(ident, full).astype(BF16)


def advect_kernel(low_ref, own_ref, high_ref, cl_ref, co_ref, ch_ref, dep_ref, surf_ref, o_ref, fac):
    members, fields = own_ref.shape[1], own_ref.shape[2]
    lane = iota((8, 128), 1)

    def coeffs(c):
        half, sq = 0.5 * c, 0.5 * c * c
        return half + sq, 1.0 - c * c, sq - half

    courant = [(cl_ref, 1), (co_ref, 0), (co_ref, 1), (ch_ref, 0)]
    cy = [coeffs(r[1, k]) for r, k in courant]
    cx = []
    for r, k in courant:
        a, b, c = coeffs(r[0, k])
        cx.append((jnp.where(lane == 0, 0.0, a), b, jnp.where(lane == 127, 0.0, c)))
    for row in range(2):
        fac[row] = jnp.exp(-dep_ref[...] * surf_ref[row : row + 1, :])

    def rows(south, mid, north, k):
        a, b, c = cy[k]
        return a * south + b * mid + c * north

    def cols(q, k):
        a, b, c = cx[k]
        return a * pltpu.roll(q, 1, 1) + b * q + c * pltpu.roll(q, 127, 1)

    def member(m, carry):
        for f in range(0, fields, 16):
            pieces = [[], []]
            loads = [
                r[k, m, f : f + 16].astype(F32)
                for r, k in [
                    (low_ref, 0), (low_ref, 1), (own_ref, 0),
                    (own_ref, 1), (high_ref, 0), (high_ref, 1),
                ]
            ]
            for h in (0, 8):
                q = [x[h : h + 8] for x in loads]
                q1 = [cols(rows(q[i], q[i + 1], q[i + 2], i), i) for i in range(4)]
                for r in range(2):
                    q2 = cols(rows(q1[r], q1[r + 1], q1[r + 2], r + 1), r + 1)
                    pieces[r].append(q2 * fac[r, f + h : f + h + 8])
            for r in range(2):
                o_ref[r, m, f : f + 16] = jnp.concatenate(pieces[r], axis=0).astype(BF16)
        return carry

    lax.fori_loop(0, members, member, 0)


def call(kernel, outs, scratch=(), flops=10**8, nbytes=10**6):
    return pl.pallas_call(
        kernel,
        out_shape=outs,
        scratch_shapes=list(scratch),
        compiler_params=pltpu.CompilerParams(vmem_limit_bytes=40 << 20),
        cost_estimate=pl.CostEstimate(flops=flops, bytes_accessed=nbytes, transcendentals=0),
    )


def from_low(x):
    count = lax.axis_size("space")
    return lax.ppermute(x, "space", [(i, i + 1) for i in range(count - 1)])


def from_high(x):
    count = lax.axis_size("space")
    return lax.ppermute(x, "space", [(i + 1, i) for i in range(count - 1)])


def shards(
    ensemble,
    obs_value,
    obs_error,
    obs_cell,
    obs_species,
    patch_index,
    patch_count,
    courant_x,
    courant_y,
    dep_velocity,
    surface_factor,
):
    local, fields, tile_rows, columns = ensemble.shape
    species = dep_velocity.shape[0]
    levels = fields // species
    n_obs = obs_cell.shape[1]
    per = patch_index.shape[1]
    maxobs = patch_index.shape[2]
    groups_mem = 8

    surface = ensemble.reshape(local, species, levels, tile_rows, columns)[:, :, 0]
    cell = obs_cell[0]
    pick = (
        jnp.arange(tile_rows * columns, dtype=jnp.int32)[:, None] == cell[None, :]
    ).astype(BF16)
    at_cell = jnp.dot(
        surface.reshape(local * species, tile_rows * columns), pick, preferred_element_type=F32
    ).reshape(local, species, n_obs)
    chosen = jnp.arange(species, dtype=jnp.int32)[:, None] == obs_species
    equiv = jnp.sum(jnp.where(chosen[None], at_cell, 0.0), axis=1)
    everywhere = lax.all_to_all(
        jnp.broadcast_to(equiv[None], (groups_mem, local, n_obs)), "mem", 0, 0, tiled=True
    ).reshape(groups_mem * local, n_obs)

    wind = jnp.stack([courant_x, courant_y])
    packed = jnp.concatenate(
        [
            everywhere,
            obs_value,
            obs_error,
            (obs_cell // columns).astype(F32),
            (obs_cell % columns).astype(F32),
            jnp.zeros((4, n_obs), F32),
            wind.reshape(8, 256),
        ],
        axis=0,
    )
    low, high = from_low(packed), from_high(packed)

    payload = ensemble.reshape(local, fields, tile_rows, 4, per)
    payload = jnp.pad(payload, ((0, 0), (0, 256 - fields), (0, 0), (0, 0), (0, 0)))
    payload = jnp.transpose(payload, (2, 3, 4, 0, 1)).reshape(groups_mem, per, local, 256)
    state = lax.all_to_all(payload, "mem", 0, 0, tiled=True)

    used = jnp.arange(maxobs, dtype=jnp.int32)[None, :] < patch_count[0][:, None]
    idx = jnp.where(used, patch_index[0], -1).reshape(1, per * maxobs)
    cell_id = lax.axis_index("mem") * per + jnp.arange(per, dtype=jnp.int32)
    cell_id = jnp.broadcast_to(cell_id[:, None], (per, maxobs)).reshape(1, per * maxobs)
    pos = jnp.concatenate([cell_id // columns, cell_id % columns], axis=0).astype(F32)

    groups = per // 4
    hi, lo = call(
        weights_kernel,
        [jax.ShapeDtypeStruct((groups, 64, 256), BF16)] * 2,
        [
            pltpu.VMEM((groups, 64, 256), F32),
            pltpu.VMEM((groups, 64, 256), F32),
            pltpu.VMEM((groups, 8, 256), F32),
            pltpu.VMEM((groups, 8, 256), F32),
        ],
        flops=10**10,
    )(low[:72], packed[:72], high[:72], idx, pos)
    back = call(
        transform_kernel,
        [jax.ShapeDtypeStruct((groups_mem, local, 40, 128), BF16)],
        [pltpu.VMEM((2, 64 * per, 128), F32)],
        flops=10**9,
    )(hi, lo, state)[0]
    returned = lax.all_to_all(back, "mem", 0, 0, tiled=True)
    planes = call(
        relayout_kernel,
        jax.ShapeDtypeStruct((tile_rows, local, fields, columns), BF16),
        flops=10**9,
    )(returned)
    below, above = from_low(planes), from_high(planes)

    def rims(array):
        wind_now = array[72:80].reshape(2, levels, tile_rows, columns)
        wind_now = jnp.transpose(wind_now, (0, 2, 1, 3))
        return jnp.concatenate([wind_now, wind_now], axis=2)

    rate = jnp.where(
        (jnp.arange(fields, dtype=jnp.int32) % levels == 0)[:, None],
        jnp.repeat(dep_velocity, levels)[:, None],
        0.0,
    )
    done = call(
        advect_kernel,
        jax.ShapeDtypeStruct((tile_rows, local, fields, columns), BF16),
        [pltpu.VMEM((tile_rows, fields, columns), F32)],
        flops=10**8,
    )(below, planes, above, rims(low), rims(packed), rims(high), rate, surface_factor)
    return jnp.transpose(done, (1, 2, 0, 3))


def solution(mesh):
    in_specs = (
        P("mem", None, "space", None),
        P("space", None),
        P("space", None),
        P("space", None),
        P("space", None),
        P("space", "mem", None),
        P("space", "mem"),
        P(None, "space", None),
        P(None, "space", None),
        P(),
        P("space", None),
    )
    out_specs = P("mem", None, "space", None)
    return jax.shard_map(shards, mesh=mesh, in_specs=in_specs, out_specs=out_specs, check_vma=False)
```

profile of v0, /device:TPU:384, one launch (start us, length us, event | category | flops | bytes accessed | tf_op | source)
XLA Modules:
  0.0 105.7 jit_solution(683951999528689453)
XLA Ops:
  0.0 0.7 copy-done.8
  0.7 1.1 %slice.22 = bf16[8,40,1,2,128]{4,3,2,1,0:T(2,128)(2,1)S(1)} slice(bf16[8,40,4,2,128]{4,3,2,1,0:T(2,128)(2,1)} %bitcast.38), slice={[0:8], [0:40], [0:1], [0:2], [0:128]} | slice | bytes 327680 | tf_op jit(solution)/shard_map/slice | solution.py:286
  1.8 0.2 fusion
  2.1 0.6 broadcast_in_dim.45
  2.7 4.5 %all-to-all-start = ((f32[8,8,256]{2,1,0:T(8,128)}), f32[8,8,256]{2,1,0:T(8,128)S(1)}, u32[]{:S(2)}, u32[]{:S(2)}) async-start(f32[8,8,256]{2,1,0:T(8,128)} %broadcast_in_dim.45), calls=%async_computation | async-start | bytes 131072 | tf_op jit(solution)/shard_map/all_to_all | solution.py:296
  7.2 1.9 %copy.19 = bf16[8,160,2,128]{1,3,2,0:T(8,128)(2,1)S(1)} copy(bf16[8,160,2,128]{3,2,1,0:T(2,128)(2,1)S(1)} %copy-done.1) | data formatting | bytes 1310720 | tf_op args[0]
  9.2 0.1 squeeze.3
  9.3 0.7 copy-done.9
  9.9 0.1 iota_compare_fusion.3
  10.0 0.1 lt.48
  10.2 0.1 reshape.269
  10.3 0.3 pad_bitcast_fusion
  10.6 0.6 copy-done.6
  11.3 1.6 %copy.20 = bf16[2,4,32,8,256]{4,3,2,1,0:T(8,128)(2,1)} copy(bf16[2,4,32,8,256]{4,2,1,0,3:T(8,128)(2,1)S(1)} %pad_bitcast_fusion) | data formatting | bytes 2097152 | tf_op jit(solution)/shard_map/transpose | solution.py:317
  12.9 4.8 %all-to-all-start.1 = ((bf16[8,32,8,256]{3,2,1,0:T(8,128)(2,1)}), bf16[8,32,8,256]{3,2,1,0:T(8,128)(2,1)S(1)}, u32[]{:S(2)}, u32[]{:S(2)}) async-start(bf16[8,32,8,256]{3,2,1,0:T(8,128)(2,1)} %bitcast.11), calls=%async_computation.1 | async-start | bytes 2097152 | tf_op jit(solution)/shard_map/all_to_all | solution.py:318
  17.8 0.7 copy-done.4
  18.5 6.3 %collective-permute-start.1 = (f32[80,256]{1,0:T(8,128)S(1)}, f32[80,256]{1,0:T(8,128)S(1)}, u32[]{:S(2)}, u32[]{:S(2)}) collective-permute-start(f32[80,256]{1,0:T(8,128)S(1)} %concatenate.18), channel_id=1, source_target_pairs={{1,0},{2,1},{3,2},{4,3},{5,4},{6,5},{7,6},{8,7},{9,8},{10,9},{11,1... | collective-permute-start | bytes 245768 | tf_op jit(solution)/shard_map/ppermute | solution.py:262
  24.8 1.9 %collective-permute-start = (f32[80,256]{1,0:T(8,128)S(1)}, f32[80,256]{1,0:T(8,128)S(1)}, u32[]{:S(2)}, u32[]{:S(2)}) collective-permute-start(f32[80,256]{1,0:T(8,128)S(1)} %concatenate.18), channel_id=1, source_target_pairs={{0,1},{1,2},{2,3},{3,4},{4,5},{5,6},{6,7},{7,8},{8,9},{9,10},{10,1... | collective-permute-start | bytes 245768 | tf_op jit(solution)/shard_map/ppermute | solution.py:257
  26.8 0.4 collective-permute-done.1
  27.1 7.4 %collective-permute-done = f32[80,256]{1,0:T(8,128)S(1)} collective-permute-done((f32[80,256]{1,0:T(8,128)S(1)}, f32[80,256]{1,0:T(8,128)S(1)}, u32[]{:S(2)}, u32[]{:S(2)}) %collective-permute-start) | collective-permute-done | bytes 81952 | tf_op jit(solution)/shard_map/ppermute | solution.py:257
  34.6 19.8 %shard_map.112 = (bf16[8,64,256]{2,1,0:T(8,128)(2,1)S(1)}, bf16[8,64,256]{2,1,0:T(8,128)(2,1)S(1)}) custom-call(f32[72,256]{1,0:T(8,128)S(1)} %slice.23.left, f32[72,256]{1,0:T(8,128)S(1)} %concatenate.19.own, f32[72,256]{1,0:T(8,128)S(1)} %slice.24.right, s32[1,1024]{1,0:T(1,128)S(1)} %broadcast_select_fusion.idx_ref, f32[2,1024]{1,0:T(2,128)S(1)} %add_convert_fusion.pos_ref), custom_call_target="tpu_custom_call" | custom-call | flops 10000000000 | bytes 1000000 | tf_op jit(solution)/shard_map/pallas_call | solution.py:327
  54.4 2.1 %shard_map.113 = bf16[8,8,40,128]{3,2,1,0:T(8,128)(2,1)S(1)} custom-call(bf16[8,64,256]{2,1,0:T(8,128)(2,1)S(1)} %get-tuple-element.7.hi_ref, bf16[8,64,256]{2,1,0:T(8,128)(2,1)S(1)} %get-tuple-element.8.lo_ref, bf16[8,32,8,256]{3,2,1,0:T(8,128)(2,1)S(1)} %all-to-all-done.1.x_ref), custom_call_target="tpu_custom_call" | custom-call | flops 1000000000 | bytes 1000000 | tf_op jit(solution)/shard_map/pallas_call | solution.py:338
  56.4 16.3 %all_to_all.15.x_ref = bf16[8,8,40,128]{3,2,1,0:T(8,128)(2,1)S(1)} all-to-all(bf16[8,8,40,128]{3,2,1,0:T(8,128)(2,1)S(1)} %shard_map.113), channel_id=1, replica_groups=mesh['mem'=8,'space'=64] {'mem'}, dimensions={0} | all-to-all | bytes 1310720 | tf_op jit(solution)/shard_map/all_to_all | solution.py:344
  72.7 0.6 shard_map.114.own_ref
  73.3 1.9 %collective-permute-start.3 = (bf16[2,8,160,128]{3,2,1,0:T(8,128)(2,1)S(1)}, bf16[2,8,160,128]{3,2,1,0:T(8,128)(2,1)S(1)}, u32[]{:S(2)}, u32[]{:S(2)}) collective-permute-start(bf16[2,8,160,128]{3,2,1,0:T(8,128)(2,1)S(1)} %shard_map.114.own_ref), channel_id=1, source_target_pairs={{1,0},{2,1},{3,2},{4,3},{5,4},{6,5},{7,6},{8,7},{9,8},{10,9},{11,1... | collective-permute-start | bytes 1966088 | tf_op jit(solution)/shard_map/ppermute | solution.py:262
  75.2 3.9 %collective-permute-start.2 = (bf16[2,8,160,128]{3,2,1,0:T(8,128)(2,1)S(1)}, bf16[2,8,160,128]{3,2,1,0:T(8,128)(2,1)S(1)}, u32[]{:S(2)}, u32[]{:S(2)}) collective-permute-start(bf16[2,8,160,128]{3,2,1,0:T(8,128)(2,1)S(1)} %shard_map.114.own_ref), channel_id=1, source_target_pairs={{0,1},{1,2},{2,3},{3,4},{4,5},{5,6},{6,7},{7,8},{8,9},{9,10},{10,1... | collective-permute-start | bytes 1966088 | tf_op jit(solution)/shard_map/ppermute | solution.py:257
  79.2 0.1 broadcast_in_dim.49
  79.2 0.1 broadcast_in_dim_reshape.4
  79.5 12.0 %collective-permute-done.3.high_ref = bf16[2,8,160,128]{3,2,1,0:T(8,128)(2,1)S(1)} collective-permute-done((bf16[2,8,160,128]{3,2,1,0:T(8,128)(2,1)S(1)}, bf16[2,8,160,128]{3,2,1,0:T(8,128)(2,1)S(1)}, u32[]{:S(2)}, u32[]{:S(2)}) %collective-permute-start.3) | collective-permute-done | bytes 655392 | tf_op jit(solution)/shard_map/ppermute | solution.py:262
  91.5 5.2 %collective-permute-done.2.low_ref = bf16[2,8,160,128]{3,2,1,0:T(8,128)(2,1)S(1)} collective-permute-done((bf16[2,8,160,128]{3,2,1,0:T(8,128)(2,1)S(1)}, bf16[2,8,160,128]{3,2,1,0:T(8,128)(2,1)S(1)}, u32[]{:S(2)}, u32[]{:S(2)}) %collective-permute-start.2) | collective-permute-done | bytes 655392 | tf_op jit(solution)/shard_map/ppermute | solution.py:257
  96.7 7.4 %shard_map.115 = bf16[2,8,160,128]{3,2,1,0:T(8,128)(2,1)S(1)} custom-call(bf16[2,8,160,128]{3,2,1,0:T(8,128)(2,1)S(1)} %collective-permute-done.2.low_ref, bf16[2,8,160,128]{3,2,1,0:T(8,128)(2,1)S(1)} %shard_map.114.own_ref, bf16[2,8,160,128]{3,2,1,0:T(8,128)(2,1)S(1)} %collective-permute-done.3.high_ref, f32[2,2,8,128]{3,2,1,0:T(8,128)S(1)} %pad_maximum_fusion.cl_ref, ...), custom_call_target="tpu_custom_call" | custom-call | flops 100000000 | bytes 1000000 | tf_op jit(solution)/shard_map/pallas_call | solution.py:362
  104.2 1.5 %copy.24 = bf16[8,160,2,128]{3,2,1,0:T(2,128)(2,1)} copy(bf16[8,160,2,128]{3,1,0,2:T(8,128)(2,1)S(1)} %bitcast.35) | data formatting | bytes 1310720 | tf_op jit(solution)/shard_map/transpose | solution.py:368
  (49 shorter events, 0.5 us)
Async XLA Ops:
  0.0 0.7 copy-start.8
  0.7 1.1 %copy-start.3 = (s32[1,256]{1,0:T(1,128)S(1)}, s32[1,256]{1,0:T(1,128)}, u32[]{:S(2)}) copy-start(s32[1,256]{1,0:T(1,128)} %param.14) | copy-start | bytes 3076
  0.7 6.5 %copy-start.1 = (bf16[8,160,2,128]{3,2,1,0:T(2,128)(2,1)S(1)}, bf16[8,160,2,128]{3,2,1,0:T(2,128)(2,1)}, u32[]{:S(2)}) copy-start(bf16[8,160,2,128]{3,2,1,0:T(2,128)(2,1)} %param.11) | copy-start | bytes 1966084
  2.7 10.2 %all-to-all-start = ((f32[8,8,256]{2,1,0:T(8,128)}), f32[8,8,256]{2,1,0:T(8,128)S(1)}, u32[]{:S(2)}, u32[]{:S(2)}) async-start(f32[8,8,256]{2,1,0:T(8,128)} %broadcast_in_dim.45), calls=%async_computation | async-start | bytes 131072 | tf_op jit(solution)/shard_map/all_to_all | solution.py:296
  7.2 2.0 %copy-start.2 = (s32[1,32,32]{2,1,0:T(8,128)S(1)}, s32[1,32,32]{2,1,0:T(8,128)}, u32[]{:S(2)}) copy-start(s32[1,32,32]{2,1,0:T(8,128)} %param.16) | copy-start | bytes 12292
  9.3 0.7 copy-start.9
  10.6 0.7 copy-start.6
  10.6 0.7 copy-start.7
  12.9 41.5 %all-to-all-start.1 = ((bf16[8,32,8,256]{3,2,1,0:T(8,128)(2,1)}), bf16[8,32,8,256]{3,2,1,0:T(8,128)(2,1)S(1)}, u32[]{:S(2)}, u32[]{:S(2)}) async-start(bf16[8,32,8,256]{3,2,1,0:T(8,128)(2,1)} %bitcast.11), calls=%async_computation.1 | async-start | bytes 2097152 | tf_op jit(solution)/shard_map/all_to_all | solution.py:318
  17.7 0.7 copy-start.4
  17.7 0.7 copy-start.5
  18.5 8.7 %collective-permute-start.1 = (f32[80,256]{1,0:T(8,128)S(1)}, f32[80,256]{1,0:T(8,128)S(1)}, u32[]{:S(2)}, u32[]{:S(2)}) collective-permute-start(f32[80,256]{1,0:T(8,128)S(1)} %concatenate.18), channel_id=1, source_target_pairs={{1,0},{2,1},{3,2},{4,3},{5,4},{6,5},{7,6},{8,7},{9,8},{10,9},{11,1... | collective-permute-start | bytes 245768 | tf_op jit(solution)/shard_map/ppermute | solution.py:262
  24.8 9.8 %collective-permute-start = (f32[80,256]{1,0:T(8,128)S(1)}, f32[80,256]{1,0:T(8,128)S(1)}, u32[]{:S(2)}, u32[]{:S(2)}) collective-permute-start(f32[80,256]{1,0:T(8,128)S(1)} %concatenate.18), channel_id=1, source_target_pairs={{0,1},{1,2},{2,3},{3,4},{4,5},{5,6},{6,7},{7,8},{8,9},{9,10},{10,1... | collective-permute-start | bytes 245768 | tf_op jit(solution)/shard_map/ppermute | solution.py:257
  72.7 6.4 %copy-start.10 = (f32[40]{0:T(128)S(1)}, f32[40]{0:T(128)}, u32[]{:S(2)}) copy-start(f32[40]{0:T(128)} %param.20) | copy-start | bytes 484
  73.3 18.2 %collective-permute-start.3 = (bf16[2,8,160,128]{3,2,1,0:T(8,128)(2,1)S(1)}, bf16[2,8,160,128]{3,2,1,0:T(8,128)(2,1)S(1)}, u32[]{:S(2)}, u32[]{:S(2)}) collective-permute-start(bf16[2,8,160,128]{3,2,1,0:T(8,128)(2,1)S(1)} %shard_map.114.own_ref), channel_id=1, source_target_pairs={{1,0},{2,1},{3,2},{4,3},{5,4},{6,5},{7,6},{8,7},{9,8},{10,9},{11,1... | collective-permute-start | bytes 1966088 | tf_op jit(solution)/shard_map/ppermute | solution.py:262
  75.2 21.5 %collective-permute-start.2 = (bf16[2,8,160,128]{3,2,1,0:T(8,128)(2,1)S(1)}, bf16[2,8,160,128]{3,2,1,0:T(8,128)(2,1)S(1)}, u32[]{:S(2)}, u32[]{:S(2)}) collective-permute-start(bf16[2,8,160,128]{3,2,1,0:T(8,128)(2,1)S(1)} %shard_map.114.own_ref), channel_id=1, source_target_pairs={{0,1},{1,2},{2,3},{3,4},{4,5},{5,6},{6,7},{7,8},{8,9},{9,10},{10,1... | collective-permute-start | bytes 1966088 | tf_op jit(solution)/shard_map/ppermute | solution.py:257
  79.4 17.3 %copy-start = (f32[2,128]{1,0:T(2,128)S(1)}, f32[2,128]{1,0:T(2,128)}, u32[]{:S(2)}) copy-start(f32[2,128]{1,0:T(2,128)} %surf_ref.1) | copy-start | bytes 3076
where the time goes:
time: 106 us
  Pallas kernels  29.9 us (28%)
  waiting for transfers between devices  25.1 us (24%)
  starting transfers between devices  23.4 us (22%)
  blocking collectives  16.3 us (15%)
  local copies, waits for them, and re-layouts  10.3 us (10%)
    pallas_call x1, Pallas kernels, shards(): call(weights_kernel, [jax.ShapeDtypeStruct((groups, 64, 256), BF16)] * 2,...  19.8 us
    all_to_all x1, blocking collectives, shards(): returned = lax.all_to_all(back, 'mem', 0, 0, tiled=True)  16.3 us
    ppermute x2, waiting for transfers between devices, from_low(): return lax.ppermute(x, 'space', [(i, i + 1) for i in range(count - 1)])  12.7 us
    ppermute x2, waiting for transfers between devices, from_high(): return lax.ppermute(x, 'space', [(i + 1, i) for i in range(count - 1)])  12.4 us
    ppermute x2, starting transfers between devices, from_high(): return lax.ppermute(x, 'space', [(i + 1, i) for i in range(count - 1)])  8.24 us
    pallas_call x1, Pallas kernels, shards(): call(advect_kernel, jax.ShapeDtypeStruct((tile_rows, local, fields, colum...  7.43 us
    ppermute x2, starting transfers between devices, from_low(): return lax.ppermute(x, 'space', [(i, i + 1) for i in range(count - 1)])  5.84 us
    all_to_all x1, starting transfers between devices, shards(): state = lax.all_to_all(payload, 'mem', 0, 0, tiled=True)  4.8 us
  transfers between devices with their start and end apart: 6, of which 4 were waited for; matrix products, arithmetic and copies ran while one was open for 4% of the time, Pallas kernels for 19%

commit v1 on v0

v1 whole, which is shorter than its diff:
```python
import functools
import math

import jax
import jax.numpy as jnp
from jax import lax
from jax.experimental import pallas as pl
from jax.experimental.pallas import tpu as pltpu
from jax.sharding import PartitionSpec as P

NEWTON = 8
SUBSTEPS = 2
LOC = 1
F32 = jnp.float32
BF16 = jnp.bfloat16
VMEM = pl.BlockSpec(memory_space=pltpu.VMEM)


def iota(shape, dim):
    return lax.broadcasted_iota(jnp.int32, shape, dim)


def split2(x):
    hi = x.astype(BF16)
    return hi, (x - hi.astype(F32)).astype(BF16)


def split3(x):
    hi = x.astype(BF16).astype(F32)
    mid = (x - hi).astype(BF16).astype(F32)
    return hi, mid, x - hi - mid


def mm(a, b):
    return jnp.dot(a, b, preferred_element_type=F32)


def mm_nt(a, b):
    return lax.dot_general(a, b, (((1,), (1,)), ((), ())), preferred_element_type=F32)


def block_rows(x, width):
    lane = iota(x.shape, 1) // width
    zero = jnp.zeros_like(x)
    return jnp.concatenate(
        [jnp.where(lane == b, x, zero) for b in range(x.shape[1] // width)], axis=0
    )


def product(a2, b2, dot=mm):
    rows = a2[0].shape[0]
    first = dot(jnp.concatenate(a2, axis=0), b2[0])
    return first[:rows] + first[rows:] + dot(a2[0], b2[1])


def blocks2(x, width):
    hi, lo = split2(x)
    return block_rows(hi, width), block_rows(lo, width)


def side_by_side(x):
    return jnp.concatenate(split2(x), axis=1)


def paired(x, masks):
    cols = [jnp.concatenate([part * masks[0], part * masks[1]], axis=0) for part in split2(x)]
    once = jnp.concatenate(cols, axis=1)
    return jnp.concatenate([once, once], axis=0)


def pair_product(a, b):
    out = mm(a, b)
    return out[:, :128] + out[:, 128:]


def weights_kernel(left, own, right, idx_ref, pos_ref, hi_ref, lo_ref, t_ref, z_ref, m_ref, q_ref, tr_ref):
    members, maxobs = 64, 32
    pairs = t_ref.shape[0]
    parts = [left[...], own[...], right[...]]
    equiv = jnp.concatenate([p[:members] for p in parts], axis=1)
    info = jnp.concatenate([p[members : members + 8] for p in parts], axis=1)
    n_obs = info.shape[1]
    tile = n_obs // 3
    row_obs = info[2:3] + ((iota((1, n_obs), 1) // tile).astype(F32) - 1.0) * 2.0
    sub = iota((8, n_obs), 0)
    rows = [*split3(info[0:1]), *split3(info[1:2]), row_obs, info[3:4]]
    table = jnp.zeros((8, n_obs), F32)
    for r, line in enumerate(rows):
        table = jnp.where(sub == r, line, table)
    lhs = jnp.concatenate([equiv, table, jnp.zeros((8, n_obs), F32)], axis=0).astype(BF16)

    eye = (iota((members, 128), 0) == iota((members, 128), 1) % 64).astype(F32)
    eye2 = jnp.concatenate([eye, eye], axis=1)
    spread = (iota((128, 256), 0) // maxobs == iota((128, 256), 1) // 64).astype(BF16)
    lane = iota((members, 128), 1)
    masks = [(lane < 64).astype(F32).astype(BF16), (lane >= 64).astype(F32).astype(BF16)]
    quarters = range(pairs // 4)
    sls = [slice(n * 256, n * 256 + 256) for n in quarters]
    gots = []
    for sl in sls:
        onehot = (iota((n_obs, 256), 0) == idx_ref[:, sl]).astype(F32).astype(BF16)
        gots.append(mm(lhs, onehot))
    grams = []
    for sl, got in zip(sls, gots):
        raw = got[:members]
        mean = jnp.sum(raw, axis=0, keepdims=True) * (1.0 / members)
        dev = raw - mean
        value = got[64:65] + got[65:66] + got[66:67]
        error = got[67:68] + got[68:69] + got[69:70]
        active = idx_ref[:, sl] >= 0
        d2 = (got[70:71] - pos_ref[0:1, sl]) ** 2 + (got[71:72] - pos_ref[1:2, sl]) ** 2
        rho = jnp.where(
            active, jnp.exp(-d2 / (2.0 * LOC * LOC)) / jnp.where(active, error, 1.0), 0.0
        )
        scaled = dev * rho
        pull = rho * (value - mean)
        power = jnp.sum(dev * scaled, axis=0, keepdims=True)
        for part in range(2):
            gs = slice(part * 128, part * 128 + 128)
            lhs_g = jnp.concatenate(
                [scaled[:, gs], jnp.broadcast_to(pull[:, gs], (16, 128))], axis=0
            )
            both = product(split2(lhs_g), blocks2(dev[:, gs], maxobs), mm_nt)
            sub16 = iota((16, 128), 0)
            p_hi, p_mid, p_lo = split3(power[:, gs])
            power3 = jnp.where(
                sub16 == 0, p_hi, jnp.where(sub16 == 1, p_mid, jnp.where(sub16 == 2, p_lo, 0.0))
            )
            grams.append((both, mm(power3.astype(BF16), spread)))
    for g, (both, powers) in enumerate(grams):
        trace = (members - 1.0) * members + jnp.sum(powers, axis=0, keepdims=True)
        pmat = (both[:members] + (members - 1.0) * eye2) * (1.0 / trace)
        for k in range(2):
            ks = slice(k * 128, k * 128 + 128)
            p = g * 2 + k
            t_ref[p] = pmat[:, ks]
            q_ref[p] = both[members : members + 16, ks]
            tr_ref[p] = jnp.broadcast_to(trace[:, ks], (8, 128))
    for p in range(pairs):
        middle = 1.5 * eye - 0.5 * t_ref[p]
        rows_m = jnp.concatenate([middle, q_ref[p]], axis=0)
        out = pair_product(side_by_side(rows_m), paired(middle, masks))
        z_ref[p] = middle
        q_ref[p] = out[members:]
        m_ref[p] = out[:members]
    for p in range(pairs):
        t_ref[p] = pair_product(side_by_side(t_ref[p]), paired(m_ref[p], masks))

    def step(_, carry):
        for p in range(pairs):
            middle = 1.5 * eye - 0.5 * t_ref[p]
            rows_m = jnp.concatenate([middle, z_ref[p], q_ref[p]], axis=0)
            out = pair_product(side_by_side(rows_m), paired(middle, masks))
            m_ref[p] = out[:members]
            z_ref[p] = out[members : 2 * members]
            q_ref[p] = out[2 * members :]
        for p in range(pairs):
            t_ref[p] = pair_product(side_by_side(t_ref[p]), paired(m_ref[p], masks))
        return carry

    lax.fori_loop(0, NEWTON - 2, step, 0)
    for p in range(pairs):
        middle = 1.5 * eye - 0.5 * t_ref[p]
        rows_z = jnp.concatenate([z_ref[p], q_ref[p]], axis=0)
        out = pair_product(side_by_side(rows_z), paired(middle, masks))
        z_ref[p] = out[:members]
        q_ref[p] = out[members:]
    for p in range(pairs):
        root = z_ref[p]
        trace = tr_ref[p][:1]
        pulled = pair_product(side_by_side(q_ref[p]), paired(root, masks))[:1] / trace
        scale = math.sqrt(members - 1.0) / jnp.sqrt(trace)
        p0 = (members - 1.0) / trace
        z0 = jnp.ones_like(p0)
        for _ in range(NEWTON):
            m0 = 1.5 - 0.5 * z0 * p0
            p0 = p0 * m0
            z0 = m0 * z0
        full = scale * root + (pulled + (1.0 - scale * z0) * (1.0 / members))
        hi, lo = split2(full)
        ks = slice((p % 2) * 128, (p % 2) * 128 + 128)
        hi_ref[p // 2, :, ks] = hi
        lo_ref[p // 2, :, ks] = lo


def equivalents_kernel(planes, cell, kind, value, error, wind_x, wind_y, o_ref, info, *scratch):
    local, fields = planes.shape[1], planes.shape[2]
    n_obs = o_ref.shape[2]
    sems, buf_i, buf_f, buf_w = scratch
    jobs = [(cell, buf_i.at[0]), (kind, buf_i.at[1]), (value, buf_f.at[0]), (error, buf_f.at[1])]
    jobs += [(wind_x, buf_w.at[0]), (wind_y, buf_w.at[1])]
    copies = [pltpu.make_async_copy(src, dst, sems.at[n]) for n, (src, dst) in enumerate(jobs)]
    for copy in copies:
        copy.start()
    for copy in copies:
        copy.wait()
    cells = buf_i[0]
    pick = (iota((256, n_obs), 0) == cells).astype(F32).astype(BF16)
    wanted = iota((fields, n_obs), 0) == buf_i[1] * 4
    found = [
        mm(jnp.concatenate([planes[0, m], planes[1, m]], axis=1), pick) for m in range(local)
    ]
    rows = [jnp.sum(jnp.where(wanted, x, 0.0), axis=0, keepdims=True) for x in found]
    full = jnp.concatenate(rows, axis=0)
    for d in range(o_ref.shape[0]):
        o_ref[d] = full
    row = (cells >= 128).astype(jnp.int32)
    sub = iota((8, n_obs), 0)
    lines = [buf_f[0], buf_f[1], row.astype(F32), (cells - 128 * row).astype(F32)]
    top = jnp.zeros((8, n_obs), F32)
    for r, line in enumerate(lines):
        top = jnp.where(sub == r, line, top)
    info[:8] = top
    for axis in range(2):
        for level in range(4):
            for half in range(2):
                info[8 + axis * 4 + level : 9 + axis * 4 + level, half * 128 : half * 128 + 128] = (
                    buf_w[axis, level, half : half + 1]
                )


def payload_kernel(planes, o_ref, main, rest):
    local = planes.shape[1]
    ident = (iota((128, 128), 0) == iota((128, 128), 1)).astype(F32).astype(BF16)
    lane = iota((8, 128), 1) // 32
    turned = []
    for row in range(2):
        for m in range(local):
            x = planes[row, m]
            turned.append(mm_nt(ident, jnp.concatenate([x[:128]] + [x[128:]] * 4, axis=0)))
    for row in range(2):
        for m in range(local):
            out = turned[row * local + m]
            main[pl.ds(row * 1024 + m, 128, stride=local), :] = out[:, :128]
            for q in range(4):
                tail = jnp.zeros((8, 128), F32)
                for cc in range(4):
                    at = q * 32 + cc * 8
                    tail = jnp.where(lane == cc, out[at : at + 8, 128:], tail)
                rest[pl.ds((row * 4 + q) * 64 + m, 8, stride=local), :] = tail
    for dest in range(8):
        o_ref[dest, :256] = main[dest * 256 : dest * 256 + 256, :].astype(BF16)
        o_ref[dest, 256:] = rest[dest * 64 : dest * 64 + 64, :].astype(BF16)


def transform_kernel(hi_ref, lo_ref, x_ref, *refs):
    outs, scr = refs[:-1], refs[-1]
    groups = hi_ref.shape[0]
    per = 32

    def members_of(base):
        x = x_ref[:, base : base + 16].astype(F32)
        return [x[:, k * 8 : k * 8 + 8].reshape(64, 128) for k in range(2)]

    lane64 = iota((64, 128), 1)
    masks = [(lane64 < 64).astype(F32).astype(BF16), (lane64 >= 64).astype(F32).astype(BF16)]

    def solved(p):
        ks = slice((p % 2) * 128, (p % 2) * 128 + 128)
        hi, lo = hi_ref[p // 2, :, ks], lo_ref[p // 2, :, ks]
        lhs = jnp.concatenate(
            [jnp.concatenate([hi * k, lo * k], axis=1) for k in masks], axis=0
        )
        x = jnp.concatenate(
            [
                jnp.concatenate(members_of(p * 16), axis=0),
                jnp.concatenate(members_of(256 + (p % 4) * 16), axis=0),
            ],
            axis=1,
        ).astype(BF16)
        return mm(lhs, jnp.concatenate([x, x], axis=0))

    ahead = 3
    count = 2 * groups
    results = {p: solved(p) for p in range(ahead)}
    for p in range(count):
        if p + ahead < count:
            results[p + ahead] = solved(p + ahead)
        out = results.pop(p)
        for c in range(2):
            val = out[c * 64 : c * 64 + 64]
            scr[0, pl.ds(p * 2 + c, 64, stride=per), :] = val[:, :128]
            scr[1, pl.ds(p * 2 + c, 64, stride=per), :] = val[:, 128:]
    lane = iota((8, 128), 1) // 32
    chunk = 8 // len(outs)
    for ml in range(8):
        for dest in range(8):
            base = (dest * 8 + ml) * per
            main = scr[0, base : base + per, :]
            rest = jnp.zeros((8, 128), F32)
            for cc in range(4):
                rest = jnp.where(lane == cc, scr[1, base + cc * 8 : base + cc * 8 + 8, :], rest)
            outs[ml // chunk][dest, ml % chunk] = jnp.concatenate(
                [main, rest, jnp.zeros_like(rest)], axis=0
            ).astype(BF16)[:40]


def relayout_kernel(x_ref, *outs):
    fields, chunk = outs[0].shape[2], outs[0].shape[1]
    f, at = iota((fields, 256), 0), iota((fields, 256), 1)
    ident = (((at < 128) & (f == at)) | ((at >= 128) & (f - 128 == at % 32))).astype(F32)
    ident = ident.astype(BF16)
    lane = iota((8, 128), 1) // 32
    for row in range(2):
        for ml in range(x_ref.shape[1]):
            mains, rests = [], []
            for q in range(4):
                block = x_ref[row * 4 + q, ml].astype(F32)
                mains.append(block[:32])
                rests += [jnp.where(lane == cc, block[32:40], 0.0) for cc in range(4)]
            full = jnp.concatenate(
                [jnp.concatenate(mains, axis=0), jnp.concatenate(rests, axis=0)], axis=1
            ).astype(BF16)
            outs[ml // chunk][row, ml % chunk] = mm_nt(ident, full).astype(BF16)


def advect_kernel(low_ref, own_ref, high_ref, cl_ref, co_ref, ch_ref, fac, o_ref):
    members, fields = own_ref.shape[1], own_ref.shape[2]
    lane = iota((8, 128), 1)

    def coeffs(ref, axis, row):
        c = ref[72:80, row * 128 : row * 128 + 128][axis * 4 : axis * 4 + 4]
        c = jnp.concatenate([c, c], axis=0)
        half, sq = 0.5 * c, 0.5 * c * c
        return half + sq, 1.0 - c * c, sq - half

    courant = [(cl_ref, 1), (co_ref, 0), (co_ref, 1), (ch_ref, 0)]
    cy = [coeffs(r, 1, k) for r, k in courant]
    cx = []
    for r, k in courant:
        a, b, c = coeffs(r, 0, k)
        cx.append((jnp.where(lane == 0, 0.0, a), b, jnp.where(lane == 127, 0.0, c)))
    shift_in, shift_out = iota((256, 256), 0) % 128, iota((256, 256), 1)
    shift = (
        ((shift_out < 128) & (shift_in == shift_out - 1))
        | ((shift_out >= 128) & (shift_in == shift_out - 127))
    ).astype(F32).astype(BF16)
    part = 80

    def scale(c, q):
        return (q.reshape(part // 8, 8, 128) * c[None]).reshape(part, 128)

    def rows(south, mid, north, k):
        a, b, c = cy[k]
        return scale(a, south) + scale(b, mid) + scale(c, north)

    def cols(planes, first):
        both = mm(
            jnp.concatenate([jnp.concatenate(split2(q), axis=1) for q in planes], axis=0), shift
        )
        outs = []
        for n, q in enumerate(planes):
            a, b, c = cx[first + n]
            near = both[n * part : n * part + part]
            outs.append(scale(a, near[:, :128]) + scale(b, q) + scale(c, near[:, 128:]))
        return outs

    units = [(m, f) for m in range(members) for f in range(0, fields, part)]

    def first(m, f):
        q = [
            r[k, m, f : f + part].astype(F32)
            for r, k in [
                (low_ref, 0), (low_ref, 1), (own_ref, 0),
                (own_ref, 1), (high_ref, 0), (high_ref, 1),
            ]
        ]
        return cols([rows(q[i], q[i + 1], q[i + 2], i) for i in range(4)], 0)

    ahead = 2
    mids = {u: first(*units[u]) for u in range(ahead)}
    for u, (m, f) in enumerate(units):
        if u + ahead < len(units):
            mids[u + ahead] = first(*units[u + ahead])
        q1 = mids.pop(u)
        q2 = cols([rows(q1[i], q1[i + 1], q1[i + 2], i + 1) for i in range(2)], 1)
        for r in range(2):
            o_ref[r, m, f : f + part] = (q2[r] * fac[r, f : f + part]).astype(BF16)


def call(kernel, outs, scratch=(), flops=10**8, nbytes=10**6):
    return pl.pallas_call(
        kernel,
        out_shape=outs,
        scratch_shapes=list(scratch),
        compiler_params=pltpu.CompilerParams(vmem_limit_bytes=40 << 20),
        cost_estimate=pl.CostEstimate(flops=flops, bytes_accessed=nbytes, transcendentals=0),
    )


def from_low(x):
    count = lax.axis_size("space")
    return lax.ppermute(x, "space", [(i, i + 1) for i in range(count - 1)])


def from_high(x):
    count = lax.axis_size("space")
    return lax.ppermute(x, "space", [(i + 1, i) for i in range(count - 1)])


def shards(
    ensemble,
    obs_value,
    obs_error,
    obs_cell,
    obs_species,
    patch_index,
    patch_count,
    courant_x,
    courant_y,
    dep_velocity,
    surface_factor,
):
    local, fields, tile_rows, columns = ensemble.shape
    levels = fields // dep_velocity.shape[0]
    n_obs = obs_cell.shape[1]
    per = patch_index.shape[1]
    maxobs = patch_index.shape[2]
    groups_mem = 8

    chunks = 2
    planes_in = jnp.transpose(ensemble, (2, 0, 1, 3))
    hbm = pl.BlockSpec(memory_space=pltpu.HBM)
    equiv, info = pl.pallas_call(
        equivalents_kernel,
        out_shape=[
            jax.ShapeDtypeStruct((groups_mem, local, n_obs), F32),
            jax.ShapeDtypeStruct((16, n_obs), F32),
        ],
        in_specs=[VMEM] + [hbm] * 6,
        scratch_shapes=[
            pltpu.SemaphoreType.DMA((6,)),
            pltpu.VMEM((2, 1, n_obs), jnp.int32),
            pltpu.VMEM((2, 1, n_obs), F32),
            pltpu.VMEM((2, levels, tile_rows, columns), F32),
        ],
        compiler_params=pltpu.CompilerParams(vmem_limit_bytes=40 << 20),
        cost_estimate=pl.CostEstimate(flops=10**8, bytes_accessed=10**6, transcendentals=0),
    )(planes_in, obs_cell, obs_species, obs_value, obs_error, courant_x, courant_y)
    everywhere = lax.all_to_all(equiv, "mem", 0, 0, tiled=True)
    payload = call(
        payload_kernel,
        jax.ShapeDtypeStruct((groups_mem, 320, 128), BF16),
        [pltpu.VMEM((2048, 128), F32), pltpu.VMEM((512, 128), F32)],
        flops=10**8,
    )(planes_in)

    packed = jnp.concatenate([everywhere.reshape(groups_mem * local, n_obs), info], axis=0)
    payload, packed = lax.optimization_barrier((payload, packed))
    low, high = from_low(packed), from_high(packed)
    state = lax.all_to_all(payload, "mem", 0, 0, tiled=True)

    used = jnp.arange(maxobs, dtype=jnp.int32)[None, :] < patch_count[0][:, None]
    idx = jnp.where(used, patch_index[0], -1).reshape(1, per * maxobs)
    cell_id = lax.axis_index("mem") * per + jnp.arange(per, dtype=jnp.int32)
    cell_id = jnp.broadcast_to(cell_id[:, None], (per, maxobs)).reshape(1, per * maxobs)
    pos = jnp.concatenate([cell_id // columns, cell_id % columns], axis=0).astype(F32)
    rate = jnp.where(
        (jnp.arange(fields, dtype=jnp.int32) % levels == 0)[:, None],
        jnp.repeat(dep_velocity, levels)[:, None],
        0.0,
    )
    factor = jnp.exp(-rate[None] * surface_factor[:, None, :])

    groups = per // 4
    hi, lo = call(
        weights_kernel,
        [jax.ShapeDtypeStruct((groups, 64, 256), BF16)] * 2,
        [
            pltpu.VMEM((2 * groups, 64, 128), F32),
            pltpu.VMEM((2 * groups, 64, 128), F32),
            pltpu.VMEM((2 * groups, 64, 128), F32),
            pltpu.VMEM((2 * groups, 16, 128), F32),
            pltpu.VMEM((2 * groups, 8, 128), F32),
        ],
        flops=10**10,
    )(low, packed, high, idx, pos)
    back = call(
        transform_kernel,
        [jax.ShapeDtypeStruct((groups_mem, local, 40, 128), BF16)],
        [pltpu.VMEM((2, 64 * per, 128), F32)],
        flops=10**9,
    )(hi, lo, state)[0]
    returned = lax.all_to_all(back, "mem", 0, 0, tiled=True)
    part_shape = jax.ShapeDtypeStruct((tile_rows, local // chunks, fields, columns), BF16)
    parts = call(relayout_kernel, [part_shape] * chunks, flops=10**8)(returned)
    halos = [(from_low(x), from_high(x)) for x in parts]
    outs = [
        call(advect_kernel, part_shape, flops=10**9)(below, x, above, low, packed, high, factor)
        for x, (below, above) in zip(parts, halos)
    ]
    done = jnp.concatenate(outs, axis=1)
    return jnp.transpose(done, (1, 2, 0, 3))


def solution(mesh):
    in_specs = (
        P("mem", None, "space", None),
        P("space", None),
        P("space", None),
        P("space", None),
        P("space", None),
        P("space", "mem", None),
        P("space", "mem"),
        P(None, "space", None),
        P(None, "space", None),
        P(),
        P("space", None),
    )
    out_specs = P("mem", None, "space", None)
    return jax.shard_map(shards, mesh=mesh, in_specs=in_specs, out_specs=out_specs, check_vma=False)
```

time: 106 us -> 87.1 us (0.82)
  the two profiles are of different devices: /device:TPU:384 before, /device:TPU:230 now
where the time goes in v1:
time: 87.1 us; the launch traced here: 86.6 us
  starting transfers between devices  36.9 us (42%)
  waiting for transfers between devices  29.7 us (34%)
  Pallas kernels  15 us (17%)
  local copies, waits for them, and re-layouts  4.43 us (5%)
    ppermute x3, starting transfers between devices, from_low(): return lax.ppermute(x, 'space', [(i, i + 1) for i in range(count - 1)])  19.4 us
    ppermute x3, waiting for transfers between devices, from_high(): return lax.ppermute(x, 'space', [(i + 1, i) for i in range(count - 1)])  14.5 us
    all_to_all x1, waiting for transfers between devices, shards(): returned = lax.all_to_all(back, 'mem', 0, 0, tiled=True)  11.5 us
    pallas_call x1, Pallas kernels, shards(): call(weights_kernel, [jax.ShapeDtypeStruct((groups, 64, 256), BF16)] * 2,...  7.14 us
    ppermute x3, starting transfers between devices, from_high(): return lax.ppermute(x, 'space', [(i + 1, i) for i in range(count - 1)])  5.76 us
    all_to_all x1, starting transfers between devices, shards(): everywhere = lax.all_to_all(equiv, 'mem', 0, 0, tiled=True)  4.48 us
    all_to_all x1, starting transfers between devices, shards(): returned = lax.all_to_all(back, 'mem', 0, 0, tiled=True)  3.67 us
    all_to_all x1, starting transfers between devices, shards(): state = lax.all_to_all(payload, 'mem', 0, 0, tiled=True)  3.55 us
  transfers between devices with their start and end apart: 9, of which 6 were waited for; matrix products, arithmetic and copies ran while one was open for 1% of the time, Pallas kernels for 11%

profile of v1, /device:TPU:230, one launch (start us, length us, event | category | flops | bytes accessed | tf_op | source)
XLA Modules:
  0.0 86.6 jit_solution(3490239005442473789)
XLA Ops:
  0.0 1.2 %copy.17 = bf16[8,160,2,128]{3,1,0,2:T(8,128)(2,1)S(1)} copy(bf16[8,160,2,128]{3,2,1,0:T(2,128)(2,1)} %param.11) | data formatting | bytes 1310720 | tf_op args[0]
  1.3 0.6 copy-done.2
  1.9 1.1 %shard_map.110 = (f32[8,8,256]{2,1,0:T(8,128)}, f32[16,256]{1,0:T(8,128)S(1)}) custom-call(bf16[2,8,160,128]{3,2,1,0:T(8,128)(2,1)S(1)} %bitcast.7, s32[1,256]{1,0:T(1,128)S(1)} %copy-done.2, s32[1,256]{1,0:T(1,128)S(1)} %copy-done.3, f32[1,256]{1,0:T(1,128)S(1)} %copy-done.4, f32[1,256]{1,0:T(1,128)S(1)} %copy-done.5, f32[4,2,128]{2,1,0:T(2,128)S(1)} %copy-done, ...), custom_call_target="tpu_custom_call" | custom-call | flops 100000000 | bytes 1000000 | tf_op jit(solution)/shard_map/pallas_call | solution.py:424
  3.0 4.5 %all-to-all-start = ((f32[8,8,256]{2,1,0:T(8,128)}), f32[8,8,256]{2,1,0:T(8,128)S(1)}, u32[]{:S(2)}, u32[]{:S(2)}) async-start(f32[8,8,256]{2,1,0:T(8,128)} %get-tuple-element.13), calls=%async_computation | async-start | bytes 131072 | tf_op jit(solution)/shard_map/all_to_all | solution.py:440
  7.6 0.1 reshape.209
  7.7 0.5 copy-done.8
  8.2 0.1 iota_compare_fusion
  8.3 0.1 lt.41
  8.4 0.1 squeeze.3
  8.5 1.3 %shard_map.109 = bf16[8,320,128]{2,1,0:T(8,128)(2,1)} custom-call(bf16[2,8,160,128]{3,2,1,0:T(8,128)(2,1)S(1)} %bitcast.8), custom_call_target="tpu_custom_call" | custom-call | flops 100000000 | bytes 1000000 | tf_op jit(solution)/shard_map/pallas_call | solution.py:441
  9.8 3.3 %all-to-all-done = f32[8,8,256]{2,1,0:T(8,128)S(1)} async-done(((f32[8,8,256]{2,1,0:T(8,128)}), f32[8,8,256]{2,1,0:T(8,128)S(1)}, u32[]{:S(2)}, u32[]{:S(2)}) %all-to-all-start) | async-done | bytes 65568 | tf_op jit(solution)/shard_map/all_to_all | solution.py:440
  13.1 4.9 %collective-permute-start = (f32[80,256]{1,0:T(8,128)S(1)}, f32[80,256]{1,0:T(8,128)S(1)}, u32[]{:S(2)}, u32[]{:S(2)}) collective-permute-start(f32[80,256]{1,0:T(8,128)S(1)} %pad_maximum_fusion.own.co_ref), channel_id=1, source_target_pairs={{0,1},{1,2},{2,3},{3,4},{4,5},{5,6},{6,7},{7,8},{8,9},{9,10},{10,1... | collective-permute-start | bytes 245768 | tf_op jit(solution)/shard_map/ppermute | solution.py:393
  18.1 1.9 %collective-permute-start.1 = (f32[80,256]{1,0:T(8,128)S(1)}, f32[80,256]{1,0:T(8,128)S(1)}, u32[]{:S(2)}, u32[]{:S(2)}) collective-permute-start(f32[80,256]{1,0:T(8,128)S(1)} %pad_maximum_fusion.own.co_ref), channel_id=1, source_target_pairs={{1,0},{2,1},{3,2},{4,3},{5,4},{6,5},{7,6},{8,7},{9,8},{10,9},{11,1... | collective-permute-start | bytes 245768 | tf_op jit(solution)/shard_map/ppermute | solution.py:398
  20.0 3.6 %all-to-all-start.1 = ((bf16[8,320,128]{2,1,0:T(8,128)(2,1)}), bf16[8,320,128]{2,1,0:T(8,128)(2,1)S(1)}, u32[]{:S(2)}, u32[]{:S(2)}) async-start(bf16[8,320,128]{2,1,0:T(8,128)(2,1)} %shard_map.109), calls=%async_computation.1 | async-start | bytes 1310720 | tf_op jit(solution)/shard_map/all_to_all | solution.py:451
  23.6 4.1 %collective-permute-done.1.right.ch_ref = f32[80,256]{1,0:T(8,128)S(1)} collective-permute-done((f32[80,256]{1,0:T(8,128)S(1)}, f32[80,256]{1,0:T(8,128)S(1)}, u32[]{:S(2)}, u32[]{:S(2)}) %collective-permute-start.1) | collective-permute-done | bytes 81952 | tf_op jit(solution)/shard_map/ppermute | solution.py:398
  27.7 7.1 %shard_map.111 = (bf16[8,64,256]{2,1,0:T(8,128)(2,1)S(1)}, bf16[8,64,256]{2,1,0:T(8,128)(2,1)S(1)}) custom-call(f32[80,256]{1,0:T(8,128)S(1)} %collective-permute-done.left.cl_ref, f32[80,256]{1,0:T(8,128)S(1)} %pad_maximum_fusion.own.co_ref, f32[80,256]{1,0:T(8,128)S(1)} %collective-permute-done.1.right.ch_ref, s32[1,1024]{1,0:T(1,128)S(1)} %broadcast_select_fusion.idx_ref, ...), custom_call_target="tpu_custom_call" | custom-call | flops 10000000000 | bytes 1000000 | tf_op jit(solution)/shard_map/pallas_call | solution.py:466
  34.9 0.4 all-to-all-done.1.x_ref
  35.2 2.7 %shard_map.112 = bf16[8,8,40,128]{3,2,1,0:T(8,128)(2,1)} custom-call(bf16[8,64,256]{2,1,0:T(8,128)(2,1)S(1)} %get-tuple-element.16.hi_ref, bf16[8,64,256]{2,1,0:T(8,128)(2,1)S(1)} %get-tuple-element.17.lo_ref, bf16[8,320,128]{2,1,0:T(8,128)(2,1)S(1)} %all-to-all-done.1.x_ref), custom_call_target="tpu_custom_call" | custom-call | flops 1000000000 | bytes 1000000 | tf_op jit(solution)/shard_map/pallas_call | solution.py:478
  37.9 3.7 %all-to-all-start.2 = ((bf16[8,8,40,128]{3,2,1,0:T(8,128)(2,1)}), bf16[8,8,40,128]{3,2,1,0:T(8,128)(2,1)S(1)}, u32[]{:S(2)}, u32[]{:S(2)}) async-start(bf16[8,8,40,128]{3,2,1,0:T(8,128)(2,1)} %shard_map.112), calls=%async_computation.2 | async-start | bytes 1310720 | tf_op jit(solution)/shard_map/all_to_all | solution.py:484
  41.7 0.1 broadcast_in_dim_reshape.3
  41.8 11.5 %all-to-all-done.2.x_ref = bf16[8,8,40,128]{3,2,1,0:T(8,128)(2,1)S(1)} async-done(((bf16[8,8,40,128]{3,2,1,0:T(8,128)(2,1)}), bf16[8,8,40,128]{3,2,1,0:T(8,128)(2,1)S(1)}, u32[]{:S(2)}, u32[]{:S(2)}) %all-to-all-start.2) | async-done | bytes 655392 | tf_op jit(solution)/shard_map/all_to_all | solution.py:484
  53.3 0.5 shard_map.113
  53.8 7.2 %collective-permute-start.2 = (bf16[2,4,160,128]{3,2,1,0:T(8,128)(2,1)S(1)}, bf16[2,4,160,128]{3,2,1,0:T(8,128)(2,1)S(1)}, u32[]{:S(2)}, u32[]{:S(2)}) collective-permute-start(bf16[2,4,160,128]{3,2,1,0:T(8,128)(2,1)S(1)} %get-tuple-element.19.own_ref), channel_id=1, source_target_pairs={{0,1},{1,2},{2,3},{3,4},{4,5},{5,6},{6,7},{7,8},{8,9},{9,10},{10,1... | collective-permute-start | bytes 983048 | tf_op jit(solution)/shard_map/ppermute | solution.py:393
  61.0 1.9 %collective-permute-start.3 = (bf16[2,4,160,128]{3,2,1,0:T(8,128)(2,1)S(1)}, bf16[2,4,160,128]{3,2,1,0:T(8,128)(2,1)S(1)}, u32[]{:S(2)}, u32[]{:S(2)}) collective-permute-start(bf16[2,4,160,128]{3,2,1,0:T(8,128)(2,1)S(1)} %get-tuple-element.19.own_ref), channel_id=1, source_target_pairs={{1,0},{2,1},{3,2},{4,3},{5,4},{6,5},{7,6},{8,7},{9,8},{10,9},{11,1... | collective-permute-start | bytes 983048 | tf_op jit(solution)/shard_map/ppermute | solution.py:398
  63.0 7.2 %collective-permute-start.4 = (bf16[2,4,160,128]{3,2,1,0:T(8,128)(2,1)S(1)}, bf16[2,4,160,128]{3,2,1,0:T(8,128)(2,1)S(1)}, u32[]{:S(2)}, u32[]{:S(2)}) collective-permute-start(bf16[2,4,160,128]{3,2,1,0:T(8,128)(2,1)S(1)} %get-tuple-element.20.own_ref), channel_id=1, source_target_pairs={{0,1},{1,2},{2,3},{3,4},{4,5},{5,6},{6,7},{7,8},{8,9},{9,10},{10,1... | collective-permute-start | bytes 983048 | tf_op jit(solution)/shard_map/ppermute | solution.py:393
  70.2 1.9 %collective-permute-start.5 = (bf16[2,4,160,128]{3,2,1,0:T(8,128)(2,1)S(1)}, bf16[2,4,160,128]{3,2,1,0:T(8,128)(2,1)S(1)}, u32[]{:S(2)}, u32[]{:S(2)}) collective-permute-start(bf16[2,4,160,128]{3,2,1,0:T(8,128)(2,1)S(1)} %get-tuple-element.20.own_ref), channel_id=1, source_target_pairs={{1,0},{2,1},{3,2},{4,3},{5,4},{6,5},{7,6},{8,7},{9,8},{10,9},{11,1... | collective-permute-start | bytes 983048 | tf_op jit(solution)/shard_map/ppermute | solution.py:398
  72.2 0.1 multiply_exponential_fusion.fac
  72.3 2.9 %collective-permute-done.3.high_ref = bf16[2,4,160,128]{3,2,1,0:T(8,128)(2,1)S(1)} collective-permute-done((bf16[2,4,160,128]{3,2,1,0:T(8,128)(2,1)S(1)}, bf16[2,4,160,128]{3,2,1,0:T(8,128)(2,1)S(1)}, u32[]{:S(2)}, u32[]{:S(2)}) %collective-permute-start.3) | collective-permute-done | bytes 327712 | tf_op jit(solution)/shard_map/ppermute | solution.py:398
  75.2 1.2 %shard_map.114 = bf16[2,4,160,128]{3,2,1,0:T(8,128)(2,1)S(1)} custom-call(bf16[2,4,160,128]{3,2,1,0:T(8,128)(2,1)S(1)} %collective-permute-done.2.low_ref, bf16[2,4,160,128]{3,2,1,0:T(8,128)(2,1)S(1)} %get-tuple-element.19.own_ref, bf16[2,4,160,128]{3,2,1,0:T(8,128)(2,1)S(1)} %collective-permute-done.3.high_ref, ...), custom_call_target="tpu_custom_call" | custom-call | flops 1000000000 | bytes 1000000 | tf_op jit(solution)/shard_map/pallas_call | solution.py:489
  76.4 7.4 %collective-permute-done.5.high_ref = bf16[2,4,160,128]{3,2,1,0:T(8,128)(2,1)S(1)} collective-permute-done((bf16[2,4,160,128]{3,2,1,0:T(8,128)(2,1)S(1)}, bf16[2,4,160,128]{3,2,1,0:T(8,128)(2,1)S(1)}, u32[]{:S(2)}, u32[]{:S(2)}) %collective-permute-start.5) | collective-permute-done | bytes 327712 | tf_op jit(solution)/shard_map/ppermute | solution.py:398
  83.8 1.2 %shard_map.115 = bf16[2,4,160,128]{3,2,1,0:T(8,128)(2,1)S(1)} custom-call(bf16[2,4,160,128]{3,2,1,0:T(8,128)(2,1)S(1)} %collective-permute-done.4.low_ref, bf16[2,4,160,128]{3,2,1,0:T(8,128)(2,1)S(1)} %get-tuple-element.20.own_ref, bf16[2,4,160,128]{3,2,1,0:T(8,128)(2,1)S(1)} %collective-permute-done.5.high_ref, ...), custom_call_target="tpu_custom_call" | custom-call | flops 1000000000 | bytes 1000000 | tf_op jit(solution)/shard_map/pallas_call | solution.py:489
  85.1 1.5 %copy.15 = bf16[8,160,2,128]{3,2,1,0:T(2,128)(2,1)} copy(bf16[8,160,2,128]{3,1,0,2:T(8,128)(2,1)S(1)} %maximum_bitcast_fusion) | data formatting | bytes 1310720 | tf_op jit(solution)/shard_map/transpose | solution.py:493
  (31 shorter events, 0.3 us)
Async XLA Ops:
  0.0 1.3 %copy-start = (f32[4,2,128]{2,1,0:T(2,128)S(1)}, f32[4,2,128]{2,1,0:T(2,128)}, u32[]{:S(2)}) copy-start(f32[4,2,128]{2,1,0:T(2,128)} %wind_x.1) | copy-start | bytes 12292
  0.0 1.3 %copy-start.1 = (f32[4,2,128]{2,1,0:T(2,128)S(1)}, f32[4,2,128]{2,1,0:T(2,128)}, u32[]{:S(2)}) copy-start(f32[4,2,128]{2,1,0:T(2,128)} %wind_y.1) | copy-start | bytes 12292
  0.0 1.3 %copy-start.3 = (s32[1,256]{1,0:T(1,128)S(1)}, s32[1,256]{1,0:T(1,128)}, u32[]{:S(2)}) copy-start(s32[1,256]{1,0:T(1,128)} %kind.1) | copy-start | bytes 3076
  0.0 1.3 %copy-start.4 = (f32[1,256]{1,0:T(1,128)S(1)}, f32[1,256]{1,0:T(1,128)}, u32[]{:S(2)}) copy-start(f32[1,256]{1,0:T(1,128)} %value.1) | copy-start | bytes 3076
  0.0 1.3 %copy-start.5 = (f32[1,256]{1,0:T(1,128)S(1)}, f32[1,256]{1,0:T(1,128)}, u32[]{:S(2)}) copy-start(f32[1,256]{1,0:T(1,128)} %error.1) | copy-start | bytes 3076
  1.3 0.7 copy-start.2
  3.0 10.1 %all-to-all-start = ((f32[8,8,256]{2,1,0:T(8,128)}), f32[8,8,256]{2,1,0:T(8,128)S(1)}, u32[]{:S(2)}, u32[]{:S(2)}) async-start(f32[8,8,256]{2,1,0:T(8,128)} %get-tuple-element.13), calls=%async_computation | async-start | bytes 131072 | tf_op jit(solution)/shard_map/all_to_all | solution.py:440
  7.6 0.7 copy-start.8
  7.6 0.7 copy-start.6
  13.1 10.5 %collective-permute-start = (f32[80,256]{1,0:T(8,128)S(1)}, f32[80,256]{1,0:T(8,128)S(1)}, u32[]{:S(2)}, u32[]{:S(2)}) collective-permute-start(f32[80,256]{1,0:T(8,128)S(1)} %pad_maximum_fusion.own.co_ref), channel_id=1, source_target_pairs={{0,1},{1,2},{2,3},{3,4},{4,5},{5,6},{6,7},{7,8},{8,9},{9,10},{10,1... | collective-permute-start | bytes 245768 | tf_op jit(solution)/shard_map/ppermute | solution.py:393
  18.1 9.7 %collective-permute-start.1 = (f32[80,256]{1,0:T(8,128)S(1)}, f32[80,256]{1,0:T(8,128)S(1)}, u32[]{:S(2)}, u32[]{:S(2)}) collective-permute-start(f32[80,256]{1,0:T(8,128)S(1)} %pad_maximum_fusion.own.co_ref), channel_id=1, source_target_pairs={{1,0},{2,1},{3,2},{4,3},{5,4},{6,5},{7,6},{8,7},{9,8},{10,9},{11,1... | collective-permute-start | bytes 245768 | tf_op jit(solution)/shard_map/ppermute | solution.py:398
  20.0 15.2 %all-to-all-start.1 = ((bf16[8,320,128]{2,1,0:T(8,128)(2,1)}), bf16[8,320,128]{2,1,0:T(8,128)(2,1)S(1)}, u32[]{:S(2)}, u32[]{:S(2)}) async-start(bf16[8,320,128]{2,1,0:T(8,128)(2,1)} %shard_map.109), calls=%async_computation.1 | async-start | bytes 1310720 | tf_op jit(solution)/shard_map/all_to_all | solution.py:451
  37.9 3.7 %copy-start.9 = (f32[40]{0:T(128)S(1)}, f32[40]{0:T(128)}, u32[]{:S(2)}) copy-start(f32[40]{0:T(128)} %param.20) | copy-start | bytes 484
  37.9 15.4 %all-to-all-start.2 = ((bf16[8,8,40,128]{3,2,1,0:T(8,128)(2,1)}), bf16[8,8,40,128]{3,2,1,0:T(8,128)(2,1)S(1)}, u32[]{:S(2)}, u32[]{:S(2)}) async-start(bf16[8,8,40,128]{3,2,1,0:T(8,128)(2,1)} %shard_map.112), calls=%async_computation.2 | async-start | bytes 1310720 | tf_op jit(solution)/shard_map/all_to_all | solution.py:484
  53.8 18.5 %collective-permute-start.2 = (bf16[2,4,160,128]{3,2,1,0:T(8,128)(2,1)S(1)}, bf16[2,4,160,128]{3,2,1,0:T(8,128)(2,1)S(1)}, u32[]{:S(2)}, u32[]{:S(2)}) collective-permute-start(bf16[2,4,160,128]{3,2,1,0:T(8,128)(2,1)S(1)} %get-tuple-element.19.own_ref), channel_id=1, source_target_pairs={{0,1},{1,2},{2,3},{3,4},{4,5},{5,6},{6,7},{7,8},{8,9},{9,10},{10,1... | collective-permute-start | bytes 983048 | tf_op jit(solution)/shard_map/ppermute | solution.py:393
  61.0 14.2 %collective-permute-start.3 = (bf16[2,4,160,128]{3,2,1,0:T(8,128)(2,1)S(1)}, bf16[2,4,160,128]{3,2,1,0:T(8,128)(2,1)S(1)}, u32[]{:S(2)}, u32[]{:S(2)}) collective-permute-start(bf16[2,4,160,128]{3,2,1,0:T(8,128)(2,1)S(1)} %get-tuple-element.19.own_ref), channel_id=1, source_target_pairs={{1,0},{2,1},{3,2},{4,3},{5,4},{6,5},{7,6},{8,7},{9,8},{10,9},{11,1... | collective-permute-start | bytes 983048 | tf_op jit(solution)/shard_map/ppermute | solution.py:398
  63.0 9.2 %copy-start.7 = (f32[2,128]{1,0:T(2,128)S(1)}, f32[2,128]{1,0:T(2,128)}, u32[]{:S(2)}) copy-start(f32[2,128]{1,0:T(2,128)} %param.21) | copy-start | bytes 3076
  63.0 13.4 %collective-permute-start.4 = (bf16[2,4,160,128]{3,2,1,0:T(8,128)(2,1)S(1)}, bf16[2,4,160,128]{3,2,1,0:T(8,128)(2,1)S(1)}, u32[]{:S(2)}, u32[]{:S(2)}) collective-permute-start(bf16[2,4,160,128]{3,2,1,0:T(8,128)(2,1)S(1)} %get-tuple-element.20.own_ref), channel_id=1, source_target_pairs={{0,1},{1,2},{2,3},{3,4},{4,5},{5,6},{6,7},{7,8},{8,9},{9,10},{10,1... | collective-permute-start | bytes 983048 | tf_op jit(solution)/shard_map/ppermute | solution.py:393
  70.2 13.6 %collective-permute-start.5 = (bf16[2,4,160,128]{3,2,1,0:T(8,128)(2,1)S(1)}, bf16[2,4,160,128]{3,2,1,0:T(8,128)(2,1)S(1)}, u32[]{:S(2)}, u32[]{:S(2)}) collective-permute-start(bf16[2,4,160,128]{3,2,1,0:T(8,128)(2,1)S(1)} %get-tuple-element.20.own_ref), channel_id=1, source_target_pairs={{1,0},{2,1},{3,2},{4,3},{5,4},{6,5},{7,6},{8,7},{9,8},{10,9},{11,1... | collective-permute-start | bytes 983048 | tf_op jit(solution)/shard_map/ppermute | solution.py:398

commit v2 on v1

--- a/solution.py
+++ b/solution.py
@@ -73,10 +73,16 @@
     return out[:, :128] + out[:, 128:]
 
 
-def weights_kernel(left, own, right, idx_ref, pos_ref, hi_ref, lo_ref, t_ref, z_ref, m_ref, q_ref, tr_ref):
+def by_parity(is_odd, a, b):
+    return jnp.where(is_odd, a, b), jnp.where(is_odd, b, a)
+
+
+def weights_kernel(odd, near_a, own, near_b, idx_ref, pos_ref, hi_ref, lo_ref, t_ref, z_ref, m_ref, q_ref, tr_ref):
     members, maxobs = 64, 32
     pairs = t_ref.shape[0]
-    parts = [left[...], own[...], right[...]]
+    is_odd = odd[0, 0] == 1
+    low, high = by_parity(is_odd, near_a[...], near_b[...])
+    parts = [low, own[...], high]
     equiv = jnp.concatenate([p[:members] for p in parts], axis=1)
     info = jnp.concatenate([p[members : members + 8] for p in parts], axis=1)
     n_obs = info.shape[1]
@@ -183,64 +189,75 @@
         lo_ref[p // 2, :, ks] = lo
 
 
-def equivalents_kernel(planes, cell, kind, value, error, wind_x, wind_y, o_ref, info, *scratch):
-    local, fields = planes.shape[1], planes.shape[2]
-    n_obs = o_ref.shape[2]
-    sems, buf_i, buf_f, buf_w = scratch
-    jobs = [(cell, buf_i.at[0]), (kind, buf_i.at[1]), (value, buf_f.at[0]), (error, buf_f.at[1])]
-    jobs += [(wind_x, buf_w.at[0]), (wind_y, buf_w.at[1])]
+def equivalents_kernel(ens, cell, kind, o_ref, held, picks, sems):
+    span = ens.shape[0] // 8
+    n_obs = cell.shape[1]
+    jobs = [(cell, picks.at[0]), (kind, picks.at[1])]
+    jobs += [(ens.at[pl.ds(m * span, span)], held.at[m]) for m in range(8)]
     copies = [pltpu.make_async_copy(src, dst, sems.at[n]) for n, (src, dst) in enumerate(jobs)]
     for copy in copies:
         copy.start()
-    for copy in copies:
-        copy.wait()
-    cells = buf_i[0]
-    pick = (iota((256, n_obs), 0) == cells).astype(F32).astype(BF16)
-    wanted = iota((fields, n_obs), 0) == buf_i[1] * 4
-    found = [
-        mm(jnp.concatenate([planes[0, m], planes[1, m]], axis=1), pick) for m in range(local)
-    ]
-    rows = [jnp.sum(jnp.where(wanted, x, 0.0), axis=0, keepdims=True) for x in found]
+    copies[0].wait()
+    copies[1].wait()
+    cells = picks[0]
+    row = (cells >= 128).astype(jnp.int32)
+    pick = (iota((128, n_obs), 0) == cells - 128 * row).astype(F32).astype(BF16)
+    wanted = iota((span, n_obs), 0) == picks[1] * 8 + row
+    rows = []
+    for m in range(0, 8, 2):
+        copies[2 + m].wait()
+        copies[3 + m].wait()
+        found = [mm(held[m + k], pick) for k in range(2)]
+        rows += [jnp.sum(jnp.where(wanted, x, 0.0), axis=0, keepdims=True) for x in found]
     full = jnp.concatenate(rows, axis=0)
     for d in range(o_ref.shape[0]):
         o_ref[d] = full
+
+
+def payload_kernel(ens, cell, value, error, wind_x, wind_y, o_ref, info, flat, main, rest):
+    local = 8
+    fields = ens.shape[0] // (2 * local)
+    ident = (iota((128, 128), 0) == iota((128, 128), 1)).astype(F32).astype(BF16)
+    lane = iota((8, 128), 1) // 32
+    flat[...] = ens[...].astype(F32)
+
+    def turned(n):
+        row, m = n // local, n % local
+        x = flat[pl.ds(m * 2 * fields + row, fields, stride=2), :].astype(BF16)
+        return mm_nt(ident, jnp.concatenate([x[:128]] + [x[128:]] * 4, axis=0))
+
+    ahead = 3
+    queue = [turned(n) for n in range(ahead)]
+    for n in range(2 * local):
+        row, m = n // local, n % local
+        if n + ahead < 2 * local:
+            queue.append(turned(n + ahead))
+        out = queue.pop(0)
+        main[pl.ds(row * 1024 + m, 128, stride=local), :] = out[:, :128]
+        for q in range(4):
+            tail = jnp.zeros((8, 128), F32)
+            for cc in range(4):
+                at = q * 32 + cc * 8
+                tail = jnp.where(lane == cc, out[at : at + 8, 128:], tail)
+            rest[pl.ds((row * 4 + q) * 64 + m, 8, stride=local), :] = tail
+    for dest in range(8):
+        o_ref[dest, :256] = main[dest * 256 : dest * 256 + 256, :].astype(BF16)
+        o_ref[dest, 256:] = rest[dest * 64 : dest * 64 + 64, :].astype(BF16)
+    cells = cell[...]
+    n_obs = cells.shape[1]
     row = (cells >= 128).astype(jnp.int32)
     sub = iota((8, n_obs), 0)
-    lines = [buf_f[0], buf_f[1], row.astype(F32), (cells - 128 * row).astype(F32)]
+    lines = [value[...], error[...], row.astype(F32), (cells - 128 * row).astype(F32)]
     top = jnp.zeros((8, n_obs), F32)
     for r, line in enumerate(lines):
         top = jnp.where(sub == r, line, top)
     info[:8] = top
-    for axis in range(2):
+    for axis, wind in enumerate((wind_x, wind_y)):
         for level in range(4):
             for half in range(2):
                 info[8 + axis * 4 + level : 9 + axis * 4 + level, half * 128 : half * 128 + 128] = (
-                    buf_w[axis, level, half : half + 1]
+                    wind[level, half : half + 1]
                 )
-
-
-def payload_kernel(planes, o_ref, main, rest):
-    local = planes.shape[1]
-    ident = (iota((128, 128), 0) == iota((128, 128), 1)).astype(F32).astype(BF16)
-    lane = iota((8, 128), 1) // 32
-    turned = []
-    for row in range(2):
-        for m in range(local):
-            x = planes[row, m]
-            turned.append(mm_nt(ident, jnp.concatenate([x[:128]] + [x[128:]] * 4, axis=0)))
-    for row in range(2):
-        for m in range(local):
-            out = turned[row * local + m]
-            main[pl.ds(row * 1024 + m, 128, stride=local), :] = out[:, :128]
-            for q in range(4):
-                tail = jnp.zeros((8, 128), F32)
-                for cc in range(4):
-                    at = q * 32 + cc * 8
-                    tail = jnp.where(lane == cc, out[at : at + 8, 128:], tail)
-                rest[pl.ds((row * 4 + q) * 64 + m, 8, stride=local), :] = tail
-    for dest in range(8):
-        o_ref[dest, :256] = main[dest * 256 : dest * 256 + 256, :].astype(BF16)
-        o_ref[dest, 256:] = rest[dest * 64 : dest * 64 + 64, :].astype(BF16)
 
 
 def transform_kernel(hi_ref, lo_ref, x_ref, *refs):
@@ -296,7 +313,8 @@
 
 
 def relayout_kernel(x_ref, *outs):
-    fields, chunk = outs[0].shape[2], outs[0].shape[1]
+    fields = outs[0].shape[2]
+    places = [(o, k) for o in outs for k in range(o.shape[1])]
     f, at = iota((fields, 256), 0), iota((fields, 256), 1)
     ident = (((at < 128) & (f == at)) | ((at >= 128) & (f - 128 == at % 32))).astype(F32)
     ident = ident.astype(BF16)
@@ -311,25 +329,38 @@
             full = jnp.concatenate(
                 [jnp.concatenate(mains, axis=0), jnp.concatenate(rests, axis=0)], axis=1
             ).astype(BF16)
-            outs[ml // chunk][row, ml % chunk] = mm_nt(ident, full).astype(BF16)
-
-
-def advect_kernel(low_ref, own_ref, high_ref, cl_ref, co_ref, ch_ref, fac, o_ref):
-    members, fields = own_ref.shape[1], own_ref.shape[2]
+            out, k = places[ml]
+            out[row, k] = mm_nt(ident, full).astype(BF16)
+
+
+def advect_kernel(odd, a_ref, own_ref, b_ref, ca_ref, co_ref, cb_ref, dep_ref, surf_ref, *refs):
+    o_ref, fac, flat = refs[-3:]
+    fields = own_ref.shape[2]
+    is_odd = odd[0, 0] == 1
     lane = iota((8, 128), 1)
-
-    def coeffs(ref, axis, row):
-        c = ref[72:80, row * 128 : row * 128 + 128][axis * 4 : axis * 4 + 4]
+    wind_low, wind_high = by_parity(is_odd, ca_ref[72:80], cb_ref[72:80])
+    wind_own = co_ref[72:80]
+
+    def coeffs(wind, axis, row):
+        c = wind[axis * 4 : axis * 4 + 4, row * 128 : row * 128 + 128]
         c = jnp.concatenate([c, c], axis=0)
         half, sq = 0.5 * c, 0.5 * c * c
         return half + sq, 1.0 - c * c, sq - half
 
-    courant = [(cl_ref, 1), (co_ref, 0), (co_ref, 1), (ch_ref, 0)]
-    cy = [coeffs(r, 1, k) for r, k in courant]
+    courant = [(wind_low, 1), (wind_own, 0), (wind_own, 1), (wind_high, 0)]
+    cy = [coeffs(w, 1, k) for w, k in courant]
     cx = []
-    for r, k in courant:
-        a, b, c = coeffs(r, 0, k)
+    for w, k in courant:
+        a, b, c = coeffs(w, 0, k)
         cx.append((jnp.where(lane == 0, 0.0, a), b, jnp.where(lane == 127, 0.0, c)))
+
+    @pl.when(pl.program_id(0) == 0)
+    def _():
+        own_level = iota((fields, dep_ref.shape[1]), 0) == 4 * iota((fields, dep_ref.shape[1]), 1)
+        rate = jnp.sum(jnp.where(own_level, dep_ref[...], 0.0), axis=1, keepdims=True)
+        for row in range(2):
+            fac[row] = jnp.exp(-rate * surf_ref[row : row + 1, :])
+
     shift_in, shift_out = iota((256, 256), 0) % 128, iota((256, 256), 1)
     shift = (
         ((shift_out < 128) & (shift_in == shift_out - 1))
@@ -355,47 +386,61 @@
             outs.append(scale(a, near[:, :128]) + scale(b, q) + scale(c, near[:, 128:]))
         return outs
 
+    members = o_ref.shape[0] // (2 * fields)
     units = [(m, f) for m in range(members) for f in range(0, fields, part)]
 
-    def first(m, f):
-        q = [
-            r[k, m, f : f + part].astype(F32)
-            for r, k in [
-                (low_ref, 0), (low_ref, 1), (own_ref, 0),
-                (own_ref, 1), (high_ref, 0), (high_ref, 1),
-            ]
+    def first(j, f):
+        m = pl.program_id(0) * members + j
+        near = [
+            by_parity(is_odd, a_ref[k, m, f : f + part], b_ref[k, m, f : f + part])
+            for k in range(2)
         ]
+        q = [near[0][0], near[1][0], own_ref[0, m, f : f + part]]
+        q += [own_ref[1, m, f : f + part], near[0][1], near[1][1]]
+        q = [x.astype(F32) for x in q]
         return cols([rows(q[i], q[i + 1], q[i + 2], i) for i in range(4)], 0)
 
     ahead = 2
     mids = {u: first(*units[u]) for u in range(ahead)}
-    for u, (m, f) in enumerate(units):
+    for u, (j, f) in enumerate(units):
         if u + ahead < len(units):
             mids[u + ahead] = first(*units[u + ahead])
         q1 = mids.pop(u)
         q2 = cols([rows(q1[i], q1[i + 1], q1[i + 2], i + 1) for i in range(2)], 1)
+        base = (j * fields + f) * 2
         for r in range(2):
-            o_ref[r, m, f : f + part] = (q2[r] * fac[r, f : f + part]).astype(BF16)
-
-
-def call(kernel, outs, scratch=(), flops=10**8, nbytes=10**6):
+            flat[pl.ds(base + r, part, stride=2), :] = q2[r] * fac[r, f : f + part]
+        o_ref[base : base + 2 * part] = flat[base : base + 2 * part, :].astype(BF16)
+
+
+def params():
+    return pltpu.CompilerParams(vmem_limit_bytes=40 << 20)
+
+
+def cost(flops):
+    return pl.CostEstimate(flops=flops, bytes_accessed=10**6, transcendentals=0)
+
+
+def call(kernel, outs, scratch=(), flops=10**8, specs=None):
     return pl.pallas_call(
         kernel,
         out_shape=outs,
+        **({} if specs is None else {"in_specs": specs}),
         scratch_shapes=list(scratch),
-        compiler_params=pltpu.CompilerParams(vmem_limit_bytes=40 << 20),
-        cost_estimate=pl.CostEstimate(flops=flops, bytes_accessed=nbytes, transcendentals=0),
+        compiler_params=params(),
+        cost_estimate=cost(flops),
     )
 
 
-def from_low(x):
-    count = lax.axis_size("space")
-    return lax.ppermute(x, "space", [(i, i + 1) for i in range(count - 1)])
-
-
-def from_high(x):
-    count = lax.axis_size("space")
-    return lax.ppermute(x, "space", [(i + 1, i) for i in range(count - 1)])
+def swap(x, first):
+    pairs = []
+    for low in range(first, lax.axis_size("space") - 1, 2):
+        pairs += [(low, low + 1), (low + 1, low)]
+    return lax.ppermute(x, "space", pairs)
+
+
+def block_at(first, i):
+    return first + i, 0
 
 
 def shards(
@@ -418,50 +463,44 @@
     maxobs = patch_index.shape[2]
     groups_mem = 8
 
-    chunks = 2
-    planes_in = jnp.transpose(ensemble, (2, 0, 1, 3))
+    sizes = (6, 2)
+    flat = ensemble.reshape(local * fields * tile_rows, columns)
     hbm = pl.BlockSpec(memory_space=pltpu.HBM)
-    equiv, info = pl.pallas_call(
+    equiv = pl.pallas_call(
         equivalents_kernel,
-        out_shape=[
-            jax.ShapeDtypeStruct((groups_mem, local, n_obs), F32),
+        out_shape=jax.ShapeDtypeStruct((groups_mem, local, n_obs), F32),
+        in_specs=[hbm] * 3,
+        scratch_shapes=[
+            pltpu.VMEM((local, fields * tile_rows, columns), BF16),
+            pltpu.VMEM((2, 1, n_obs), jnp.int32),
+            pltpu.SemaphoreType.DMA((2 + local,)),
+        ],
+        compiler_params=pltpu.CompilerParams(vmem_limit_bytes=67000000),
+        cost_estimate=cost(10**8),
+    )(flat, obs_cell, obs_species)
+    everywhere = lax.all_to_all(equiv, "mem", 0, 0, tiled=True)
+    payload, info = call(
+        payload_kernel,
+        [
+            jax.ShapeDtypeStruct((groups_mem, 320, 128), BF16),
             jax.ShapeDtypeStruct((16, n_obs), F32),
         ],
-        in_specs=[VMEM] + [hbm] * 6,
-        scratch_shapes=[
-            pltpu.SemaphoreType.DMA((6,)),
-            pltpu.VMEM((2, 1, n_obs), jnp.int32),
-            pltpu.VMEM((2, 1, n_obs), F32),
-            pltpu.VMEM((2, levels, tile_rows, columns), F32),
-        ],
-        compiler_params=pltpu.CompilerParams(vmem_limit_bytes=40 << 20),
-        cost_estimate=pl.CostEstimate(flops=10**8, bytes_accessed=10**6, transcendentals=0),
-    )(planes_in, obs_cell, obs_species, obs_value, obs_error, courant_x, courant_y)
-    everywhere = lax.all_to_all(equiv, "mem", 0, 0, tiled=True)
-    payload = call(
-        payload_kernel,
-        jax.ShapeDtypeStruct((groups_mem, 320, 128), BF16),
-        [pltpu.VMEM((2048, 128), F32), pltpu.VMEM((512, 128), F32)],
+        [pltpu.VMEM(flat.shape, F32), pltpu.VMEM((2048, 128), F32), pltpu.VMEM((512, 128), F32)],
         flops=10**8,
-    )(planes_in)
-
+    )(flat, obs_cell, obs_value, obs_error, courant_x, courant_y)
     packed = jnp.concatenate([everywhere.reshape(groups_mem * local, n_obs), info], axis=0)
     payload, packed = lax.optimization_barrier((payload, packed))
-    low, high = from_low(packed), from_high(packed)
+    near_a, near_b = swap(packed, 0), swap(packed, 1)
     state = lax.all_to_all(payload, "mem", 0, 0, tiled=True)
+    odd = (lax.axis_index("space") % 2).reshape(1, 1)
 
     used = jnp.arange(maxobs, dtype=jnp.int32)[None, :] < patch_count[0][:, None]
     idx = jnp.where(used, patch_index[0], -1).reshape(1, per * maxobs)
     cell_id = lax.axis_index("mem") * per + jnp.arange(per, dtype=jnp.int32)
     cell_id = jnp.broadcast_to(cell_id[:, None], (per, maxobs)).reshape(1, per * maxobs)
     pos = jnp.concatenate([cell_id // columns, cell_id % columns], axis=0).astype(F32)
-    rate = jnp.where(
-        (jnp.arange(fields, dtype=jnp.int32) % levels == 0)[:, None],
-        jnp.repeat(dep_velocity, levels)[:, None],
-        0.0,
-    )
-    factor = jnp.exp(-rate[None] * surface_factor[:, None, :])
-
+
+    smem = pl.BlockSpec(memory_space=pltpu.SMEM)
     groups = per // 4
     hi, lo = call(
         weights_kernel,
@@ -474,7 +513,8 @@
             pltpu.VMEM((2 * groups, 8, 128), F32),
         ],
         flops=10**10,
-    )(low, packed, high, idx, pos)
+        specs=[smem] + [VMEM] * 5,
+    )(odd, near_a, packed, near_b, idx, pos)
     back = call(
         transform_kernel,
         [jax.ShapeDtypeStruct((groups_mem, local, 40, 128), BF16)],
@@ -482,15 +522,38 @@
         flops=10**9,
     )(hi, lo, state)[0]
     returned = lax.all_to_all(back, "mem", 0, 0, tiled=True)
-    part_shape = jax.ShapeDtypeStruct((tile_rows, local // chunks, fields, columns), BF16)
-    parts = call(relayout_kernel, [part_shape] * chunks, flops=10**8)(returned)
-    halos = [(from_low(x), from_high(x)) for x in parts]
-    outs = [
-        call(advect_kernel, part_shape, flops=10**9)(below, x, above, low, packed, high, factor)
-        for x, (below, above) in zip(parts, halos)
-    ]
-    done = jnp.concatenate(outs, axis=1)
-    return jnp.transpose(done, (1, 2, 0, 3))
+    parts = call(
+        relayout_kernel,
+        [jax.ShapeDtypeStruct((tile_rows, n, fields, columns), BF16) for n in sizes],
+        flops=10**8,
+    )(returned)
+    halos = [(swap(x, 0), swap(x, 1)) for x in parts]
+
+    done, block = None, 2 * tile_rows * fields
+    start = 0
+    for n, x, (side_a, side_b) in zip(sizes, parts, halos):
+        operands = [odd, side_a, x, side_b, near_a, packed, near_b]
+        operands += [dep_velocity.reshape(1, -1), surface_factor]
+        in_specs = [smem] + [VMEM] * 8
+        if done is not None:
+            operands.append(done)
+            in_specs.append(pl.BlockSpec(memory_space=pl.ANY))
+        done = pl.pallas_call(
+            advect_kernel,
+            out_shape=jax.ShapeDtypeStruct(flat.shape, BF16),
+            grid=(n // 2,),
+            in_specs=in_specs,
+            out_specs=pl.BlockSpec((block, columns), functools.partial(block_at, start // 2)),
+            scratch_shapes=[
+                pltpu.VMEM((tile_rows, fields, columns), F32),
+                pltpu.VMEM((block, columns), F32),
+            ],
+            input_output_aliases={} if start == 0 else {9: 0},
+            compiler_params=params(),
+            cost_estimate=cost(10**9),
+        )(*operands)
+        start += n
+    return done.reshape(local, fields, tile_rows, columns)
 
 
 def solution(mesh):

time: 87.1 us -> 79.9 us (0.917)
  the two profiles are of different devices: /device:TPU:230 before, /device:TPU:384 now
where the time goes in v2:
time: 79.9 us; the launch traced here: 79.3 us
  starting transfers between devices  30.1 us (38%)
  Pallas kernels  17.9 us (22%)
  blocking collectives  14.2 us (18%)
  waiting for transfers between devices  14.1 us (18%)
  local copies, waits for them, and re-layouts  2.66 us (3%)
    ppermute x6, starting transfers between devices, swap(): return lax.ppermute(x, 'space', pairs)  22.1 us
    all_to_all x1, blocking collectives, shards(): returned = lax.all_to_all(back, 'mem', 0, 0, tiled=True)  14.2 us
    ppermute x6, waiting for transfers between devices, swap(): return lax.ppermute(x, 'space', pairs)  8.61 us
    pallas_call x1, Pallas kernels, shards(): call(weights_kernel, [jax.ShapeDtypeStruct((groups, 64, 256), BF16)] * 2,...  7.18 us
    all_to_all x1, starting transfers between devices, shards(): everywhere = lax.all_to_all(equiv, 'mem', 0, 0, tiled=True)  4.49 us
    pallas_call x2, Pallas kernels, shards(): pl.pallas_call(advect_kernel, out_shape=jax.ShapeDtypeStruct(flat.shape,...  4.46 us
    all_to_all x1, waiting for transfers between devices, shards(): state = lax.all_to_all(payload, 'mem', 0, 0, tiled=True)  4.1 us
    all_to_all x1, starting transfers between devices, shards(): state = lax.all_to_all(payload, 'mem', 0, 0, tiled=True)  3.55 us
  transfers between devices with their start and end apart: 8, of which 5 were waited for; matrix products, arithmetic and copies ran while one was open for 1% of the time, Pallas kernels for 15%

profile of v2, /device:TPU:384, one launch (start us, length us, event | category | flops | bytes accessed | tf_op | source)
XLA Modules:
  0.0 79.3 jit_solution(15323383222667668088)
XLA Ops:
  0.0 2.6 %shard_map.110 = f32[8,8,256]{2,1,0:T(8,128)} custom-call(bf16[2560,128]{1,0:T(8,128)(2,1)} %bitcast.6, s32[1,256]{1,0:T(1,128)} %cell.3, s32[1,256]{1,0:T(1,128)} %kind.1), custom_call_target="tpu_custom_call" | custom-call | flops 100000000 | bytes 1000000 | tf_op jit(solution)/shard_map/pallas_call | solution.py:469
  2.6 4.5 %all-to-all-start = ((f32[8,8,256]{2,1,0:T(8,128)}), f32[8,8,256]{2,1,0:T(8,128)S(1)}, u32[]{:S(2)}, u32[]{:S(2)}) async-start(f32[8,8,256]{2,1,0:T(8,128)} %shard_map.110), calls=%async_computation | async-start | bytes 131072 | tf_op jit(solution)/shard_map/all_to_all | solution.py:481
  7.1 0.1 broadcast_in_dim.12
  7.2 0.1 reshape.200
  7.3 0.5 copy-done.9
  7.8 0.1 iota_compare_fusion
  7.9 0.1 lt.42
  8.0 0.1 squeeze.3
  8.2 0.6 copy-done.4
  8.8 0.0 copy-done.5
  8.8 0.0 copy-done.2
  8.8 0.0 copy-done.1
  8.9 1.1 %copy-done = bf16[8,160,2,128]{3,2,1,0:T(2,128)(2,1)S(1)} copy-done((bf16[8,160,2,128]{3,2,1,0:T(2,128)(2,1)S(1)}, bf16[8,160,2,128]{3,2,1,0:T(2,128)(2,1)}, u32[]{:S(2)}) %copy-start) | copy-done | bytes 655384
  10.0 1.4 %shard_map.109 = (bf16[8,320,128]{2,1,0:T(8,128)(2,1)}, f32[16,256]{1,0:T(8,128)S(1)}) custom-call(bf16[2560,128]{1,0:T(8,128)(2,1)S(1)} %bitcast.7, s32[1,256]{1,0:T(1,128)S(1)} %copy-done.3, f32[1,256]{1,0:T(1,128)S(1)} %copy-done.4, f32[1,256]{1,0:T(1,128)S(1)} %copy-done.5, f32[4,2,128]{2,1,0:T(2,128)S(1)} %copy-done.1, f32[4,2,128]{2,1,0:T(2,128)S(1)} %copy-done.2), custom_call_target="tpu_custom_call" | custom-call | flops 100000000 | bytes 1000000 | tf_op jit(solution)/shard_map/pallas_call | solution.py:482
  11.3 1.4 %all-to-all-done = f32[8,8,256]{2,1,0:T(8,128)S(1)} async-done(((f32[8,8,256]{2,1,0:T(8,128)}), f32[8,8,256]{2,1,0:T(8,128)S(1)}, u32[]{:S(2)}, u32[]{:S(2)}) %all-to-all-start) | async-done | bytes 65568 | tf_op jit(solution)/shard_map/all_to_all | solution.py:481
  12.7 3.4 %collective-permute-start = (f32[80,256]{1,0:T(8,128)S(1)}, f32[80,256]{1,0:T(8,128)S(1)}, u32[]{:S(2)}, u32[]{:S(2)}) collective-permute-start(f32[80,256]{1,0:T(8,128)S(1)} %pad_maximum_fusion.own.co_ref), channel_id=1, source_target_pairs={{0,1},{1,0},{2,3},{3,2},{4,5},{5,4},{6,7},{7,6},{8,9},{9,8},{10,11... | collective-permute-start | bytes 245768 | tf_op jit(solution)/shard_map/ppermute | solution.py:439
  16.1 5.7 %collective-permute-start.1 = (f32[80,256]{1,0:T(8,128)S(1)}, f32[80,256]{1,0:T(8,128)S(1)}, u32[]{:S(2)}, u32[]{:S(2)}) collective-permute-start(f32[80,256]{1,0:T(8,128)S(1)} %pad_maximum_fusion.own.co_ref), channel_id=1, source_target_pairs={{1,2},{2,1},{3,4},{4,3},{5,6},{6,5},{7,8},{8,7},{9,10},{10,9},{11,... | collective-permute-start | bytes 245768 | tf_op jit(solution)/shard_map/ppermute | solution.py:439
  21.8 3.6 %all-to-all-start.1 = ((bf16[8,320,128]{2,1,0:T(8,128)(2,1)}), bf16[8,320,128]{2,1,0:T(8,128)(2,1)S(1)}, u32[]{:S(2)}, u32[]{:S(2)}) async-start(bf16[8,320,128]{2,1,0:T(8,128)(2,1)} %get-tuple-element.18), calls=%async_computation.1 | async-start | bytes 1310720 | tf_op jit(solution)/shard_map/all_to_all | solution.py:494
  25.4 0.4 collective-permute-done.1.near_b.cb_ref
  25.8 7.2 %shard_map.111 = (bf16[8,64,256]{2,1,0:T(8,128)(2,1)S(1)}, bf16[8,64,256]{2,1,0:T(8,128)(2,1)S(1)}) custom-call(s32[1,1]{1,0:T(1,128)} %bitcast.odd, f32[80,256]{1,0:T(8,128)S(1)} %collective-permute-done.near_a.ca_ref, f32[80,256]{1,0:T(8,128)S(1)} %pad_maximum_fusion.own.co_ref, f32[80,256]{1,0:T(8,128)S(1)} %collective-permute-done.1.near_b.cb_ref, ...), custom_call_target="tpu_custom_call" | custom-call | flops 10000000000 | bytes 1000000 | tf_op jit(solution)/shard_map/pallas_call | solution.py:505
  33.0 4.1 %all-to-all-done.1.x_ref = bf16[8,320,128]{2,1,0:T(8,128)(2,1)S(1)} async-done(((bf16[8,320,128]{2,1,0:T(8,128)(2,1)}), bf16[8,320,128]{2,1,0:T(8,128)(2,1)S(1)}, u32[]{:S(2)}, u32[]{:S(2)}) %all-to-all-start.1) | async-done | bytes 655392 | tf_op jit(solution)/shard_map/all_to_all | solution.py:494
  37.1 1.8 %shard_map.112 = bf16[8,8,40,128]{3,2,1,0:T(8,128)(2,1)S(1)} custom-call(bf16[8,64,256]{2,1,0:T(8,128)(2,1)S(1)} %get-tuple-element.16.hi_ref, bf16[8,64,256]{2,1,0:T(8,128)(2,1)S(1)} %get-tuple-element.17.lo_ref, bf16[8,320,128]{2,1,0:T(8,128)(2,1)S(1)} %all-to-all-done.1.x_ref), custom_call_target="tpu_custom_call" | custom-call | flops 1000000000 | bytes 1000000 | tf_op jit(solution)/shard_map/pallas_call | solution.py:518
  38.9 14.2 %all_to_all.15.x_ref = bf16[8,8,40,128]{3,2,1,0:T(8,128)(2,1)S(1)} all-to-all(bf16[8,8,40,128]{3,2,1,0:T(8,128)(2,1)S(1)} %shard_map.112), channel_id=1, replica_groups=mesh['mem'=8,'space'=64] {'mem'}, dimensions={0} | all-to-all | bytes 1310720 | tf_op jit(solution)/shard_map/all_to_all | solution.py:524
  53.1 0.5 shard_map.113
  53.6 1.9 %collective-permute-start.4 = (bf16[2,6,160,128]{3,2,1,0:T(8,128)(2,1)S(1)}, bf16[2,6,160,128]{3,2,1,0:T(8,128)(2,1)S(1)}, u32[]{:S(2)}, u32[]{:S(2)}) collective-permute-start(bf16[2,6,160,128]{3,2,1,0:T(8,128)(2,1)S(1)} %get-tuple-element.20.own_ref), channel_id=1, source_target_pairs={{0,1},{1,0},{2,3},{3,2},{4,5},{5,4},{6,7},{7,6},{8,9},{9,8},{10,11... | collective-permute-start | bytes 1474568 | tf_op jit(solution)/shard_map/ppermute | solution.py:439
  55.5 3.5 %collective-permute-start.5 = (bf16[2,6,160,128]{3,2,1,0:T(8,128)(2,1)S(1)}, bf16[2,6,160,128]{3,2,1,0:T(8,128)(2,1)S(1)}, u32[]{:S(2)}, u32[]{:S(2)}) collective-permute-start(bf16[2,6,160,128]{3,2,1,0:T(8,128)(2,1)S(1)} %get-tuple-element.20.own_ref), channel_id=1, source_target_pairs={{1,2},{2,1},{3,4},{4,3},{5,6},{6,5},{7,8},{8,7},{9,10},{10,9},{11,... | collective-permute-start | bytes 1474568 | tf_op jit(solution)/shard_map/ppermute | solution.py:439
  59.0 2.4 %collective-permute-start.2 = (bf16[2,2,160,128]{3,2,1,0:T(8,128)(2,1)S(1)}, bf16[2,2,160,128]{3,2,1,0:T(8,128)(2,1)S(1)}, u32[]{:S(2)}, u32[]{:S(2)}) collective-permute-start(bf16[2,2,160,128]{3,2,1,0:T(8,128)(2,1)S(1)} %get-tuple-element.19.own_ref), channel_id=1, source_target_pairs={{0,1},{1,0},{2,3},{3,2},{4,5},{5,4},{6,7},{7,6},{8,9},{9,8},{10,11... | collective-permute-start | bytes 491528 | tf_op jit(solution)/shard_map/ppermute | solution.py:439
  61.4 5.2 %collective-permute-start.3 = (bf16[2,2,160,128]{3,2,1,0:T(8,128)(2,1)S(1)}, bf16[2,2,160,128]{3,2,1,0:T(8,128)(2,1)S(1)}, u32[]{:S(2)}, u32[]{:S(2)}) collective-permute-start(bf16[2,2,160,128]{3,2,1,0:T(8,128)(2,1)S(1)} %get-tuple-element.19.own_ref), channel_id=1, source_target_pairs={{1,2},{2,1},{3,4},{4,3},{5,6},{6,5},{7,8},{8,7},{9,10},{10,9},{11,... | collective-permute-start | bytes 491528 | tf_op jit(solution)/shard_map/ppermute | solution.py:439
  66.6 3.0 %collective-permute-done.4.a_ref = bf16[2,6,160,128]{3,2,1,0:T(8,128)(2,1)S(1)} collective-permute-done((bf16[2,6,160,128]{3,2,1,0:T(8,128)(2,1)S(1)}, bf16[2,6,160,128]{3,2,1,0:T(8,128)(2,1)S(1)}, u32[]{:S(2)}, u32[]{:S(2)}) %collective-permute-start.4) | collective-permute-done | bytes 491552 | tf_op jit(solution)/shard_map/ppermute | solution.py:439
  69.6 5.2 %collective-permute-done.5.b_ref = bf16[2,6,160,128]{3,2,1,0:T(8,128)(2,1)S(1)} collective-permute-done((bf16[2,6,160,128]{3,2,1,0:T(8,128)(2,1)S(1)}, bf16[2,6,160,128]{3,2,1,0:T(8,128)(2,1)S(1)}, u32[]{:S(2)}, u32[]{:S(2)}) %collective-permute-start.5) | collective-permute-done | bytes 491552 | tf_op jit(solution)/shard_map/ppermute | solution.py:439
  74.9 3.0 %shard_map.114.refs_0_ = bf16[2560,128]{1,0:T(8,128)(2,1)} custom-call(s32[1,1]{1,0:T(1,128)} %bitcast.odd, bf16[2,6,160,128]{3,2,1,0:T(8,128)(2,1)S(1)} %collective-permute-done.4.a_ref, bf16[2,6,160,128]{3,2,1,0:T(8,128)(2,1)S(1)} %get-tuple-element.20.own_ref, bf16[2,6,160,128]{3,2,1,0:T(8,128)(2,1)S(1)} %collective-permute-done.5.b_ref, ...), custom_call_target="tpu_custom_call" | custom-call | flops 1000000000 | bytes 1000000 | tf_op jit(solution)/shard_map/pallas_call | solution.py:541
  77.9 1.4 %shard_map.115 = bf16[2560,128]{1,0:T(8,128)(2,1)} custom-call(s32[1,1]{1,0:T(1,128)} %bitcast.odd, bf16[2,2,160,128]{3,2,1,0:T(8,128)(2,1)S(1)} %collective-permute-done.2.a_ref, bf16[2,2,160,128]{3,2,1,0:T(8,128)(2,1)S(1)} %get-tuple-element.19.own_ref, bf16[2,2,160,128]{3,2,1,0:T(8,128)(2,1)S(1)} %collective-permute-done.3.b_ref, ...), custom_call_target="tpu_custom_call", output_to_operand_aliasing={{}: (9, {})} | custom-call | flops 1000000000 | bytes 1000000 | tf_op jit(solution)/shard_map/pallas_call | solution.py:541
  (23 shorter events, 0.1 us)
Async XLA Ops:
  2.6 10.1 %all-to-all-start = ((f32[8,8,256]{2,1,0:T(8,128)}), f32[8,8,256]{2,1,0:T(8,128)S(1)}, u32[]{:S(2)}, u32[]{:S(2)}) async-start(f32[8,8,256]{2,1,0:T(8,128)} %shard_map.110), calls=%async_computation | async-start | bytes 131072 | tf_op jit(solution)/shard_map/all_to_all | solution.py:481
  7.2 0.7 copy-start.9
  7.3 0.7 copy-start.8
  8.1 0.7 copy-start.4
  8.1 0.7 copy-start.5
  8.1 0.7 copy-start.2
  8.2 0.7 copy-start.1
  8.2 0.7 copy-start.3
  8.9 1.1 %copy-start = (bf16[8,160,2,128]{3,2,1,0:T(2,128)(2,1)S(1)}, bf16[8,160,2,128]{3,2,1,0:T(2,128)(2,1)}, u32[]{:S(2)}) copy-start(bf16[8,160,2,128]{3,2,1,0:T(2,128)(2,1)} %param.11) | copy-start | bytes 1966084
  12.7 12.7 %collective-permute-start = (f32[80,256]{1,0:T(8,128)S(1)}, f32[80,256]{1,0:T(8,128)S(1)}, u32[]{:S(2)}, u32[]{:S(2)}) collective-permute-start(f32[80,256]{1,0:T(8,128)S(1)} %pad_maximum_fusion.own.co_ref), channel_id=1, source_target_pairs={{0,1},{1,0},{2,3},{3,2},{4,5},{5,4},{6,7},{7,6},{8,9},{9,8},{10,11... | collective-permute-start | bytes 245768 | tf_op jit(solution)/shard_map/ppermute | solution.py:439
  16.1 9.7 %collective-permute-start.1 = (f32[80,256]{1,0:T(8,128)S(1)}, f32[80,256]{1,0:T(8,128)S(1)}, u32[]{:S(2)}, u32[]{:S(2)}) collective-permute-start(f32[80,256]{1,0:T(8,128)S(1)} %pad_maximum_fusion.own.co_ref), channel_id=1, source_target_pairs={{1,2},{2,1},{3,4},{4,3},{5,6},{6,5},{7,8},{8,7},{9,10},{10,9},{11,... | collective-permute-start | bytes 245768 | tf_op jit(solution)/shard_map/ppermute | solution.py:439
  21.8 15.2 %all-to-all-start.1 = ((bf16[8,320,128]{2,1,0:T(8,128)(2,1)}), bf16[8,320,128]{2,1,0:T(8,128)(2,1)S(1)}, u32[]{:S(2)}, u32[]{:S(2)}) async-start(bf16[8,320,128]{2,1,0:T(8,128)(2,1)} %get-tuple-element.18), calls=%async_computation.1 | async-start | bytes 1310720 | tf_op jit(solution)/shard_map/all_to_all | solution.py:494
  53.6 16.0 %collective-permute-start.4 = (bf16[2,6,160,128]{3,2,1,0:T(8,128)(2,1)S(1)}, bf16[2,6,160,128]{3,2,1,0:T(8,128)(2,1)S(1)}, u32[]{:S(2)}, u32[]{:S(2)}) collective-permute-start(bf16[2,6,160,128]{3,2,1,0:T(8,128)(2,1)S(1)} %get-tuple-element.20.own_ref), channel_id=1, source_target_pairs={{0,1},{1,0},{2,3},{3,2},{4,5},{5,4},{6,7},{7,6},{8,9},{9,8},{10,11... | collective-permute-start | bytes 1474568 | tf_op jit(solution)/shard_map/ppermute | solution.py:439
  55.5 19.4 %collective-permute-start.5 = (bf16[2,6,160,128]{3,2,1,0:T(8,128)(2,1)S(1)}, bf16[2,6,160,128]{3,2,1,0:T(8,128)(2,1)S(1)}, u32[]{:S(2)}, u32[]{:S(2)}) collective-permute-start(bf16[2,6,160,128]{3,2,1,0:T(8,128)(2,1)S(1)} %get-tuple-element.20.own_ref), channel_id=1, source_target_pairs={{1,2},{2,1},{3,4},{4,3},{5,6},{6,5},{7,8},{8,7},{9,10},{10,9},{11,... | collective-permute-start | bytes 1474568 | tf_op jit(solution)/shard_map/ppermute | solution.py:439
  59.0 15.9 %copy-start.6 = (f32[2,128]{1,0:T(2,128)S(1)}, f32[2,128]{1,0:T(2,128)}, u32[]{:S(2)}) copy-start(f32[2,128]{1,0:T(2,128)} %surf_ref.3) | copy-start | bytes 3076
  59.0 15.9 %copy-start.7 = (f32[40]{0:T(128)S(1)}, f32[40]{0:T(128)}, u32[]{:S(2)}) copy-start(f32[40]{0:T(128)} %param.20) | copy-start | bytes 484
  59.0 18.9 %collective-permute-start.2 = (bf16[2,2,160,128]{3,2,1,0:T(8,128)(2,1)S(1)}, bf16[2,2,160,128]{3,2,1,0:T(8,128)(2,1)S(1)}, u32[]{:S(2)}, u32[]{:S(2)}) collective-permute-start(bf16[2,2,160,128]{3,2,1,0:T(8,128)(2,1)S(1)} %get-tuple-element.19.own_ref), channel_id=1, source_target_pairs={{0,1},{1,0},{2,3},{3,2},{4,5},{5,4},{6,7},{7,6},{8,9},{9,8},{10,11... | collective-permute-start | bytes 491528 | tf_op jit(solution)/shard_map/ppermute | solution.py:439
  61.4 16.5 %collective-permute-start.3 = (bf16[2,2,160,128]{3,2,1,0:T(8,128)(2,1)S(1)}, bf16[2,2,160,128]{3,2,1,0:T(8,128)(2,1)S(1)}, u32[]{:S(2)}, u32[]{:S(2)}) collective-permute-start(bf16[2,2,160,128]{3,2,1,0:T(8,128)(2,1)S(1)} %get-tuple-element.19.own_ref), channel_id=1, source_target_pairs={{1,2},{2,1},{3,4},{4,3},{5,6},{6,5},{7,8},{8,7},{9,10},{10,9},{11,... | collective-permute-start | bytes 491528 | tf_op jit(solution)/shard_map/ppermute | solution.py:439

commit v3 on v2

--- a/solution.py
+++ b/solution.py
@@ -214,12 +214,23 @@
         o_ref[d] = full
 
 
-def payload_kernel(ens, cell, value, error, wind_x, wind_y, o_ref, info, flat, main, rest):
+def payload_kernel(
+    ens, cell, value, error, wind_x, wind_y, o_ref, info, flat, main, rest, held, ints, floats, winds, sems
+):
     local = 8
-    fields = ens.shape[0] // (2 * local)
+    span = ens.shape[0] // local
+    fields = span // 2
+    jobs = [(ens.at[pl.ds(m * span, span)], held.at[pl.ds(m * span, span)]) for m in range(local)]
+    jobs += [(cell, ints), (value, floats.at[0]), (error, floats.at[1])]
+    jobs += [(wind_x, winds.at[0]), (wind_y, winds.at[1])]
+    copies = [pltpu.make_async_copy(src, dst, sems.at[n]) for n, (src, dst) in enumerate(jobs)]
+    for copy in copies:
+        copy.start()
     ident = (iota((128, 128), 0) == iota((128, 128), 1)).astype(F32).astype(BF16)
     lane = iota((8, 128), 1) // 32
-    flat[...] = ens[...].astype(F32)
+    for m in range(local):
+        copies[m].wait()
+        flat[m * span : m * span + span] = held[m * span : m * span + span].astype(F32)
 
     def turned(n):
         row, m = n // local, n % local
@@ -243,20 +254,22 @@
     for dest in range(8):
         o_ref[dest, :256] = main[dest * 256 : dest * 256 + 256, :].astype(BF16)
         o_ref[dest, 256:] = rest[dest * 64 : dest * 64 + 64, :].astype(BF16)
-    cells = cell[...]
+    for copy in copies[local:]:
+        copy.wait()
+    cells = ints[...]
     n_obs = cells.shape[1]
     row = (cells >= 128).astype(jnp.int32)
     sub = iota((8, n_obs), 0)
-    lines = [value[...], error[...], row.astype(F32), (cells - 128 * row).astype(F32)]
+    lines = [floats[0], floats[1], row.astype(F32), (cells - 128 * row).astype(F32)]
     top = jnp.zeros((8, n_obs), F32)
     for r, line in enumerate(lines):
         top = jnp.where(sub == r, line, top)
     info[:8] = top
-    for axis, wind in enumerate((wind_x, wind_y)):
+    for axis in range(2):
         for level in range(4):
             for half in range(2):
                 info[8 + axis * 4 + level : 9 + axis * 4 + level, half * 128 : half * 128 + 128] = (
-                    wind[level, half : half + 1]
+                    winds[axis, level, half : half + 1]
                 )
 
 
@@ -333,8 +346,8 @@
             out[row, k] = mm_nt(ident, full).astype(BF16)
 
 
-def advect_kernel(odd, a_ref, own_ref, b_ref, ca_ref, co_ref, cb_ref, dep_ref, surf_ref, *refs):
-    o_ref, fac, flat = refs[-3:]
+def advect_kernel(start, odd, a_ref, own_ref, b_ref, ca_ref, co_ref, cb_ref, dep_ref, surf_ref, *refs):
+    o_ref, fac, flat, ready, sems = refs[-5:]
     fields = own_ref.shape[2]
     is_odd = odd[0, 0] == 1
     lane = iota((8, 128), 1)
@@ -354,12 +367,10 @@
         a, b, c = coeffs(w, 0, k)
         cx.append((jnp.where(lane == 0, 0.0, a), b, jnp.where(lane == 127, 0.0, c)))
 
-    @pl.when(pl.program_id(0) == 0)
-    def _():
-        own_level = iota((fields, dep_ref.shape[1]), 0) == 4 * iota((fields, dep_ref.shape[1]), 1)
-        rate = jnp.sum(jnp.where(own_level, dep_ref[...], 0.0), axis=1, keepdims=True)
-        for row in range(2):
-            fac[row] = jnp.exp(-rate * surf_ref[row : row + 1, :])
+    own_level = iota((fields, dep_ref.shape[1]), 0) == 4 * iota((fields, dep_ref.shape[1]), 1)
+    rate = jnp.sum(jnp.where(own_level, dep_ref[...], 0.0), axis=1, keepdims=True)
+    for row in range(2):
+        fac[row] = jnp.exp(-rate * surf_ref[row : row + 1, :])
 
     shift_in, shift_out = iota((256, 256), 0) % 128, iota((256, 256), 1)
     shift = (
@@ -386,11 +397,10 @@
             outs.append(scale(a, near[:, :128]) + scale(b, q) + scale(c, near[:, 128:]))
         return outs
 
-    members = o_ref.shape[0] // (2 * fields)
+    members, span = own_ref.shape[1], 2 * fields
     units = [(m, f) for m in range(members) for f in range(0, fields, part)]
 
-    def first(j, f):
-        m = pl.program_id(0) * members + j
+    def first(m, f):
         near = [
             by_parity(is_odd, a_ref[k, m, f : f + part], b_ref[k, m, f : f + part])
             for k in range(2)
@@ -402,15 +412,26 @@
 
     ahead = 2
     mids = {u: first(*units[u]) for u in range(ahead)}
-    for u, (j, f) in enumerate(units):
+    copies = []
+    for u, (m, f) in enumerate(units):
         if u + ahead < len(units):
             mids[u + ahead] = first(*units[u + ahead])
         q1 = mids.pop(u)
         q2 = cols([rows(q1[i], q1[i + 1], q1[i + 2], i + 1) for i in range(2)], 1)
-        base = (j * fields + f) * 2
+        base = m * span + 2 * f
         for r in range(2):
             flat[pl.ds(base + r, part, stride=2), :] = q2[r] * fac[r, f : f + part]
-        o_ref[base : base + 2 * part] = flat[base : base + 2 * part, :].astype(BF16)
+        ready[base : base + 2 * part] = flat[base : base + 2 * part, :].astype(BF16)
+        if f + part == fields:
+            copy = pltpu.make_async_copy(
+                ready.at[pl.ds(m * span, span)],
+                o_ref.at[pl.ds((start + m) * span, span)],
+                sems.at[m],
+            )
+            copy.start()
+            copies.append(copy)
+    for copy in copies:
+        copy.wait()
 
 
 def params():
@@ -437,10 +458,6 @@
     for low in range(first, lax.axis_size("space") - 1, 2):
         pairs += [(low, low + 1), (low + 1, low)]
     return lax.ppermute(x, "space", pairs)
-
-
-def block_at(first, i):
-    return first + i, 0
 
 
 def shards(
@@ -463,7 +480,7 @@
     maxobs = patch_index.shape[2]
     groups_mem = 8
 
-    sizes = (6, 2)
+    sizes = (4, 4)
     flat = ensemble.reshape(local * fields * tile_rows, columns)
     hbm = pl.BlockSpec(memory_space=pltpu.HBM)
     equiv = pl.pallas_call(
@@ -479,17 +496,30 @@
         cost_estimate=cost(10**8),
     )(flat, obs_cell, obs_species)
     everywhere = lax.all_to_all(equiv, "mem", 0, 0, tiled=True)
-    payload, info = call(
+    payload, info = pl.pallas_call(
         payload_kernel,
-        [
+        out_shape=[
             jax.ShapeDtypeStruct((groups_mem, 320, 128), BF16),
             jax.ShapeDtypeStruct((16, n_obs), F32),
         ],
-        [pltpu.VMEM(flat.shape, F32), pltpu.VMEM((2048, 128), F32), pltpu.VMEM((512, 128), F32)],
-        flops=10**8,
+        in_specs=[hbm] * 6,
+        scratch_shapes=[
+            pltpu.VMEM(flat.shape, F32),
+            pltpu.VMEM((2048, 128), F32),
+            pltpu.VMEM((512, 128), F32),
+            pltpu.VMEM(flat.shape, BF16),
+            pltpu.VMEM((1, n_obs), jnp.int32),
+            pltpu.VMEM((2, 1, n_obs), F32),
+            pltpu.VMEM((2, levels, tile_rows, columns), F32),
+            pltpu.SemaphoreType.DMA((local + 5,)),
+        ],
+        compiler_params=pltpu.CompilerParams(vmem_limit_bytes=66900000),
+        cost_estimate=cost(10**8),
     )(flat, obs_cell, obs_value, obs_error, courant_x, courant_y)
     packed = jnp.concatenate([everywhere.reshape(groups_mem * local, n_obs), info], axis=0)
-    payload, packed = lax.optimization_barrier((payload, packed))
+    payload, packed, patch_index, patch_count = lax.optimization_barrier(
+        (payload, packed, patch_index, patch_count)
+    )
     near_a, near_b = swap(packed, 0), swap(packed, 1)
     state = lax.all_to_all(payload, "mem", 0, 0, tiled=True)
     odd = (lax.axis_index("space") % 2).reshape(1, 1)
@@ -512,7 +542,7 @@
             pltpu.VMEM((2 * groups, 16, 128), F32),
             pltpu.VMEM((2 * groups, 8, 128), F32),
         ],
-        flops=10**10,
+        flops=10**7,
         specs=[smem] + [VMEM] * 5,
     )(odd, near_a, packed, near_b, idx, pos)
     back = call(
@@ -529,24 +559,25 @@
     )(returned)
     halos = [(swap(x, 0), swap(x, 1)) for x in parts]
 
-    done, block = None, 2 * tile_rows * fields
-    start = 0
+    done, start = None, 0
     for n, x, (side_a, side_b) in zip(sizes, parts, halos):
         operands = [odd, side_a, x, side_b, near_a, packed, near_b]
         operands += [dep_velocity.reshape(1, -1), surface_factor]
         in_specs = [smem] + [VMEM] * 8
         if done is not None:
             operands.append(done)
-            in_specs.append(pl.BlockSpec(memory_space=pl.ANY))
+            in_specs.append(hbm)
+        span = n * fields * tile_rows
         done = pl.pallas_call(
-            advect_kernel,
+            functools.partial(advect_kernel, start),
             out_shape=jax.ShapeDtypeStruct(flat.shape, BF16),
-            grid=(n // 2,),
             in_specs=in_specs,
-            out_specs=pl.BlockSpec((block, columns), functools.partial(block_at, start // 2)),
+            out_specs=hbm,
             scratch_shapes=[
                 pltpu.VMEM((tile_rows, fields, columns), F32),
-                pltpu.VMEM((block, columns), F32),
+                pltpu.VMEM((span, columns), F32),
+                pltpu.VMEM((span, columns), BF16),
+                pltpu.SemaphoreType.DMA((n,)),
             ],
             input_output_aliases={} if start == 0 else {9: 0},
             compiler_params=params(),

time: 79.9 us -> 82.3 us (1.030)
  local copies, waits for them, and re-layouts: 2.66 us -> 0.35 us
  blocking collectives: 14.2 us -> 16.2 us
    all_to_all x1, waiting for transfers between devices: 4.1 us -> 0.01 us  [shards(): state = lax.all_to_all(payload, 'mem', 0, 0, tiled=True)]
    ppermute x6, waiting for transfers between devices: 8.61 us -> 12 us  [swap(): return lax.ppermute(x, 'space', pairs)]
    unnamed x20 -> x8, local copies, waits for them, and re-layouts: 2.35 us -> 0.03 us
    all_to_all x1, blocking collectives: 14.2 us -> 16.2 us  [shards(): returned = lax.all_to_all(back, 'mem', 0, 0, tiled=True)]
    all_to_all x1, waiting for transfers between devices: 1.41 us -> 2.8 us  [shards(): everywhere = lax.all_to_all(equiv, 'mem', 0, 0, tiled=True)]
  transfers between devices with their start and end apart: 8 -> 8, of which waited for: 5 -> 5; matrix products, arithmetic and copies ran while one was open for 1% -> 1% of each run, Pallas kernels for 15% -> 14%
where the time goes in v3:
time: 82.3 us; the launch traced here: 81.7 us
  starting transfers between devices  30.5 us (37%)
  Pallas kernels  18.7 us (23%)
  blocking collectives  16.2 us (20%)
  waiting for transfers between devices  14.8 us (18%)
  other arithmetic  0.86 us (1%)
    ppermute x6, starting transfers between devices, swap(): return lax.ppermute(x, 'space', pairs)  22.5 us
    all_to_all x1, blocking collectives, shards(): returned = lax.all_to_all(back, 'mem', 0, 0, tiled=True)  16.2 us
    ppermute x6, waiting for transfers between devices, swap(): return lax.ppermute(x, 'space', pairs)  12 us
    pallas_call x1, Pallas kernels, shards(): call(weights_kernel, [jax.ShapeDtypeStruct((groups, 64, 256), BF16)] * 2,...  7.19 us
    all_to_all x1, starting transfers between devices, shards(): everywhere = lax.all_to_all(equiv, 'mem', 0, 0, tiled=True)  4.49 us
    pallas_call x2, Pallas kernels, shards(): pl.pallas_call(functools.partial(advect_kernel, start), out_shape=jax.Sha...  3.99 us
    all_to_all x1, starting transfers between devices, shards(): state = lax.all_to_all(payload, 'mem', 0, 0, tiled=True)  3.54 us
    all_to_all x1, waiting for transfers between devices, shards(): everywhere = lax.all_to_all(equiv, 'mem', 0, 0, tiled=True)  2.8 us
  transfers between devices with their start and end apart: 8, of which 5 were waited for; matrix products, arithmetic and copies ran while one was open for 1% of the time, Pallas kernels for 14%

profile of v3, /device:TPU:384, one launch (start us, length us, event | category | flops | bytes accessed | tf_op | source)
XLA Modules:
  0.0 81.7 jit_solution(17248734026736034275)
XLA Ops:
  0.0 2.6 %shard_map.110 = f32[8,8,256]{2,1,0:T(8,128)} custom-call(bf16[2560,128]{1,0:T(8,128)(2,1)} %bitcast.8, s32[1,256]{1,0:T(1,128)} %cell.3, s32[1,256]{1,0:T(1,128)} %kind.1), custom_call_target="tpu_custom_call" | custom-call | flops 100000000 | bytes 1000000 | tf_op jit(solution)/shard_map/pallas_call | solution.py:486
  2.6 4.5 %all-to-all-start = ((f32[8,8,256]{2,1,0:T(8,128)}), f32[8,8,256]{2,1,0:T(8,128)S(1)}, u32[]{:S(2)}, u32[]{:S(2)}) async-start(f32[8,8,256]{2,1,0:T(8,128)} %shard_map.110), calls=%async_computation | async-start | bytes 131072 | tf_op jit(solution)/shard_map/all_to_all | solution.py:498
  7.1 0.1 broadcast_in_dim.12
  7.2 0.1 reshape.200
  7.3 2.6 %shard_map.109 = (bf16[8,320,128]{2,1,0:T(8,128)(2,1)}, f32[16,256]{1,0:T(8,128)}) custom-call(bf16[2560,128]{1,0:T(8,128)(2,1)} %bitcast.9, s32[1,256]{1,0:T(1,128)} %cell.3, f32[1,256]{1,0:T(1,128)} %value.1, f32[1,256]{1,0:T(1,128)} %error.1, f32[4,2,128]{2,1,0:T(2,128)} %wind_x.1, f32[4,2,128]{2,1,0:T(2,128)} %wind_y.1), custom_call_target="tpu_custom_call" | custom-call | flops 100000000 | bytes 1000000 | tf_op jit(solution)/shard_map/pallas_call | solution.py:499
  9.9 2.8 %all-to-all-done = f32[8,8,256]{2,1,0:T(8,128)S(1)} async-done(((f32[8,8,256]{2,1,0:T(8,128)}), f32[8,8,256]{2,1,0:T(8,128)S(1)}, u32[]{:S(2)}, u32[]{:S(2)}) %all-to-all-start) | async-done | bytes 65568 | tf_op jit(solution)/shard_map/all_to_all | solution.py:498
  12.7 0.7 pad_maximum_fusion.own.co_ref
  13.5 3.5 %all-to-all-start.1 = ((bf16[8,320,128]{2,1,0:T(8,128)(2,1)}), bf16[8,320,128]{2,1,0:T(8,128)(2,1)S(1)}, u32[]{:S(2)}, u32[]{:S(2)}) async-start(bf16[8,320,128]{2,1,0:T(8,128)(2,1)} %get-tuple-element.22), calls=%async_computation.1 | async-start | bytes 1310720 | tf_op jit(solution)/shard_map/all_to_all | solution.py:524
  17.0 0.0 copy-start.2
  17.1 0.0 copy-start.3
  17.1 3.4 %collective-permute-start = (f32[80,256]{1,0:T(8,128)S(1)}, f32[80,256]{1,0:T(8,128)S(1)}, u32[]{:S(2)}, u32[]{:S(2)}) collective-permute-start(f32[80,256]{1,0:T(8,128)S(1)} %pad_maximum_fusion.own.co_ref), channel_id=1, source_target_pairs={{0,1},{1,0},{2,3},{3,2},{4,5},{5,4},{6,7},{7,6},{8,9},{9,8},{10,11... | collective-permute-start | bytes 245768 | tf_op jit(solution)/shard_map/ppermute | solution.py:460
  20.5 5.7 %collective-permute-start.1 = (f32[80,256]{1,0:T(8,128)S(1)}, f32[80,256]{1,0:T(8,128)S(1)}, u32[]{:S(2)}, u32[]{:S(2)}) collective-permute-start(f32[80,256]{1,0:T(8,128)S(1)} %pad_maximum_fusion.own.co_ref), channel_id=1, source_target_pairs={{1,2},{2,1},{3,4},{4,3},{5,6},{6,5},{7,8},{8,7},{9,10},{10,9},{11,... | collective-permute-start | bytes 245768 | tf_op jit(solution)/shard_map/ppermute | solution.py:460
  26.2 0.1 iota_compare_fusion
  26.2 0.1 lt.42
  26.3 0.1 squeeze.3
  26.4 3.7 %collective-permute-done.1.near_b.cb_ref = f32[80,256]{1,0:T(8,128)S(1)} collective-permute-done((f32[80,256]{1,0:T(8,128)S(1)}, f32[80,256]{1,0:T(8,128)S(1)}, u32[]{:S(2)}, u32[]{:S(2)}) %collective-permute-start.1) | collective-permute-done | bytes 81952 | tf_op jit(solution)/shard_map/ppermute | solution.py:460
  30.2 7.2 %shard_map.111 = (bf16[8,64,256]{2,1,0:T(8,128)(2,1)S(1)}, bf16[8,64,256]{2,1,0:T(8,128)(2,1)S(1)}) custom-call(s32[1,1]{1,0:T(1,128)} %bitcast.odd, f32[80,256]{1,0:T(8,128)S(1)} %collective-permute-done.near_a.ca_ref, f32[80,256]{1,0:T(8,128)S(1)} %pad_maximum_fusion.own.co_ref, f32[80,256]{1,0:T(8,128)S(1)} %collective-permute-done.1.near_b.cb_ref, ...), custom_call_target="tpu_custom_call" | custom-call | flops 10000000 | bytes 1000000 | tf_op jit(solution)/shard_map/pallas_call | solution.py:535
  37.4 0.0 all-to-all-done.1.x_ref
  37.4 1.8 %shard_map.112 = bf16[8,8,40,128]{3,2,1,0:T(8,128)(2,1)S(1)} custom-call(bf16[8,64,256]{2,1,0:T(8,128)(2,1)S(1)} %get-tuple-element.20.hi_ref, bf16[8,64,256]{2,1,0:T(8,128)(2,1)S(1)} %get-tuple-element.21.lo_ref, bf16[8,320,128]{2,1,0:T(8,128)(2,1)S(1)} %all-to-all-done.1.x_ref), custom_call_target="tpu_custom_call" | custom-call | flops 1000000000 | bytes 1000000 | tf_op jit(solution)/shard_map/pallas_call | solution.py:548
  39.2 16.2 %all_to_all.15.x_ref = bf16[8,8,40,128]{3,2,1,0:T(8,128)(2,1)S(1)} all-to-all(bf16[8,8,40,128]{3,2,1,0:T(8,128)(2,1)S(1)} %shard_map.112), channel_id=1, replica_groups=mesh['mem'=8,'space'=64] {'mem'}, dimensions={0} | all-to-all | bytes 1310720 | tf_op jit(solution)/shard_map/all_to_all | solution.py:554
  55.5 0.5 shard_map.113
  56.0 1.9 %collective-permute-start.4 = (bf16[2,4,160,128]{3,2,1,0:T(8,128)(2,1)S(1)}, bf16[2,4,160,128]{3,2,1,0:T(8,128)(2,1)S(1)}, u32[]{:S(2)}, u32[]{:S(2)}) collective-permute-start(bf16[2,4,160,128]{3,2,1,0:T(8,128)(2,1)S(1)} %get-tuple-element.24.own_ref), channel_id=1, source_target_pairs={{0,1},{1,0},{2,3},{3,2},{4,5},{5,4},{6,7},{7,6},{8,9},{9,8},{10,11... | collective-permute-start | bytes 983048 | tf_op jit(solution)/shard_map/ppermute | solution.py:460
  57.9 5.6 %collective-permute-start.5 = (bf16[2,4,160,128]{3,2,1,0:T(8,128)(2,1)S(1)}, bf16[2,4,160,128]{3,2,1,0:T(8,128)(2,1)S(1)}, u32[]{:S(2)}, u32[]{:S(2)}) collective-permute-start(bf16[2,4,160,128]{3,2,1,0:T(8,128)(2,1)S(1)} %get-tuple-element.24.own_ref), channel_id=1, source_target_pairs={{1,2},{2,1},{3,4},{4,3},{5,6},{6,5},{7,8},{8,7},{9,10},{10,9},{11,... | collective-permute-start | bytes 983048 | tf_op jit(solution)/shard_map/ppermute | solution.py:460
  63.6 0.0 copy-start
  63.6 0.0 copy-start.1
  63.6 1.9 %collective-permute-start.2 = (bf16[2,4,160,128]{3,2,1,0:T(8,128)(2,1)S(1)}, bf16[2,4,160,128]{3,2,1,0:T(8,128)(2,1)S(1)}, u32[]{:S(2)}, u32[]{:S(2)}) collective-permute-start(bf16[2,4,160,128]{3,2,1,0:T(8,128)(2,1)S(1)} %get-tuple-element.23.own_ref), channel_id=1, source_target_pairs={{0,1},{1,0},{2,3},{3,2},{4,5},{5,4},{6,7},{7,6},{8,9},{9,8},{10,11... | collective-permute-start | bytes 983048 | tf_op jit(solution)/shard_map/ppermute | solution.py:460
  65.5 3.9 %collective-permute-start.3 = (bf16[2,4,160,128]{3,2,1,0:T(8,128)(2,1)S(1)}, bf16[2,4,160,128]{3,2,1,0:T(8,128)(2,1)S(1)}, u32[]{:S(2)}, u32[]{:S(2)}) collective-permute-start(bf16[2,4,160,128]{3,2,1,0:T(8,128)(2,1)S(1)} %get-tuple-element.23.own_ref), channel_id=1, source_target_pairs={{1,2},{2,1},{3,4},{4,3},{5,6},{6,5},{7,8},{8,7},{9,10},{10,9},{11,... | collective-permute-start | bytes 983048 | tf_op jit(solution)/shard_map/ppermute | solution.py:460
  69.5 2.9 %collective-permute-done.5.b_ref = bf16[2,4,160,128]{3,2,1,0:T(8,128)(2,1)S(1)} collective-permute-done((bf16[2,4,160,128]{3,2,1,0:T(8,128)(2,1)S(1)}, bf16[2,4,160,128]{3,2,1,0:T(8,128)(2,1)S(1)}, u32[]{:S(2)}, u32[]{:S(2)}) %collective-permute-start.5) | collective-permute-done | bytes 327712 | tf_op jit(solution)/shard_map/ppermute | solution.py:460
  72.4 2.0 %shard_map.114.refs_0_ = bf16[2560,128]{1,0:T(8,128)(2,1)} custom-call(s32[1,1]{1,0:T(1,128)} %bitcast.odd, bf16[2,4,160,128]{3,2,1,0:T(8,128)(2,1)S(1)} %collective-permute-done.4.a_ref, bf16[2,4,160,128]{3,2,1,0:T(8,128)(2,1)S(1)} %get-tuple-element.24.own_ref, bf16[2,4,160,128]{3,2,1,0:T(8,128)(2,1)S(1)} %collective-permute-done.5.b_ref, ...), custom_call_target="tpu_custom_call" | custom-call | flops 1000000000 | bytes 1000000 | tf_op jit(solution)/shard_map/pallas_call | solution.py:571
  74.4 0.1 collective-permute-done.2.a_ref
  74.5 5.2 %collective-permute-done.3.b_ref = bf16[2,4,160,128]{3,2,1,0:T(8,128)(2,1)S(1)} collective-permute-done((bf16[2,4,160,128]{3,2,1,0:T(8,128)(2,1)S(1)}, bf16[2,4,160,128]{3,2,1,0:T(8,128)(2,1)S(1)}, u32[]{:S(2)}, u32[]{:S(2)}) %collective-permute-start.3) | collective-permute-done | bytes 327712 | tf_op jit(solution)/shard_map/ppermute | solution.py:460
  79.7 2.0 %shard_map.115 = bf16[2560,128]{1,0:T(8,128)(2,1)} custom-call(s32[1,1]{1,0:T(1,128)} %bitcast.odd, bf16[2,4,160,128]{3,2,1,0:T(8,128)(2,1)S(1)} %collective-permute-done.2.a_ref, bf16[2,4,160,128]{3,2,1,0:T(8,128)(2,1)S(1)} %get-tuple-element.23.own_ref, bf16[2,4,160,128]{3,2,1,0:T(8,128)(2,1)S(1)} %collective-permute-done.3.b_ref, ...), custom_call_target="tpu_custom_call", output_to_operand_aliasing={{}: (9, {})} | custom-call | flops 1000000000 | bytes 1000000 | tf_op jit(solution)/shard_map/pallas_call | solution.py:571
  (11 shorter events, 0.1 us)
Async XLA Ops:
  2.6 10.1 %all-to-all-start = ((f32[8,8,256]{2,1,0:T(8,128)}), f32[8,8,256]{2,1,0:T(8,128)S(1)}, u32[]{:S(2)}, u32[]{:S(2)}) async-start(f32[8,8,256]{2,1,0:T(8,128)} %shard_map.110), calls=%async_computation | async-start | bytes 131072 | tf_op jit(solution)/shard_map/all_to_all | solution.py:498
  13.5 23.9 %all-to-all-start.1 = ((bf16[8,320,128]{2,1,0:T(8,128)(2,1)}), bf16[8,320,128]{2,1,0:T(8,128)(2,1)S(1)}, u32[]{:S(2)}, u32[]{:S(2)}) async-start(bf16[8,320,128]{2,1,0:T(8,128)(2,1)} %get-tuple-element.22), calls=%async_computation.1 | async-start | bytes 1310720 | tf_op jit(solution)/shard_map/all_to_all | solution.py:524
  17.0 9.3 %copy-start.2 = (s32[1,32,32]{2,1,0:T(8,128)S(1)}, s32[1,32,32]{2,1,0:T(8,128)}, u32[]{:S(2)}) copy-start(s32[1,32,32]{2,1,0:T(8,128)} %param.16) | copy-start | bytes 12292
  17.1 9.1 %copy-start.3 = (s32[1,32]{1,0:T(1,128)S(1)}, s32[1,32]{1,0:T(1,128)}, u32[]{:S(2)}) copy-start(s32[1,32]{1,0:T(1,128)} %param.17) | copy-start | bytes 388
  17.1 9.4 %collective-permute-start = (f32[80,256]{1,0:T(8,128)S(1)}, f32[80,256]{1,0:T(8,128)S(1)}, u32[]{:S(2)}, u32[]{:S(2)}) collective-permute-start(f32[80,256]{1,0:T(8,128)S(1)} %pad_maximum_fusion.own.co_ref), channel_id=1, source_target_pairs={{0,1},{1,0},{2,3},{3,2},{4,5},{5,4},{6,7},{7,6},{8,9},{9,8},{10,11... | collective-permute-start | bytes 245768 | tf_op jit(solution)/shard_map/ppermute | solution.py:460
  20.5 9.7 %collective-permute-start.1 = (f32[80,256]{1,0:T(8,128)S(1)}, f32[80,256]{1,0:T(8,128)S(1)}, u32[]{:S(2)}, u32[]{:S(2)}) collective-permute-start(f32[80,256]{1,0:T(8,128)S(1)} %pad_maximum_fusion.own.co_ref), channel_id=1, source_target_pairs={{1,2},{2,1},{3,4},{4,3},{5,6},{6,5},{7,8},{8,7},{9,10},{10,9},{11,... | collective-permute-start | bytes 245768 | tf_op jit(solution)/shard_map/ppermute | solution.py:460
  56.0 13.5 %collective-permute-start.4 = (bf16[2,4,160,128]{3,2,1,0:T(8,128)(2,1)S(1)}, bf16[2,4,160,128]{3,2,1,0:T(8,128)(2,1)S(1)}, u32[]{:S(2)}, u32[]{:S(2)}) collective-permute-start(bf16[2,4,160,128]{3,2,1,0:T(8,128)(2,1)S(1)} %get-tuple-element.24.own_ref), channel_id=1, source_target_pairs={{0,1},{1,0},{2,3},{3,2},{4,5},{5,4},{6,7},{7,6},{8,9},{9,8},{10,11... | collective-permute-start | bytes 983048 | tf_op jit(solution)/shard_map/ppermute | solution.py:460
  57.9 14.5 %collective-permute-start.5 = (bf16[2,4,160,128]{3,2,1,0:T(8,128)(2,1)S(1)}, bf16[2,4,160,128]{3,2,1,0:T(8,128)(2,1)S(1)}, u32[]{:S(2)}, u32[]{:S(2)}) collective-permute-start(bf16[2,4,160,128]{3,2,1,0:T(8,128)(2,1)S(1)} %get-tuple-element.24.own_ref), channel_id=1, source_target_pairs={{1,2},{2,1},{3,4},{4,3},{5,6},{6,5},{7,8},{8,7},{9,10},{10,9},{11,... | collective-permute-start | bytes 983048 | tf_op jit(solution)/shard_map/ppermute | solution.py:460
  63.6 8.8 %copy-start = (f32[2,128]{1,0:T(2,128)S(1)}, f32[2,128]{1,0:T(2,128)}, u32[]{:S(2)}) copy-start(f32[2,128]{1,0:T(2,128)} %surf_ref.3) | copy-start | bytes 3076
  63.6 8.8 %copy-start.1 = (f32[40]{0:T(128)S(1)}, f32[40]{0:T(128)}, u32[]{:S(2)}) copy-start(f32[40]{0:T(128)} %param.20) | copy-start | bytes 484
  63.6 10.9 %collective-permute-start.2 = (bf16[2,4,160,128]{3,2,1,0:T(8,128)(2,1)S(1)}, bf16[2,4,160,128]{3,2,1,0:T(8,128)(2,1)S(1)}, u32[]{:S(2)}, u32[]{:S(2)}) collective-permute-start(bf16[2,4,160,128]{3,2,1,0:T(8,128)(2,1)S(1)} %get-tuple-element.23.own_ref), channel_id=1, source_target_pairs={{0,1},{1,0},{2,3},{3,2},{4,5},{5,4},{6,7},{7,6},{8,9},{9,8},{10,11... | collective-permute-start | bytes 983048 | tf_op jit(solution)/shard_map/ppermute | solution.py:460
  65.5 14.2 %collective-permute-start.3 = (bf16[2,4,160,128]{3,2,1,0:T(8,128)(2,1)S(1)}, bf16[2,4,160,128]{3,2,1,0:T(8,128)(2,1)S(1)}, u32[]{:S(2)}, u32[]{:S(2)}) collective-permute-start(bf16[2,4,160,128]{3,2,1,0:T(8,128)(2,1)S(1)} %get-tuple-element.23.own_ref), channel_id=1, source_target_pairs={{1,2},{2,1},{3,4},{4,3},{5,6},{6,5},{7,8},{8,7},{9,10},{10,9},{11,... | collective-permute-start | bytes 983048 | tf_op jit(solution)/shard_map/ppermute | solution.py:460

commit v4 on v3

--- a/solution.py
+++ b/solution.py
@@ -346,69 +346,96 @@
             out[row, k] = mm_nt(ident, full).astype(BF16)
 
 
-def advect_kernel(start, odd, a_ref, own_ref, b_ref, ca_ref, co_ref, cb_ref, dep_ref, surf_ref, *refs):
-    o_ref, fac, flat, ready, sems = refs[-5:]
-    fields = own_ref.shape[2]
-    is_odd = odd[0, 0] == 1
+PART = 80
+
+
+def scale(c, q):
+    return (q.reshape(PART // 8, 8, 128) * c[None]).reshape(PART, 128)
+
+
+def shift_matrix():
+    source, to = iota((256, 256), 0) % 128, iota((256, 256), 1)
+    west = (to < 128) & (source == to - 1)
+    east = (to >= 128) & (source == to - 127)
+    return (west | east).astype(F32).astype(BF16)
+
+
+def columns_step(planes, winds, shift):
+    both = mm(jnp.concatenate([side_by_side(q) for q in planes], axis=0), shift)
+    outs = []
+    for n, (q, (a, b, c)) in enumerate(zip(planes, winds)):
+        near = both[n * PART : n * PART + PART]
+        outs.append(scale(a, near[:, :128]) + scale(b, q) + scale(c, near[:, 128:]))
+    return outs
+
+
+def side_coeffs(is_high, own_wind, side_wind):
     lane = iota((8, 128), 1)
-    wind_low, wind_high = by_parity(is_odd, ca_ref[72:80], cb_ref[72:80])
-    wind_own = co_ref[72:80]
-
-    def coeffs(wind, axis, row):
-        c = wind[axis * 4 : axis * 4 + 4, row * 128 : row * 128 + 128]
+
+    def coeffs(c):
         c = jnp.concatenate([c, c], axis=0)
         half, sq = 0.5 * c, 0.5 * c * c
         return half + sq, 1.0 - c * c, sq - half
 
-    courant = [(wind_low, 1), (wind_own, 0), (wind_own, 1), (wind_high, 0)]
-    cy = [coeffs(w, 1, k) for w, k in courant]
-    cx = []
-    for w, k in courant:
-        a, b, c = coeffs(w, 0, k)
-        cx.append((jnp.where(lane == 0, 0.0, a), b, jnp.where(lane == 127, 0.0, c)))
-
+    result = []
+    for wind, row_high in ((own_wind, 1), (side_wind, 0)):
+        rows = (wind[:, :128], wind[:, 128:])
+        w = jnp.where(is_high, rows[row_high], rows[1 - row_high])
+        south, mid, north = coeffs(w[4:8])
+        along_rows = (jnp.where(is_high, south, north), mid, jnp.where(is_high, north, south))
+        west, mid, east = coeffs(w[:4])
+        along_cols = (jnp.where(lane == 0, 0.0, west), mid, jnp.where(lane == 127, 0.0, east))
+        result.append((along_rows, along_cols))
+    return result
+
+
+def rows_step(inner, mid, outer, c):
+    return scale(c[0], inner) + scale(c[1], mid) + scale(c[2], outer)
+
+
+def side_rows(is_high, side_ref, own_ref, m, f, coeffs):
+    load = lambda ref, k: ref[k, m, f : f + PART]
+    near, far = by_parity(is_high, load(side_ref, 0), load(side_ref, 1))
+    close, other = by_parity(is_high, load(own_ref, 1), load(own_ref, 0))
+    near, far, close, other = [x.astype(F32) for x in (near, far, close, other)]
+    return [
+        rows_step(other, close, near, coeffs[0][0]),
+        rows_step(close, near, far, coeffs[1][0]),
+    ]
+
+
+def all_units(own_ref):
+    return [(m, f) for m in range(own_ref.shape[1]) for f in range(0, own_ref.shape[2], PART)]
+
+
+def first_side_kernel(odd, side_ref, own_ref, side_wind, own_wind, o_ref):
+    is_high = odd[0, 0] == 0
+    coeffs = side_coeffs(is_high, own_wind[72:80], side_wind[72:80])
+    shift = shift_matrix()
+    for m, f in all_units(own_ref):
+        planes = side_rows(is_high, side_ref, own_ref, m, f, coeffs)
+        outs = columns_step(planes, [c[1] for c in coeffs], shift)
+        o_ref[0, m, f : f + PART] = outs[0]
+        o_ref[1, m, f : f + PART] = outs[1]
+
+
+def advect_kernel(odd, b_ref, own_ref, a_mid, ca_ref, co_ref, cb_ref, dep_ref, surf_ref, *refs):
+    o_ref, fac, flat, ready, sems = refs
+    members, fields = own_ref.shape[1], own_ref.shape[2]
+    span = 2 * fields
+    is_odd = odd[0, 0] == 1
+    coeffs_a = side_coeffs(jnp.logical_not(is_odd), co_ref[72:80], ca_ref[72:80])
+    coeffs_b = side_coeffs(is_odd, co_ref[72:80], cb_ref[72:80])
+    shift = shift_matrix()
     own_level = iota((fields, dep_ref.shape[1]), 0) == 4 * iota((fields, dep_ref.shape[1]), 1)
     rate = jnp.sum(jnp.where(own_level, dep_ref[...], 0.0), axis=1, keepdims=True)
     for row in range(2):
         fac[row] = jnp.exp(-rate * surf_ref[row : row + 1, :])
-
-    shift_in, shift_out = iota((256, 256), 0) % 128, iota((256, 256), 1)
-    shift = (
-        ((shift_out < 128) & (shift_in == shift_out - 1))
-        | ((shift_out >= 128) & (shift_in == shift_out - 127))
-    ).astype(F32).astype(BF16)
-    part = 80
-
-    def scale(c, q):
-        return (q.reshape(part // 8, 8, 128) * c[None]).reshape(part, 128)
-
-    def rows(south, mid, north, k):
-        a, b, c = cy[k]
-        return scale(a, south) + scale(b, mid) + scale(c, north)
-
-    def cols(planes, first):
-        both = mm(
-            jnp.concatenate([jnp.concatenate(split2(q), axis=1) for q in planes], axis=0), shift
-        )
-        outs = []
-        for n, q in enumerate(planes):
-            a, b, c = cx[first + n]
-            near = both[n * part : n * part + part]
-            outs.append(scale(a, near[:, :128]) + scale(b, q) + scale(c, near[:, 128:]))
-        return outs
-
-    members, span = own_ref.shape[1], 2 * fields
-    units = [(m, f) for m in range(members) for f in range(0, fields, part)]
+    units = all_units(own_ref)
 
     def first(m, f):
-        near = [
-            by_parity(is_odd, a_ref[k, m, f : f + part], b_ref[k, m, f : f + part])
-            for k in range(2)
-        ]
-        q = [near[0][0], near[1][0], own_ref[0, m, f : f + part]]
-        q += [own_ref[1, m, f : f + part], near[0][1], near[1][1]]
-        q = [x.astype(F32) for x in q]
-        return cols([rows(q[i], q[i + 1], q[i + 2], i) for i in range(4)], 0)
+        planes = side_rows(is_odd, b_ref, own_ref, m, f, coeffs_b)
+        return columns_step(planes, [c[1] for c in coeffs_b], shift)
 
     ahead = 2
     mids = {u: first(*units[u]) for u in range(ahead)}
@@ -416,18 +443,20 @@
     for u, (m, f) in enumerate(units):
         if u + ahead < len(units):
             mids[u + ahead] = first(*units[u + ahead])
-        q1 = mids.pop(u)
-        q2 = cols([rows(q1[i], q1[i + 1], q1[i + 2], i + 1) for i in range(2)], 1)
+        own_b, out_b = mids.pop(u)
+        own_a, out_a = a_mid[0, m, f : f + PART], a_mid[1, m, f : f + PART]
+        planes = [
+            rows_step(own_b, own_a, out_a, coeffs_a[0][0]),
+            rows_step(own_a, own_b, out_b, coeffs_b[0][0]),
+        ]
+        ends = by_parity(is_odd, *columns_step(planes, [coeffs_a[0][1], coeffs_b[0][1]], shift))
         base = m * span + 2 * f
         for r in range(2):
-            flat[pl.ds(base + r, part, stride=2), :] = q2[r] * fac[r, f : f + part]
-        ready[base : base + 2 * part] = flat[base : base + 2 * part, :].astype(BF16)
-        if f + part == fields:
-            copy = pltpu.make_async_copy(
-                ready.at[pl.ds(m * span, span)],
-                o_ref.at[pl.ds((start + m) * span, span)],
-                sems.at[m],
-            )
+            flat[pl.ds(base + r, PART, stride=2), :] = ends[r] * fac[r, f : f + PART]
+        ready[base : base + 2 * PART] = flat[base : base + 2 * PART, :].astype(BF16)
+        if f + PART == fields:
+            rows = pl.ds(m * span, span)
+            copy = pltpu.make_async_copy(ready.at[rows], o_ref.at[rows], sems.at[m])
             copy.start()
             copies.append(copy)
     for copy in copies:
@@ -480,7 +509,6 @@
     maxobs = patch_index.shape[2]
     groups_mem = 8
 
-    sizes = (4, 4)
     flat = ensemble.reshape(local * fields * tile_rows, columns)
     hbm = pl.BlockSpec(memory_space=pltpu.HBM)
     equiv = pl.pallas_call(
@@ -513,7 +541,7 @@
             pltpu.VMEM((2, levels, tile_rows, columns), F32),
             pltpu.SemaphoreType.DMA((local + 5,)),
         ],
-        compiler_params=pltpu.CompilerParams(vmem_limit_bytes=66900000),
+        compiler_params=pltpu.CompilerParams(vmem_limit_bytes=66600000),
         cost_estimate=cost(10**8),
     )(flat, obs_cell, obs_value, obs_error, courant_x, courant_y)
     packed = jnp.concatenate([everywhere.reshape(groups_mem * local, n_obs), info], axis=0)
@@ -542,7 +570,7 @@
             pltpu.VMEM((2 * groups, 16, 128), F32),
             pltpu.VMEM((2 * groups, 8, 128), F32),
         ],
-        flops=10**7,
+        flops=10**10,
         specs=[smem] + [VMEM] * 5,
     )(odd, near_a, packed, near_b, idx, pos)
     back = call(
@@ -552,38 +580,34 @@
         flops=10**9,
     )(hi, lo, state)[0]
     returned = lax.all_to_all(back, "mem", 0, 0, tiled=True)
-    parts = call(
-        relayout_kernel,
-        [jax.ShapeDtypeStruct((tile_rows, n, fields, columns), BF16) for n in sizes],
+    plane_shape = (tile_rows, local, fields, columns)
+    planes = call(
+        relayout_kernel, [jax.ShapeDtypeStruct(plane_shape, BF16)], flops=10**8
+    )(returned)[0]
+    side_a, side_b = swap(planes, 0), swap(planes, 1)
+    a_mid = call(
+        first_side_kernel,
+        jax.ShapeDtypeStruct(plane_shape, F32),
         flops=10**8,
-    )(returned)
-    halos = [(swap(x, 0), swap(x, 1)) for x in parts]
-
-    done, start = None, 0
-    for n, x, (side_a, side_b) in zip(sizes, parts, halos):
-        operands = [odd, side_a, x, side_b, near_a, packed, near_b]
-        operands += [dep_velocity.reshape(1, -1), surface_factor]
-        in_specs = [smem] + [VMEM] * 8
-        if done is not None:
-            operands.append(done)
-            in_specs.append(hbm)
-        span = n * fields * tile_rows
-        done = pl.pallas_call(
-            functools.partial(advect_kernel, start),
-            out_shape=jax.ShapeDtypeStruct(flat.shape, BF16),
-            in_specs=in_specs,
-            out_specs=hbm,
-            scratch_shapes=[
-                pltpu.VMEM((tile_rows, fields, columns), F32),
-                pltpu.VMEM((span, columns), F32),
-                pltpu.VMEM((span, columns), BF16),
-                pltpu.SemaphoreType.DMA((n,)),
-            ],
-            input_output_aliases={} if start == 0 else {9: 0},
-            compiler_params=params(),
-            cost_estimate=cost(10**9),
-        )(*operands)
-        start += n
+        specs=[smem] + [VMEM] * 4,
+    )(odd, side_a, planes, near_a, packed)
+    done = pl.pallas_call(
+        advect_kernel,
+        out_shape=jax.ShapeDtypeStruct(flat.shape, BF16),
+        in_specs=[smem] + [VMEM] * 8,
+        out_specs=hbm,
+        scratch_shapes=[
+            pltpu.VMEM((tile_rows, fields, columns), F32),
+            pltpu.VMEM(flat.shape, F32),
+            pltpu.VMEM(flat.shape, BF16),
+            pltpu.SemaphoreType.DMA((local,)),
+        ],
+        compiler_params=params(),
+        cost_estimate=cost(10**9),
+    )(
+        odd, side_b, planes, a_mid, near_a, packed, near_b,
+        dep_velocity.reshape(1, -1), surface_factor,
+    )
     return done.reshape(local, fields, tile_rows, columns)
 
 

time: 82.3 us -> 82.1 us (level)
  waiting for transfers between devices: 14.8 us -> 24.7 us
  starting transfers between devices: 30.5 us -> 23 us
  blocking collectives: 16.2 us -> 14.2 us
    ppermute x6 -> x4, starting transfers between devices: 22.5 us -> 15 us  [swap(): return lax.ppermute(x, 'space', pairs)]
    ppermute x6 -> x4, waiting for transfers between devices: 12 us -> 18 us  [swap(): return lax.ppermute(x, 'space', pairs)]
    all_to_all x1, waiting for transfers between devices: 0.01 us -> 3.88 us  [shards(): state = lax.all_to_all(payload, 'mem', 0, 0, tiled=True)]
    all_to_all x1, blocking collectives: 16.2 us -> 14.2 us  [shards(): returned = lax.all_to_all(back, 'mem', 0, 0, tiled=True)]
  transfers between devices with their start and end apart: 8 -> 6, of which waited for: 5 -> 5; matrix products, arithmetic and copies ran while one was open for 1% -> 1% of each run, Pallas kernels for 14% -> 13%
where the time goes in v4:
time: 82.1 us; the launch traced here: 81.5 us
  waiting for transfers between devices  24.7 us (30%)
  starting transfers between devices  23 us (28%)
  Pallas kernels  18.3 us (22%)
  blocking collectives  14.2 us (17%)
  other arithmetic  0.86 us (1%)
    ppermute x4, waiting for transfers between devices, swap(): return lax.ppermute(x, 'space', pairs)  18 us
    ppermute x4, starting transfers between devices, swap(): return lax.ppermute(x, 'space', pairs)  15 us
    all_to_all x1, blocking collectives, shards(): returned = lax.all_to_all(back, 'mem', 0, 0, tiled=True)  14.2 us
    pallas_call x1, Pallas kernels, shards(): call(weights_kernel, [jax.ShapeDtypeStruct((groups, 64, 256), BF16)] * 2,...  7.19 us
    all_to_all x1, starting transfers between devices, shards(): everywhere = lax.all_to_all(equiv, 'mem', 0, 0, tiled=True)  4.48 us
    all_to_all x1, waiting for transfers between devices, shards(): state = lax.all_to_all(payload, 'mem', 0, 0, tiled=True)  3.88 us
    all_to_all x1, starting transfers between devices, shards(): state = lax.all_to_all(payload, 'mem', 0, 0, tiled=True)  3.55 us
    all_to_all x1, waiting for transfers between devices, shards(): everywhere = lax.all_to_all(equiv, 'mem', 0, 0, tiled=True)  2.75 us
  transfers between devices with their start and end apart: 6, of which 5 were waited for; matrix products, arithmetic and copies ran while one was open for 1% of the time, Pallas kernels for 13%

profile of v4, /device:TPU:384, one launch (start us, length us, event | category | flops | bytes accessed | tf_op | source)
XLA Modules:
  0.0 81.5 jit_solution(49057785454794028)
XLA Ops:
  0.0 2.6 %shard_map.110 = f32[8,8,256]{2,1,0:T(8,128)} custom-call(bf16[2560,128]{1,0:T(8,128)(2,1)} %bitcast.7, s32[1,256]{1,0:T(1,128)} %cell.3, s32[1,256]{1,0:T(1,128)} %kind.1), custom_call_target="tpu_custom_call" | custom-call | flops 100000000 | bytes 1000000 | tf_op jit(solution)/shard_map/pallas_call | solution.py:514
  2.7 4.5 %all-to-all-start = ((f32[8,8,256]{2,1,0:T(8,128)}), f32[8,8,256]{2,1,0:T(8,128)S(1)}, u32[]{:S(2)}, u32[]{:S(2)}) async-start(f32[8,8,256]{2,1,0:T(8,128)} %shard_map.110), calls=%async_computation | async-start | bytes 131072 | tf_op jit(solution)/shard_map/all_to_all | solution.py:526
  7.1 0.1 broadcast_in_dim.12
  7.2 0.1 reshape.199
  7.4 2.6 %shard_map.109 = (bf16[8,320,128]{2,1,0:T(8,128)(2,1)}, f32[16,256]{1,0:T(8,128)}) custom-call(bf16[2560,128]{1,0:T(8,128)(2,1)} %bitcast.8, s32[1,256]{1,0:T(1,128)} %cell.3, f32[1,256]{1,0:T(1,128)} %value.1, f32[1,256]{1,0:T(1,128)} %error.1, f32[4,2,128]{2,1,0:T(2,128)} %wind_x.1, f32[4,2,128]{2,1,0:T(2,128)} %wind_y.1), custom_call_target="tpu_custom_call" | custom-call | flops 100000000 | bytes 1000000 | tf_op jit(solution)/shard_map/pallas_call | solution.py:527
  10.0 2.8 %all-to-all-done = f32[8,8,256]{2,1,0:T(8,128)S(1)} async-done(((f32[8,8,256]{2,1,0:T(8,128)}), f32[8,8,256]{2,1,0:T(8,128)S(1)}, u32[]{:S(2)}, u32[]{:S(2)}) %all-to-all-start) | async-done | bytes 65568 | tf_op jit(solution)/shard_map/all_to_all | solution.py:526
  12.8 0.7 pad_maximum_fusion.own.own_wind.co_ref
  13.5 6.3 %collective-permute-start.1 = (f32[80,256]{1,0:T(8,128)S(1)}, f32[80,256]{1,0:T(8,128)S(1)}, u32[]{:S(2)}, u32[]{:S(2)}) collective-permute-start(f32[80,256]{1,0:T(8,128)S(1)} %pad_maximum_fusion.own.own_wind.co_ref), channel_id=1, source_target_pairs={{1,2},{2,1},{3,4},{4,3},{5,6},{6,5},{7,8},{8,7},{9,10},{10,9},{11,... | collective-permute-start | bytes 245768 | tf_op jit(solution)/shard_map/ppermute | solution.py:489
  19.8 1.9 %collective-permute-start = (f32[80,256]{1,0:T(8,128)S(1)}, f32[80,256]{1,0:T(8,128)S(1)}, u32[]{:S(2)}, u32[]{:S(2)}) collective-permute-start(f32[80,256]{1,0:T(8,128)S(1)} %pad_maximum_fusion.own.own_wind.co_ref), channel_id=1, source_target_pairs={{0,1},{1,0},{2,3},{3,2},{4,5},{5,4},{6,7},{7,6},{8,9},{9,8},{10,11... | collective-permute-start | bytes 245768 | tf_op jit(solution)/shard_map/ppermute | solution.py:489
  21.7 0.0 copy-done.3
  21.7 0.1 iota_compare_fusion
  21.8 0.1 lt.42
  21.9 0.0 copy-done.2
  21.9 0.1 squeeze.3
  22.0 3.5 %all-to-all-start.1 = ((bf16[8,320,128]{2,1,0:T(8,128)(2,1)}), bf16[8,320,128]{2,1,0:T(8,128)(2,1)S(1)}, u32[]{:S(2)}, u32[]{:S(2)}) async-start(bf16[8,320,128]{2,1,0:T(8,128)(2,1)} %get-tuple-element.20), calls=%async_computation.1 | async-start | bytes 1310720 | tf_op jit(solution)/shard_map/all_to_all | solution.py:552
  25.6 0.0 collective-permute-done.1.near_b.cb_ref
  25.6 0.6 collective-permute-done.near_a.side_wind.ca_ref
  26.1 7.2 %shard_map.111 = (bf16[8,64,256]{2,1,0:T(8,128)(2,1)S(1)}, bf16[8,64,256]{2,1,0:T(8,128)(2,1)S(1)}) custom-call(s32[1,1]{1,0:T(1,128)} %bitcast.odd, f32[80,256]{1,0:T(8,128)S(1)} %collective-permute-done.near_a.side_wind.ca_ref, f32[80,256]{1,0:T(8,128)S(1)} %pad_maximum_fusion.own.own_wind.co_ref, f32[80,256]{1,0:T(8,128)S(1)} %collective-permute-done.1.near_b.cb_ref, ...), custom_call_target="tpu_custom_call" | custom-call | flops 10000000000 | bytes 1000000 | tf_op jit(solution)/shard_map/pallas_call | solution.py:563
  33.3 3.9 %all-to-all-done.1.x_ref = bf16[8,320,128]{2,1,0:T(8,128)(2,1)S(1)} async-done(((bf16[8,320,128]{2,1,0:T(8,128)(2,1)}), bf16[8,320,128]{2,1,0:T(8,128)(2,1)S(1)}, u32[]{:S(2)}, u32[]{:S(2)}) %all-to-all-start.1) | async-done | bytes 655392 | tf_op jit(solution)/shard_map/all_to_all | solution.py:552
  37.2 1.8 %shard_map.112 = bf16[8,8,40,128]{3,2,1,0:T(8,128)(2,1)S(1)} custom-call(bf16[8,64,256]{2,1,0:T(8,128)(2,1)S(1)} %get-tuple-element.18.hi_ref, bf16[8,64,256]{2,1,0:T(8,128)(2,1)S(1)} %get-tuple-element.19.lo_ref, bf16[8,320,128]{2,1,0:T(8,128)(2,1)S(1)} %all-to-all-done.1.x_ref), custom_call_target="tpu_custom_call" | custom-call | flops 1000000000 | bytes 1000000 | tf_op jit(solution)/shard_map/pallas_call | solution.py:576
  39.0 14.2 %all_to_all.15.x_ref = bf16[8,8,40,128]{3,2,1,0:T(8,128)(2,1)S(1)} all-to-all(bf16[8,8,40,128]{3,2,1,0:T(8,128)(2,1)S(1)} %shard_map.112), channel_id=1, replica_groups=mesh['mem'=8,'space'=64] {'mem'}, dimensions={0} | all-to-all | bytes 1310720 | tf_op jit(solution)/shard_map/all_to_all | solution.py:582
  53.2 0.5 shard_map.113.own_ref
  53.7 0.0 copy-start
  53.7 0.0 copy-start.1
  53.7 3.9 %collective-permute-start.3 = (bf16[2,8,160,128]{3,2,1,0:T(8,128)(2,1)S(1)}, bf16[2,8,160,128]{3,2,1,0:T(8,128)(2,1)S(1)}, u32[]{:S(2)}, u32[]{:S(2)}) collective-permute-start(bf16[2,8,160,128]{3,2,1,0:T(8,128)(2,1)S(1)} %shard_map.113.own_ref), channel_id=1, source_target_pairs={{0,1},{1,0},{2,3},{3,2},{4,5},{5,4},{6,7},{7,6},{8,9},{9,8},{10,11... | collective-permute-start | bytes 1966088 | tf_op jit(solution)/shard_map/ppermute | solution.py:489
  57.7 2.8 %collective-permute-start.2 = (bf16[2,8,160,128]{3,2,1,0:T(8,128)(2,1)S(1)}, bf16[2,8,160,128]{3,2,1,0:T(8,128)(2,1)S(1)}, u32[]{:S(2)}, u32[]{:S(2)}) collective-permute-start(bf16[2,8,160,128]{3,2,1,0:T(8,128)(2,1)S(1)} %shard_map.113.own_ref), channel_id=1, source_target_pairs={{1,2},{2,1},{3,4},{4,3},{5,6},{6,5},{7,8},{8,7},{9,10},{10,9},{11,... | collective-permute-start | bytes 1966088 | tf_op jit(solution)/shard_map/ppermute | solution.py:489
  60.5 11.7 %collective-permute-done.3.side_ref = bf16[2,8,160,128]{3,2,1,0:T(8,128)(2,1)S(1)} collective-permute-done((bf16[2,8,160,128]{3,2,1,0:T(8,128)(2,1)S(1)}, bf16[2,8,160,128]{3,2,1,0:T(8,128)(2,1)S(1)}, u32[]{:S(2)}, u32[]{:S(2)}) %collective-permute-start.3) | collective-permute-done | bytes 655392 | tf_op jit(solution)/shard_map/ppermute | solution.py:489
  72.2 0.9 %shard_map.114.a_mid = f32[2,8,160,128]{3,2,1,0:T(8,128)S(1)} custom-call(s32[1,1]{1,0:T(1,128)} %bitcast.odd, bf16[2,8,160,128]{3,2,1,0:T(8,128)(2,1)S(1)} %collective-permute-done.3.side_ref, bf16[2,8,160,128]{3,2,1,0:T(8,128)(2,1)S(1)} %shard_map.113.own_ref, f32[80,256]{1,0:T(8,128)S(1)} %collective-permute-done.near_a.side_wind.ca_ref, ...), custom_call_target="tpu_custom_call" | custom-call | flops 100000000 | bytes 1000000 | tf_op jit(solution)/shard_map/pallas_call | solution.py:588
  73.1 5.8 %collective-permute-done.2.b_ref = bf16[2,8,160,128]{3,2,1,0:T(8,128)(2,1)S(1)} collective-permute-done((bf16[2,8,160,128]{3,2,1,0:T(8,128)(2,1)S(1)}, bf16[2,8,160,128]{3,2,1,0:T(8,128)(2,1)S(1)}, u32[]{:S(2)}, u32[]{:S(2)}) %collective-permute-start.2) | collective-permute-done | bytes 655392 | tf_op jit(solution)/shard_map/ppermute | solution.py:489
  78.9 0.0 copy-done
  78.9 0.0 copy-done.1
  78.9 2.6 %shard_map.115 = bf16[2560,128]{1,0:T(8,128)(2,1)} custom-call(s32[1,1]{1,0:T(1,128)} %bitcast.odd, bf16[2,8,160,128]{3,2,1,0:T(8,128)(2,1)S(1)} %collective-permute-done.2.b_ref, bf16[2,8,160,128]{3,2,1,0:T(8,128)(2,1)S(1)} %shard_map.113.own_ref, f32[2,8,160,128]{3,2,1,0:T(8,128)S(1)} %shard_map.114.a_mid, ...), custom_call_target="tpu_custom_call" | custom-call | flops 1000000000 | bytes 1000000 | tf_op jit(solution)/shard_map/pallas_call | solution.py:594
  (7 shorter events, 0.1 us)
Async XLA Ops:
  0.0 21.7 %copy-start.3 = (s32[1,32]{1,0:T(1,128)S(1)}, s32[1,32]{1,0:T(1,128)}, u32[]{:S(2)}) copy-start(s32[1,32]{1,0:T(1,128)} %param.17) | copy-start | bytes 388
  0.0 21.9 %copy-start.2 = (s32[1,32,32]{2,1,0:T(8,128)S(1)}, s32[1,32,32]{2,1,0:T(8,128)}, u32[]{:S(2)}) copy-start(s32[1,32,32]{2,1,0:T(8,128)} %param.16) | copy-start | bytes 12292
  2.7 10.1 %all-to-all-start = ((f32[8,8,256]{2,1,0:T(8,128)}), f32[8,8,256]{2,1,0:T(8,128)S(1)}, u32[]{:S(2)}, u32[]{:S(2)}) async-start(f32[8,8,256]{2,1,0:T(8,128)} %shard_map.110), calls=%async_computation | async-start | bytes 131072 | tf_op jit(solution)/shard_map/all_to_all | solution.py:526
  13.5 12.1 %collective-permute-start.1 = (f32[80,256]{1,0:T(8,128)S(1)}, f32[80,256]{1,0:T(8,128)S(1)}, u32[]{:S(2)}, u32[]{:S(2)}) collective-permute-start(f32[80,256]{1,0:T(8,128)S(1)} %pad_maximum_fusion.own.own_wind.co_ref), channel_id=1, source_target_pairs={{1,2},{2,1},{3,4},{4,3},{5,6},{6,5},{7,8},{8,7},{9,10},{10,9},{11,... | collective-permute-start | bytes 245768 | tf_op jit(solution)/shard_map/ppermute | solution.py:489
  19.8 6.3 %collective-permute-start = (f32[80,256]{1,0:T(8,128)S(1)}, f32[80,256]{1,0:T(8,128)S(1)}, u32[]{:S(2)}, u32[]{:S(2)}) collective-permute-start(f32[80,256]{1,0:T(8,128)S(1)} %pad_maximum_fusion.own.own_wind.co_ref), channel_id=1, source_target_pairs={{0,1},{1,0},{2,3},{3,2},{4,5},{5,4},{6,7},{7,6},{8,9},{9,8},{10,11... | collective-permute-start | bytes 245768 | tf_op jit(solution)/shard_map/ppermute | solution.py:489
  22.0 15.2 %all-to-all-start.1 = ((bf16[8,320,128]{2,1,0:T(8,128)(2,1)}), bf16[8,320,128]{2,1,0:T(8,128)(2,1)S(1)}, u32[]{:S(2)}, u32[]{:S(2)}) async-start(bf16[8,320,128]{2,1,0:T(8,128)(2,1)} %get-tuple-element.20), calls=%async_computation.1 | async-start | bytes 1310720 | tf_op jit(solution)/shard_map/all_to_all | solution.py:552
  53.7 25.2 %copy-start = (f32[2,128]{1,0:T(2,128)S(1)}, f32[2,128]{1,0:T(2,128)}, u32[]{:S(2)}) copy-start(f32[2,128]{1,0:T(2,128)} %surf_ref.1) | copy-start | bytes 3076
  53.7 25.2 %copy-start.1 = (f32[40]{0:T(128)S(1)}, f32[40]{0:T(128)}, u32[]{:S(2)}) copy-start(f32[40]{0:T(128)} %param.20) | copy-start | bytes 484
  53.7 18.5 %collective-permute-start.3 = (bf16[2,8,160,128]{3,2,1,0:T(8,128)(2,1)S(1)}, bf16[2,8,160,128]{3,2,1,0:T(8,128)(2,1)S(1)}, u32[]{:S(2)}, u32[]{:S(2)}) collective-permute-start(bf16[2,8,160,128]{3,2,1,0:T(8,128)(2,1)S(1)} %shard_map.113.own_ref), channel_id=1, source_target_pairs={{0,1},{1,0},{2,3},{3,2},{4,5},{5,4},{6,7},{7,6},{8,9},{9,8},{10,11... | collective-permute-start | bytes 1966088 | tf_op jit(solution)/shard_map/ppermute | solution.py:489
  57.7 21.2 %collective-permute-start.2 = (bf16[2,8,160,128]{3,2,1,0:T(8,128)(2,1)S(1)}, bf16[2,8,160,128]{3,2,1,0:T(8,128)(2,1)S(1)}, u32[]{:S(2)}, u32[]{:S(2)}) collective-permute-start(bf16[2,8,160,128]{3,2,1,0:T(8,128)(2,1)S(1)} %shard_map.113.own_ref), channel_id=1, source_target_pairs={{1,2},{2,1},{3,4},{4,3},{5,6},{6,5},{7,8},{8,7},{9,10},{10,9},{11,... | collective-permute-start | bytes 1966088 | tf_op jit(solution)/shard_map/ppermute | solution.py:489

commit v5 on v4

--- a/solution.py
+++ b/solution.py
@@ -190,10 +190,9 @@
 
 
 def equivalents_kernel(ens, cell, kind, o_ref, held, picks, sems):
-    span = ens.shape[0] // 8
-    n_obs = cell.shape[1]
+    species, n_obs = ens.shape[1], cell.shape[1]
     jobs = [(cell, picks.at[0]), (kind, picks.at[1])]
-    jobs += [(ens.at[pl.ds(m * span, span)], held.at[m]) for m in range(8)]
+    jobs += [(ens.at[m, :, 0], held.at[m]) for m in range(8)]
     copies = [pltpu.make_async_copy(src, dst, sems.at[n]) for n, (src, dst) in enumerate(jobs)]
     for copy in copies:
         copy.start()
@@ -202,35 +201,24 @@
     cells = picks[0]
     row = (cells >= 128).astype(jnp.int32)
     pick = (iota((128, n_obs), 0) == cells - 128 * row).astype(F32).astype(BF16)
-    wanted = iota((span, n_obs), 0) == picks[1] * 8 + row
+    wanted = iota((2 * species, n_obs), 0) == picks[1] * 2 + row
     rows = []
     for m in range(0, 8, 2):
         copies[2 + m].wait()
         copies[3 + m].wait()
-        found = [mm(held[m + k], pick) for k in range(2)]
+        found = [mm(held[m + k].reshape(2 * species, 128), pick) for k in range(2)]
         rows += [jnp.sum(jnp.where(wanted, x, 0.0), axis=0, keepdims=True) for x in found]
     full = jnp.concatenate(rows, axis=0)
     for d in range(o_ref.shape[0]):
         o_ref[d] = full
 
 
-def payload_kernel(
-    ens, cell, value, error, wind_x, wind_y, o_ref, info, flat, main, rest, held, ints, floats, winds, sems
-):
+def payload_kernel(ens, cell, value, error, wind_x, wind_y, o_ref, info, flat, main, rest):
     local = 8
-    span = ens.shape[0] // local
-    fields = span // 2
-    jobs = [(ens.at[pl.ds(m * span, span)], held.at[pl.ds(m * span, span)]) for m in range(local)]
-    jobs += [(cell, ints), (value, floats.at[0]), (error, floats.at[1])]
-    jobs += [(wind_x, winds.at[0]), (wind_y, winds.at[1])]
-    copies = [pltpu.make_async_copy(src, dst, sems.at[n]) for n, (src, dst) in enumerate(jobs)]
-    for copy in copies:
-        copy.start()
+    fields = ens.shape[0] // (2 * local)
     ident = (iota((128, 128), 0) == iota((128, 128), 1)).astype(F32).astype(BF16)
     lane = iota((8, 128), 1) // 32
-    for m in range(local):
-        copies[m].wait()
-        flat[m * span : m * span + span] = held[m * span : m * span + span].astype(F32)
+    flat[...] = ens[...].astype(F32)
 
     def turned(n):
         row, m = n // local, n % local
@@ -254,22 +242,20 @@
     for dest in range(8):
         o_ref[dest, :256] = main[dest * 256 : dest * 256 + 256, :].astype(BF16)
         o_ref[dest, 256:] = rest[dest * 64 : dest * 64 + 64, :].astype(BF16)
-    for copy in copies[local:]:
-        copy.wait()
-    cells = ints[...]
+    cells = cell[...]
     n_obs = cells.shape[1]
     row = (cells >= 128).astype(jnp.int32)
     sub = iota((8, n_obs), 0)
-    lines = [floats[0], floats[1], row.astype(F32), (cells - 128 * row).astype(F32)]
+    lines = [value[...], error[...], row.astype(F32), (cells - 128 * row).astype(F32)]
     top = jnp.zeros((8, n_obs), F32)
     for r, line in enumerate(lines):
         top = jnp.where(sub == r, line, top)
     info[:8] = top
-    for axis in range(2):
+    for axis, wind in enumerate((wind_x, wind_y)):
         for level in range(4):
             for half in range(2):
                 info[8 + axis * 4 + level : 9 + axis * 4 + level, half * 128 : half * 128 + 128] = (
-                    winds[axis, level, half : half + 1]
+                    wind[level, half : half + 1]
                 )
 
 
@@ -516,33 +502,24 @@
         out_shape=jax.ShapeDtypeStruct((groups_mem, local, n_obs), F32),
         in_specs=[hbm] * 3,
         scratch_shapes=[
-            pltpu.VMEM((local, fields * tile_rows, columns), BF16),
+            pltpu.VMEM((local, fields // levels, tile_rows, columns), BF16),
             pltpu.VMEM((2, 1, n_obs), jnp.int32),
             pltpu.SemaphoreType.DMA((2 + local,)),
         ],
         compiler_params=pltpu.CompilerParams(vmem_limit_bytes=67000000),
         cost_estimate=cost(10**8),
-    )(flat, obs_cell, obs_species)
+    )(
+        ensemble.reshape(local, fields // levels, levels, tile_rows, columns), obs_cell, obs_species
+    )
     everywhere = lax.all_to_all(equiv, "mem", 0, 0, tiled=True)
-    payload, info = pl.pallas_call(
+    payload, info = call(
         payload_kernel,
-        out_shape=[
+        [
             jax.ShapeDtypeStruct((groups_mem, 320, 128), BF16),
             jax.ShapeDtypeStruct((16, n_obs), F32),
         ],
-        in_specs=[hbm] * 6,
-        scratch_shapes=[
-            pltpu.VMEM(flat.shape, F32),
-            pltpu.VMEM((2048, 128), F32),
-            pltpu.VMEM((512, 128), F32),
-            pltpu.VMEM(flat.shape, BF16),
-            pltpu.VMEM((1, n_obs), jnp.int32),
-            pltpu.VMEM((2, 1, n_obs), F32),
-            pltpu.VMEM((2, levels, tile_rows, columns), F32),
-            pltpu.SemaphoreType.DMA((local + 5,)),
-        ],
-        compiler_params=pltpu.CompilerParams(vmem_limit_bytes=66600000),
-        cost_estimate=cost(10**8),
+        [pltpu.VMEM(flat.shape, F32), pltpu.VMEM((2048, 128), F32), pltpu.VMEM((512, 128), F32)],
+        flops=10**8,
     )(flat, obs_cell, obs_value, obs_error, courant_x, courant_y)
     packed = jnp.concatenate([everywhere.reshape(groups_mem * local, n_obs), info], axis=0)
     payload, packed, patch_index, patch_count = lax.optimization_barrier(

time: 82.1 us -> 82.8 us (level)
  local copies, waits for them, and re-layouts: 0.34 us -> 4.83 us
  waiting for transfers between devices: 24.7 us -> 22 us
  Pallas kernels: 18.3 us -> 16.6 us
  starting transfers between devices: 23 us -> 24.3 us
    unnamed x8 -> x20, local copies, waits for them, and re-layouts: 0.02 us -> 4.51 us
    all_to_all x1, waiting for transfers between devices: 2.75 us -> 0.01 us  [shards(): everywhere = lax.all_to_all(equiv, 'mem', 0, 0, tiled=True)]
    all_to_all x1, starting transfers between devices: 3.55 us -> 4.81 us  [shards(): state = lax.all_to_all(payload, 'mem', 0, 0, tiled=True)]
    pallas_call x1, Pallas kernels: 2.62 us -> 1.36 us  [shards(): call(payload_kernel, [jax.ShapeDtypeStruct((groups_mem, 320, 128), BF16),...]
  transfers between devices with their start and end apart: 6 -> 6, of which waited for: 5 -> 3; matrix products, arithmetic and copies ran while one was open for 1% -> 1% of each run, Pallas kernels for 13% -> 11%
where the time goes in v5:
time: 82.8 us; the launch traced here: 82.2 us
  starting transfers between devices  24.3 us (29%)
  waiting for transfers between devices  22 us (27%)
  Pallas kernels  16.6 us (20%)
  blocking collectives  14.2 us (17%)
  local copies, waits for them, and re-layouts  4.83 us (6%)
    ppermute x4, waiting for transfers between devices, swap(): return lax.ppermute(x, 'space', pairs)  17.5 us
    ppermute x4, starting transfers between devices, swap(): return lax.ppermute(x, 'space', pairs)  15 us
    all_to_all x1, blocking collectives, shards(): returned = lax.all_to_all(back, 'mem', 0, 0, tiled=True)  14.2 us
    pallas_call x1, Pallas kernels, shards(): call(weights_kernel, [jax.ShapeDtypeStruct((groups, 64, 256), BF16)] * 2,...  7.19 us
    all_to_all x1, starting transfers between devices, shards(): state = lax.all_to_all(payload, 'mem', 0, 0, tiled=True)  4.81 us
    all_to_all x1, waiting for transfers between devices, shards(): state = lax.all_to_all(payload, 'mem', 0, 0, tiled=True)  4.52 us
    unnamed x20, local copies, waits for them, and re-layouts  4.51 us
    all_to_all x1, starting transfers between devices, shards(): everywhere = lax.all_to_all(equiv, 'mem', 0, 0, tiled=True)  4.47 us
  transfers between devices with their start and end apart: 6, of which 3 were waited for; matrix products, arithmetic and copies ran while one was open for 1% of the time, Pallas kernels for 11%

profile of v5, /device:TPU:384, one launch (start us, length us, event | category | flops | bytes accessed | tf_op | source)
XLA Modules:
  0.0 82.2 jit_solution(10588879222176968974)
XLA Ops:
  0.0 2.2 %shard_map.110 = f32[8,8,256]{2,1,0:T(8,128)} custom-call(bf16[8,40,4,2,128]{4,3,2,1,0:T(2,128)(2,1)} %bitcast.7, s32[1,256]{1,0:T(1,128)} %cell.3, s32[1,256]{1,0:T(1,128)} %kind.1), custom_call_target="tpu_custom_call" | custom-call | flops 100000000 | bytes 1000000 | tf_op jit(solution)/shard_map/pallas_call | solution.py:500
  2.2 4.5 %all-to-all-start = ((f32[8,8,256]{2,1,0:T(8,128)}), f32[8,8,256]{2,1,0:T(8,128)S(1)}, u32[]{:S(2)}, u32[]{:S(2)}) async-start(f32[8,8,256]{2,1,0:T(8,128)} %shard_map.110), calls=%async_computation | async-start | bytes 131072 | tf_op jit(solution)/shard_map/all_to_all | solution.py:514
  6.7 0.1 broadcast_in_dim.12
  6.7 0.1 reshape.203
  6.9 0.0 copy-start
  6.9 1.1 %copy-done = bf16[8,160,2,128]{3,2,1,0:T(2,128)(2,1)S(1)} copy-done((bf16[8,160,2,128]{3,2,1,0:T(2,128)(2,1)S(1)}, bf16[8,160,2,128]{3,2,1,0:T(2,128)(2,1)}, u32[]{:S(2)}) %copy-start) | copy-done | bytes 655384
  8.0 0.7 copy-done.1
  8.7 0.7 copy-done.2
  9.4 0.7 copy-done.3
  10.1 0.7 copy-done.4
  10.7 0.7 copy-done.5
  11.4 1.4 %shard_map.109 = (bf16[8,320,128]{2,1,0:T(8,128)(2,1)}, f32[16,256]{1,0:T(8,128)S(1)}) custom-call(bf16[2560,128]{1,0:T(8,128)(2,1)S(1)} %bitcast.8, s32[1,256]{1,0:T(1,128)S(1)} %copy-done.3, f32[1,256]{1,0:T(1,128)S(1)} %copy-done.4, f32[1,256]{1,0:T(1,128)S(1)} %copy-done.5, f32[4,2,128]{2,1,0:T(2,128)S(1)} %copy-done.1, f32[4,2,128]{2,1,0:T(2,128)S(1)} %copy-done.2), custom_call_target="tpu_custom_call" | custom-call | flops 100000000 | bytes 1000000 | tf_op jit(solution)/shard_map/pallas_call | solution.py:515
  12.8 6.3 %collective-permute-start.1 = (f32[80,256]{1,0:T(8,128)S(1)}, f32[80,256]{1,0:T(8,128)S(1)}, u32[]{:S(2)}, u32[]{:S(2)}) collective-permute-start(f32[80,256]{1,0:T(8,128)S(1)} %pad_maximum_fusion.own.own_wind.co_ref), channel_id=1, source_target_pairs={{1,2},{2,1},{3,4},{4,3},{5,6},{6,5},{7,8},{8,7},{9,10},{10,9},{11,... | collective-permute-start | bytes 245768 | tf_op jit(solution)/shard_map/ppermute | solution.py:475
  19.1 1.9 %collective-permute-start = (f32[80,256]{1,0:T(8,128)S(1)}, f32[80,256]{1,0:T(8,128)S(1)}, u32[]{:S(2)}, u32[]{:S(2)}) collective-permute-start(f32[80,256]{1,0:T(8,128)S(1)} %pad_maximum_fusion.own.own_wind.co_ref), channel_id=1, source_target_pairs={{0,1},{1,0},{2,3},{3,2},{4,5},{5,4},{6,7},{7,6},{8,9},{9,8},{10,11... | collective-permute-start | bytes 245768 | tf_op jit(solution)/shard_map/ppermute | solution.py:475
  21.0 0.1 iota_compare_fusion
  21.1 0.1 lt.42
  21.2 0.1 squeeze.3
  21.3 4.8 %all-to-all-start.1 = ((bf16[8,320,128]{2,1,0:T(8,128)(2,1)}), bf16[8,320,128]{2,1,0:T(8,128)(2,1)S(1)}, u32[]{:S(2)}, u32[]{:S(2)}) async-start(bf16[8,320,128]{2,1,0:T(8,128)(2,1)} %get-tuple-element.20), calls=%async_computation.1 | async-start | bytes 1310720 | tf_op jit(solution)/shard_map/all_to_all | solution.py:529
  26.1 0.0 collective-permute-done.1.near_b.cb_ref
  26.1 7.2 %shard_map.111 = (bf16[8,64,256]{2,1,0:T(8,128)(2,1)S(1)}, bf16[8,64,256]{2,1,0:T(8,128)(2,1)S(1)}) custom-call(s32[1,1]{1,0:T(1,128)} %bitcast.odd, f32[80,256]{1,0:T(8,128)S(1)} %collective-permute-done.near_a.side_wind.ca_ref, f32[80,256]{1,0:T(8,128)S(1)} %pad_maximum_fusion.own.own_wind.co_ref, f32[80,256]{1,0:T(8,128)S(1)} %collective-permute-done.1.near_b.cb_ref, ...), custom_call_target="tpu_custom_call" | custom-call | flops 10000000000 | bytes 1000000 | tf_op jit(solution)/shard_map/pallas_call | solution.py:540
  33.3 4.5 %all-to-all-done.1.x_ref = bf16[8,320,128]{2,1,0:T(8,128)(2,1)S(1)} async-done(((bf16[8,320,128]{2,1,0:T(8,128)(2,1)}), bf16[8,320,128]{2,1,0:T(8,128)(2,1)S(1)}, u32[]{:S(2)}, u32[]{:S(2)}) %all-to-all-start.1) | async-done | bytes 655392 | tf_op jit(solution)/shard_map/all_to_all | solution.py:529
  37.9 1.8 %shard_map.112 = bf16[8,8,40,128]{3,2,1,0:T(8,128)(2,1)S(1)} custom-call(bf16[8,64,256]{2,1,0:T(8,128)(2,1)S(1)} %get-tuple-element.18.hi_ref, bf16[8,64,256]{2,1,0:T(8,128)(2,1)S(1)} %get-tuple-element.19.lo_ref, bf16[8,320,128]{2,1,0:T(8,128)(2,1)S(1)} %all-to-all-done.1.x_ref), custom_call_target="tpu_custom_call" | custom-call | flops 1000000000 | bytes 1000000 | tf_op jit(solution)/shard_map/pallas_call | solution.py:553
  39.7 14.2 %all_to_all.15.x_ref = bf16[8,8,40,128]{3,2,1,0:T(8,128)(2,1)S(1)} all-to-all(bf16[8,8,40,128]{3,2,1,0:T(8,128)(2,1)S(1)} %shard_map.112), channel_id=1, replica_groups=mesh['mem'=8,'space'=64] {'mem'}, dimensions={0} | all-to-all | bytes 1310720 | tf_op jit(solution)/shard_map/all_to_all | solution.py:559
  53.9 0.5 shard_map.113.own_ref
  54.4 0.0 copy-start.6
  54.4 0.0 copy-start.7
  54.4 3.9 %collective-permute-start.3 = (bf16[2,8,160,128]{3,2,1,0:T(8,128)(2,1)S(1)}, bf16[2,8,160,128]{3,2,1,0:T(8,128)(2,1)S(1)}, u32[]{:S(2)}, u32[]{:S(2)}) collective-permute-start(bf16[2,8,160,128]{3,2,1,0:T(8,128)(2,1)S(1)} %shard_map.113.own_ref), channel_id=1, source_target_pairs={{0,1},{1,0},{2,3},{3,2},{4,5},{5,4},{6,7},{7,6},{8,9},{9,8},{10,11... | collective-permute-start | bytes 1966088 | tf_op jit(solution)/shard_map/ppermute | solution.py:475
  58.3 2.8 %collective-permute-start.2 = (bf16[2,8,160,128]{3,2,1,0:T(8,128)(2,1)S(1)}, bf16[2,8,160,128]{3,2,1,0:T(8,128)(2,1)S(1)}, u32[]{:S(2)}, u32[]{:S(2)}) collective-permute-start(bf16[2,8,160,128]{3,2,1,0:T(8,128)(2,1)S(1)} %shard_map.113.own_ref), channel_id=1, source_target_pairs={{1,2},{2,1},{3,4},{4,3},{5,6},{6,5},{7,8},{8,7},{9,10},{10,9},{11,... | collective-permute-start | bytes 1966088 | tf_op jit(solution)/shard_map/ppermute | solution.py:475
  61.2 11.7 %collective-permute-done.3.side_ref = bf16[2,8,160,128]{3,2,1,0:T(8,128)(2,1)S(1)} collective-permute-done((bf16[2,8,160,128]{3,2,1,0:T(8,128)(2,1)S(1)}, bf16[2,8,160,128]{3,2,1,0:T(8,128)(2,1)S(1)}, u32[]{:S(2)}, u32[]{:S(2)}) %collective-permute-start.3) | collective-permute-done | bytes 655392 | tf_op jit(solution)/shard_map/ppermute | solution.py:475
  72.9 0.9 %shard_map.114.a_mid = f32[2,8,160,128]{3,2,1,0:T(8,128)S(1)} custom-call(s32[1,1]{1,0:T(1,128)} %bitcast.odd, bf16[2,8,160,128]{3,2,1,0:T(8,128)(2,1)S(1)} %collective-permute-done.3.side_ref, bf16[2,8,160,128]{3,2,1,0:T(8,128)(2,1)S(1)} %shard_map.113.own_ref, f32[80,256]{1,0:T(8,128)S(1)} %collective-permute-done.near_a.side_wind.ca_ref, ...), custom_call_target="tpu_custom_call" | custom-call | flops 100000000 | bytes 1000000 | tf_op jit(solution)/shard_map/pallas_call | solution.py:565
  73.8 5.8 %collective-permute-done.2.b_ref = bf16[2,8,160,128]{3,2,1,0:T(8,128)(2,1)S(1)} collective-permute-done((bf16[2,8,160,128]{3,2,1,0:T(8,128)(2,1)S(1)}, bf16[2,8,160,128]{3,2,1,0:T(8,128)(2,1)S(1)}, u32[]{:S(2)}, u32[]{:S(2)}) %collective-permute-start.2) | collective-permute-done | bytes 655392 | tf_op jit(solution)/shard_map/ppermute | solution.py:475
  79.6 2.6 %shard_map.115 = bf16[2560,128]{1,0:T(8,128)(2,1)} custom-call(s32[1,1]{1,0:T(1,128)} %bitcast.odd, bf16[2,8,160,128]{3,2,1,0:T(8,128)(2,1)S(1)} %collective-permute-done.2.b_ref, bf16[2,8,160,128]{3,2,1,0:T(8,128)(2,1)S(1)} %shard_map.113.own_ref, f32[2,8,160,128]{3,2,1,0:T(8,128)S(1)} %shard_map.114.a_mid, ...), custom_call_target="tpu_custom_call" | custom-call | flops 1000000000 | bytes 1000000 | tf_op jit(solution)/shard_map/pallas_call | solution.py:571
  (19 shorter events, 0.1 us)
Async XLA Ops:
  0.0 21.0 %copy-start.9 = (s32[1,32]{1,0:T(1,128)S(1)}, s32[1,32]{1,0:T(1,128)}, u32[]{:S(2)}) copy-start(s32[1,32]{1,0:T(1,128)} %param.17) | copy-start | bytes 388
  0.0 21.2 %copy-start.8 = (s32[1,32,32]{2,1,0:T(8,128)S(1)}, s32[1,32,32]{2,1,0:T(8,128)}, u32[]{:S(2)}) copy-start(s32[1,32,32]{2,1,0:T(8,128)} %param.16) | copy-start | bytes 12292
  2.2 10.6 %all-to-all-start = ((f32[8,8,256]{2,1,0:T(8,128)}), f32[8,8,256]{2,1,0:T(8,128)S(1)}, u32[]{:S(2)}, u32[]{:S(2)}) async-start(f32[8,8,256]{2,1,0:T(8,128)} %shard_map.110), calls=%async_computation | async-start | bytes 131072 | tf_op jit(solution)/shard_map/all_to_all | solution.py:514
  6.9 1.1 %copy-start = (bf16[8,160,2,128]{3,2,1,0:T(2,128)(2,1)S(1)}, bf16[8,160,2,128]{3,2,1,0:T(2,128)(2,1)}, u32[]{:S(2)}) copy-start(bf16[8,160,2,128]{3,2,1,0:T(2,128)(2,1)} %param.11) | copy-start | bytes 1966084
  8.0 0.7 copy-start.1
  8.7 0.7 copy-start.2
  9.4 0.7 copy-start.3
  10.0 0.7 copy-start.4
  10.7 0.7 copy-start.5
  12.8 13.3 %collective-permute-start.1 = (f32[80,256]{1,0:T(8,128)S(1)}, f32[80,256]{1,0:T(8,128)S(1)}, u32[]{:S(2)}, u32[]{:S(2)}) collective-permute-start(f32[80,256]{1,0:T(8,128)S(1)} %pad_maximum_fusion.own.own_wind.co_ref), channel_id=1, source_target_pairs={{1,2},{2,1},{3,4},{4,3},{5,6},{6,5},{7,8},{8,7},{9,10},{10,9},{11,... | collective-permute-start | bytes 245768 | tf_op jit(solution)/shard_map/ppermute | solution.py:475
  19.1 7.0 %collective-permute-start = (f32[80,256]{1,0:T(8,128)S(1)}, f32[80,256]{1,0:T(8,128)S(1)}, u32[]{:S(2)}, u32[]{:S(2)}) collective-permute-start(f32[80,256]{1,0:T(8,128)S(1)} %pad_maximum_fusion.own.own_wind.co_ref), channel_id=1, source_target_pairs={{0,1},{1,0},{2,3},{3,2},{4,5},{5,4},{6,7},{7,6},{8,9},{9,8},{10,11... | collective-permute-start | bytes 245768 | tf_op jit(solution)/shard_map/ppermute | solution.py:475
  21.3 16.6 %all-to-all-start.1 = ((bf16[8,320,128]{2,1,0:T(8,128)(2,1)}), bf16[8,320,128]{2,1,0:T(8,128)(2,1)S(1)}, u32[]{:S(2)}, u32[]{:S(2)}) async-start(bf16[8,320,128]{2,1,0:T(8,128)(2,1)} %get-tuple-element.20), calls=%async_computation.1 | async-start | bytes 1310720 | tf_op jit(solution)/shard_map/all_to_all | solution.py:529
  54.4 25.2 %copy-start.6 = (f32[2,128]{1,0:T(2,128)S(1)}, f32[2,128]{1,0:T(2,128)}, u32[]{:S(2)}) copy-start(f32[2,128]{1,0:T(2,128)} %surf_ref.1) | copy-start | bytes 3076
  54.4 25.2 %copy-start.7 = (f32[40]{0:T(128)S(1)}, f32[40]{0:T(128)}, u32[]{:S(2)}) copy-start(f32[40]{0:T(128)} %param.20) | copy-start | bytes 484
  54.4 18.5 %collective-permute-start.3 = (bf16[2,8,160,128]{3,2,1,0:T(8,128)(2,1)S(1)}, bf16[2,8,160,128]{3,2,1,0:T(8,128)(2,1)S(1)}, u32[]{:S(2)}, u32[]{:S(2)}) collective-permute-start(bf16[2,8,160,128]{3,2,1,0:T(8,128)(2,1)S(1)} %shard_map.113.own_ref), channel_id=1, source_target_pairs={{0,1},{1,0},{2,3},{3,2},{4,5},{5,4},{6,7},{7,6},{8,9},{9,8},{10,11... | collective-permute-start | bytes 1966088 | tf_op jit(solution)/shard_map/ppermute | solution.py:475
  58.3 21.2 %collective-permute-start.2 = (bf16[2,8,160,128]{3,2,1,0:T(8,128)(2,1)S(1)}, bf16[2,8,160,128]{3,2,1,0:T(8,128)(2,1)S(1)}, u32[]{:S(2)}, u32[]{:S(2)}) collective-permute-start(bf16[2,8,160,128]{3,2,1,0:T(8,128)(2,1)S(1)} %shard_map.113.own_ref), channel_id=1, source_target_pairs={{1,2},{2,1},{3,4},{4,3},{5,6},{6,5},{7,8},{8,7},{9,10},{10,9},{11,... | collective-permute-start | bytes 1966088 | tf_op jit(solution)/shard_map/ppermute | solution.py:475

commit v6 on v3

--- a/solution.py
+++ b/solution.py
@@ -190,10 +190,9 @@
 
 
 def equivalents_kernel(ens, cell, kind, o_ref, held, picks, sems):
-    span = ens.shape[0] // 8
-    n_obs = cell.shape[1]
+    species, n_obs = ens.shape[1], cell.shape[1]
     jobs = [(cell, picks.at[0]), (kind, picks.at[1])]
-    jobs += [(ens.at[pl.ds(m * span, span)], held.at[m]) for m in range(8)]
+    jobs += [(ens.at[m, :, 0], held.at[m]) for m in range(8)]
     copies = [pltpu.make_async_copy(src, dst, sems.at[n]) for n, (src, dst) in enumerate(jobs)]
     for copy in copies:
         copy.start()
@@ -202,35 +201,24 @@
     cells = picks[0]
     row = (cells >= 128).astype(jnp.int32)
     pick = (iota((128, n_obs), 0) == cells - 128 * row).astype(F32).astype(BF16)
-    wanted = iota((span, n_obs), 0) == picks[1] * 8 + row
+    wanted = iota((2 * species, n_obs), 0) == picks[1] * 2 + row
     rows = []
     for m in range(0, 8, 2):
         copies[2 + m].wait()
         copies[3 + m].wait()
-        found = [mm(held[m + k], pick) for k in range(2)]
+        found = [mm(held[m + k].reshape(2 * species, 128), pick) for k in range(2)]
         rows += [jnp.sum(jnp.where(wanted, x, 0.0), axis=0, keepdims=True) for x in found]
     full = jnp.concatenate(rows, axis=0)
     for d in range(o_ref.shape[0]):
         o_ref[d] = full
 
 
-def payload_kernel(
-    ens, cell, value, error, wind_x, wind_y, o_ref, info, flat, main, rest, held, ints, floats, winds, sems
-):
+def payload_kernel(ens, cell, value, error, wind_x, wind_y, o_ref, info, flat, main, rest):
     local = 8
-    span = ens.shape[0] // local
-    fields = span // 2
-    jobs = [(ens.at[pl.ds(m * span, span)], held.at[pl.ds(m * span, span)]) for m in range(local)]
-    jobs += [(cell, ints), (value, floats.at[0]), (error, floats.at[1])]
-    jobs += [(wind_x, winds.at[0]), (wind_y, winds.at[1])]
-    copies = [pltpu.make_async_copy(src, dst, sems.at[n]) for n, (src, dst) in enumerate(jobs)]
-    for copy in copies:
-        copy.start()
+    fields = ens.shape[0] // (2 * local)
     ident = (iota((128, 128), 0) == iota((128, 128), 1)).astype(F32).astype(BF16)
     lane = iota((8, 128), 1) // 32
-    for m in range(local):
-        copies[m].wait()
-        flat[m * span : m * span + span] = held[m * span : m * span + span].astype(F32)
+    flat[...] = ens[...].astype(F32)
 
     def turned(n):
         row, m = n // local, n % local
@@ -254,22 +242,20 @@
     for dest in range(8):
         o_ref[dest, :256] = main[dest * 256 : dest * 256 + 256, :].astype(BF16)
         o_ref[dest, 256:] = rest[dest * 64 : dest * 64 + 64, :].astype(BF16)
-    for copy in copies[local:]:
-        copy.wait()
-    cells = ints[...]
+    cells = cell[...]
     n_obs = cells.shape[1]
     row = (cells >= 128).astype(jnp.int32)
     sub = iota((8, n_obs), 0)
-    lines = [floats[0], floats[1], row.astype(F32), (cells - 128 * row).astype(F32)]
+    lines = [value[...], error[...], row.astype(F32), (cells - 128 * row).astype(F32)]
     top = jnp.zeros((8, n_obs), F32)
     for r, line in enumerate(lines):
         top = jnp.where(sub == r, line, top)
     info[:8] = top
-    for axis in range(2):
+    for axis, wind in enumerate((wind_x, wind_y)):
         for level in range(4):
             for half in range(2):
                 info[8 + axis * 4 + level : 9 + axis * 4 + level, half * 128 : half * 128 + 128] = (
-                    winds[axis, level, half : half + 1]
+                    wind[level, half : half + 1]
                 )
 
 
@@ -480,7 +466,7 @@
     maxobs = patch_index.shape[2]
     groups_mem = 8
 
-    sizes = (4, 4)
+    sizes = (8,)
     flat = ensemble.reshape(local * fields * tile_rows, columns)
     hbm = pl.BlockSpec(memory_space=pltpu.HBM)
     equiv = pl.pallas_call(
@@ -488,33 +474,24 @@
         out_shape=jax.ShapeDtypeStruct((groups_mem, local, n_obs), F32),
         in_specs=[hbm] * 3,
         scratch_shapes=[
-            pltpu.VMEM((local, fields * tile_rows, columns), BF16),
+            pltpu.VMEM((local, fields // levels, tile_rows, columns), BF16),
             pltpu.VMEM((2, 1, n_obs), jnp.int32),
             pltpu.SemaphoreType.DMA((2 + local,)),
         ],
         compiler_params=pltpu.CompilerParams(vmem_limit_bytes=67000000),
         cost_estimate=cost(10**8),
-    )(flat, obs_cell, obs_species)
+    )(
+        ensemble.reshape(local, fields // levels, levels, tile_rows, columns), obs_cell, obs_species
+    )
     everywhere = lax.all_to_all(equiv, "mem", 0, 0, tiled=True)
-    payload, info = pl.pallas_call(
+    payload, info = call(
         payload_kernel,
-        out_shape=[
+        [
             jax.ShapeDtypeStruct((groups_mem, 320, 128), BF16),
             jax.ShapeDtypeStruct((16, n_obs), F32),
         ],
-        in_specs=[hbm] * 6,
-        scratch_shapes=[
-            pltpu.VMEM(flat.shape, F32),
-            pltpu.VMEM((2048, 128), F32),
-            pltpu.VMEM((512, 128), F32),
-            pltpu.VMEM(flat.shape, BF16),
-            pltpu.VMEM((1, n_obs), jnp.int32),
-            pltpu.VMEM((2, 1, n_obs), F32),
-            pltpu.VMEM((2, levels, tile_rows, columns), F32),
-            pltpu.SemaphoreType.DMA((local + 5,)),
-        ],
-        compiler_params=pltpu.CompilerParams(vmem_limit_bytes=66900000),
-        cost_estimate=cost(10**8),
+        [pltpu.VMEM(flat.shape, F32), pltpu.VMEM((2048, 128), F32), pltpu.VMEM((512, 128), F32)],
+        flops=10**8,
     )(flat, obs_cell, obs_value, obs_error, courant_x, courant_y)
     packed = jnp.concatenate([everywhere.reshape(groups_mem * local, n_obs), info], axis=0)
     payload, packed, patch_index, patch_count = lax.optimization_barrier(
@@ -542,7 +519,7 @@
             pltpu.VMEM((2 * groups, 16, 128), F32),
             pltpu.VMEM((2 * groups, 8, 128), F32),
         ],
-        flops=10**7,
+        flops=10**10,
         specs=[smem] + [VMEM] * 5,
     )(odd, near_a, packed, near_b, idx, pos)
     back = call(

time: 82.3 us -> 77.9 us (0.947)
  starting transfers between devices: 30.5 us -> 22.1 us
  waiting for transfers between devices: 14.8 us -> 22.3 us
  Pallas kernels: 18.7 us -> 16.2 us
  blocking collectives: 16.2 us -> 14.2 us
  local copies, waits for them, and re-layouts: 0.35 us -> 2.13 us
    ppermute x6 -> x4, starting transfers between devices: 22.5 us -> 14.1 us  [swap(): return lax.ppermute(x, 'space', pairs)]
    ppermute x6 -> x4, waiting for transfers between devices: 12 us -> 16.2 us  [swap(): return lax.ppermute(x, 'space', pairs)]
    all_to_all x1, waiting for transfers between devices: 0.01 us -> 3.88 us  [shards(): state = lax.all_to_all(payload, 'mem', 0, 0, tiled=True)]
    all_to_all x1, blocking collectives: 16.2 us -> 14.2 us  [shards(): returned = lax.all_to_all(back, 'mem', 0, 0, tiled=True)]
    unnamed x8 -> x20, local copies, waits for them, and re-layouts: 0.03 us -> 1.81 us
    pallas_call x1, Pallas kernels: 2.62 us -> 1.36 us  [shards(): call(payload_kernel, [jax.ShapeDtypeStruct((groups_mem, 320, 128), BF16),...]
    pallas_call x2 -> x1, Pallas kernels: 3.99 us -> 3.22 us  [shards(): pl.pallas_call(functools.partial(advect_kernel, start), out_shape=jax.Sha...]
  transfers between devices with their start and end apart: 8 -> 6, of which waited for: 5 -> 4; matrix products, arithmetic and copies ran while one was open for 1% -> 1% of each run, Pallas kernels for 14% -> 11%
where the time goes in v6:
time: 77.9 us; the launch traced here: 77.3 us
  waiting for transfers between devices  22.3 us (29%)
  starting transfers between devices  22.1 us (28%)
  Pallas kernels  16.2 us (21%)
  blocking collectives  14.2 us (18%)
  local copies, waits for them, and re-layouts  2.13 us (3%)
    ppermute x4, waiting for transfers between devices, swap(): return lax.ppermute(x, 'space', pairs)  16.2 us
    all_to_all x1, blocking collectives, shards(): returned = lax.all_to_all(back, 'mem', 0, 0, tiled=True)  14.2 us
    ppermute x4, starting transfers between devices, swap(): return lax.ppermute(x, 'space', pairs)  14.1 us
    pallas_call x1, Pallas kernels, shards(): call(weights_kernel, [jax.ShapeDtypeStruct((groups, 64, 256), BF16)] * 2,...  7.18 us
    all_to_all x1, starting transfers between devices, shards(): everywhere = lax.all_to_all(equiv, 'mem', 0, 0, tiled=True)  4.49 us
    all_to_all x1, waiting for transfers between devices, shards(): state = lax.all_to_all(payload, 'mem', 0, 0, tiled=True)  3.88 us
    all_to_all x1, starting transfers between devices, shards(): state = lax.all_to_all(payload, 'mem', 0, 0, tiled=True)  3.55 us
    pallas_call x1, Pallas kernels, shards(): pl.pallas_call(functools.partial(advect_kernel, start), out_shape=jax.Sha...  3.22 us
  transfers between devices with their start and end apart: 6, of which 4 were waited for; matrix products, arithmetic and copies ran while one was open for 1% of the time, Pallas kernels for 11%

profile of v6, /device:TPU:384, one launch (start us, length us, event | category | flops | bytes accessed | tf_op | source)
XLA Modules:
  0.0 77.3 jit_solution(17181168442179846856)
XLA Ops:
  0.0 2.1 %shard_map.110 = f32[8,8,256]{2,1,0:T(8,128)} custom-call(bf16[8,40,4,2,128]{4,3,2,1,0:T(2,128)(2,1)} %bitcast.7, s32[1,256]{1,0:T(1,128)} %cell.3, s32[1,256]{1,0:T(1,128)} %kind.1), custom_call_target="tpu_custom_call" | custom-call | flops 100000000 | bytes 1000000 | tf_op jit(solution)/shard_map/pallas_call | solution.py:472
  2.2 4.5 %all-to-all-start = ((f32[8,8,256]{2,1,0:T(8,128)}), f32[8,8,256]{2,1,0:T(8,128)S(1)}, u32[]{:S(2)}, u32[]{:S(2)}) async-start(f32[8,8,256]{2,1,0:T(8,128)} %shard_map.110), calls=%async_computation | async-start | bytes 131072 | tf_op jit(solution)/shard_map/all_to_all | solution.py:486
  6.7 0.1 broadcast_in_dim.12
  6.7 0.1 reshape.203
  6.9 0.0 copy-start.4
  6.9 0.0 copy-start.5
  6.9 0.0 copy-start.2
  6.9 0.6 copy-done.4
  7.6 0.0 copy-done.5
  7.6 0.0 copy-done.2
  7.6 0.0 copy-done.1
  7.6 0.0 copy-done.3
  7.6 1.1 %copy-done = bf16[8,160,2,128]{3,2,1,0:T(2,128)(2,1)S(1)} copy-done((bf16[8,160,2,128]{3,2,1,0:T(2,128)(2,1)S(1)}, bf16[8,160,2,128]{3,2,1,0:T(2,128)(2,1)}, u32[]{:S(2)}) %copy-start) | copy-done | bytes 655384
  8.7 1.4 %shard_map.109 = (bf16[8,320,128]{2,1,0:T(8,128)(2,1)}, f32[16,256]{1,0:T(8,128)S(1)}) custom-call(bf16[2560,128]{1,0:T(8,128)(2,1)S(1)} %bitcast.8, s32[1,256]{1,0:T(1,128)S(1)} %copy-done.3, f32[1,256]{1,0:T(1,128)S(1)} %copy-done.4, f32[1,256]{1,0:T(1,128)S(1)} %copy-done.5, f32[4,2,128]{2,1,0:T(2,128)S(1)} %copy-done.1, f32[4,2,128]{2,1,0:T(2,128)S(1)} %copy-done.2), custom_call_target="tpu_custom_call" | custom-call | flops 100000000 | bytes 1000000 | tf_op jit(solution)/shard_map/pallas_call | solution.py:487
  10.1 2.2 %all-to-all-done = f32[8,8,256]{2,1,0:T(8,128)S(1)} async-done(((f32[8,8,256]{2,1,0:T(8,128)}), f32[8,8,256]{2,1,0:T(8,128)S(1)}, u32[]{:S(2)}, u32[]{:S(2)}) %all-to-all-start) | async-done | bytes 65568 | tf_op jit(solution)/shard_map/all_to_all | solution.py:486
  12.3 0.0 copy-start.8
  12.3 6.3 %collective-permute-start.1 = (f32[80,256]{1,0:T(8,128)S(1)}, f32[80,256]{1,0:T(8,128)S(1)}, u32[]{:S(2)}, u32[]{:S(2)}) collective-permute-start(f32[80,256]{1,0:T(8,128)S(1)} %pad_maximum_fusion.own.co_ref), channel_id=1, source_target_pairs={{1,2},{2,1},{3,4},{4,3},{5,6},{6,5},{7,8},{8,7},{9,10},{10,9},{11,... | collective-permute-start | bytes 245768 | tf_op jit(solution)/shard_map/ppermute | solution.py:446
  18.6 1.9 %collective-permute-start = (f32[80,256]{1,0:T(8,128)S(1)}, f32[80,256]{1,0:T(8,128)S(1)}, u32[]{:S(2)}, u32[]{:S(2)}) collective-permute-start(f32[80,256]{1,0:T(8,128)S(1)} %pad_maximum_fusion.own.co_ref), channel_id=1, source_target_pairs={{0,1},{1,0},{2,3},{3,2},{4,5},{5,4},{6,7},{7,6},{8,9},{9,8},{10,11... | collective-permute-start | bytes 245768 | tf_op jit(solution)/shard_map/ppermute | solution.py:446
  20.6 0.1 iota_compare_fusion
  20.6 0.1 lt.42
  20.7 0.1 squeeze.3
  20.8 3.5 %all-to-all-start.1 = ((bf16[8,320,128]{2,1,0:T(8,128)(2,1)}), bf16[8,320,128]{2,1,0:T(8,128)(2,1)S(1)}, u32[]{:S(2)}, u32[]{:S(2)}) async-start(bf16[8,320,128]{2,1,0:T(8,128)(2,1)} %get-tuple-element.20), calls=%async_computation.1 | async-start | bytes 1310720 | tf_op jit(solution)/shard_map/all_to_all | solution.py:501
  24.4 0.6 collective-permute-done.near_a.ca_ref
  24.9 7.2 %shard_map.111 = (bf16[8,64,256]{2,1,0:T(8,128)(2,1)S(1)}, bf16[8,64,256]{2,1,0:T(8,128)(2,1)S(1)}) custom-call(s32[1,1]{1,0:T(1,128)} %bitcast.odd, f32[80,256]{1,0:T(8,128)S(1)} %collective-permute-done.near_a.ca_ref, f32[80,256]{1,0:T(8,128)S(1)} %pad_maximum_fusion.own.co_ref, f32[80,256]{1,0:T(8,128)S(1)} %collective-permute-done.1.near_b.cb_ref, ...), custom_call_target="tpu_custom_call" | custom-call | flops 10000000000 | bytes 1000000 | tf_op jit(solution)/shard_map/pallas_call | solution.py:512
  32.1 3.9 %all-to-all-done.1.x_ref = bf16[8,320,128]{2,1,0:T(8,128)(2,1)S(1)} async-done(((bf16[8,320,128]{2,1,0:T(8,128)(2,1)}), bf16[8,320,128]{2,1,0:T(8,128)(2,1)S(1)}, u32[]{:S(2)}, u32[]{:S(2)}) %all-to-all-start.1) | async-done | bytes 655392 | tf_op jit(solution)/shard_map/all_to_all | solution.py:501
  36.0 1.8 %shard_map.112 = bf16[8,8,40,128]{3,2,1,0:T(8,128)(2,1)S(1)} custom-call(bf16[8,64,256]{2,1,0:T(8,128)(2,1)S(1)} %get-tuple-element.18.hi_ref, bf16[8,64,256]{2,1,0:T(8,128)(2,1)S(1)} %get-tuple-element.19.lo_ref, bf16[8,320,128]{2,1,0:T(8,128)(2,1)S(1)} %all-to-all-done.1.x_ref), custom_call_target="tpu_custom_call" | custom-call | flops 1000000000 | bytes 1000000 | tf_op jit(solution)/shard_map/pallas_call | solution.py:525
  37.8 14.2 %all_to_all.15.x_ref = bf16[8,8,40,128]{3,2,1,0:T(8,128)(2,1)S(1)} all-to-all(bf16[8,8,40,128]{3,2,1,0:T(8,128)(2,1)S(1)} %shard_map.112), channel_id=1, replica_groups=mesh['mem'=8,'space'=64] {'mem'}, dimensions={0} | all-to-all | bytes 1310720 | tf_op jit(solution)/shard_map/all_to_all | solution.py:531
  52.0 0.5 shard_map.113.own_ref
  52.6 3.3 %collective-permute-start.3 = (bf16[2,8,160,128]{3,2,1,0:T(8,128)(2,1)S(1)}, bf16[2,8,160,128]{3,2,1,0:T(8,128)(2,1)S(1)}, u32[]{:S(2)}, u32[]{:S(2)}) collective-permute-start(bf16[2,8,160,128]{3,2,1,0:T(8,128)(2,1)S(1)} %shard_map.113.own_ref), channel_id=1, source_target_pairs={{1,2},{2,1},{3,4},{4,3},{5,6},{6,5},{7,8},{8,7},{9,10},{10,9},{11,... | collective-permute-start | bytes 1966088 | tf_op jit(solution)/shard_map/ppermute | solution.py:446
  55.8 2.6 %collective-permute-start.2 = (bf16[2,8,160,128]{3,2,1,0:T(8,128)(2,1)S(1)}, bf16[2,8,160,128]{3,2,1,0:T(8,128)(2,1)S(1)}, u32[]{:S(2)}, u32[]{:S(2)}) collective-permute-start(bf16[2,8,160,128]{3,2,1,0:T(8,128)(2,1)S(1)} %shard_map.113.own_ref), channel_id=1, source_target_pairs={{0,1},{1,0},{2,3},{3,2},{4,5},{5,4},{6,7},{7,6},{8,9},{9,8},{10,11... | collective-permute-start | bytes 1966088 | tf_op jit(solution)/shard_map/ppermute | solution.py:446
  58.4 15.6 %collective-permute-done.3.b_ref = bf16[2,8,160,128]{3,2,1,0:T(8,128)(2,1)S(1)} collective-permute-done((bf16[2,8,160,128]{3,2,1,0:T(8,128)(2,1)S(1)}, bf16[2,8,160,128]{3,2,1,0:T(8,128)(2,1)S(1)}, u32[]{:S(2)}, u32[]{:S(2)}) %collective-permute-start.3) | collective-permute-done | bytes 655392 | tf_op jit(solution)/shard_map/ppermute | solution.py:446
  74.1 3.2 %shard_map.114 = bf16[2560,128]{1,0:T(8,128)(2,1)} custom-call(s32[1,1]{1,0:T(1,128)} %bitcast.odd, bf16[2,8,160,128]{3,2,1,0:T(8,128)(2,1)S(1)} %collective-permute-done.2.a_ref, bf16[2,8,160,128]{3,2,1,0:T(8,128)(2,1)S(1)} %shard_map.113.own_ref, bf16[2,8,160,128]{3,2,1,0:T(8,128)(2,1)S(1)} %collective-permute-done.3.b_ref, ...), custom_call_target="tpu_custom_call" | custom-call | flops 1000000000 | bytes 1000000 | tf_op jit(solution)/shard_map/pallas_call | solution.py:548
  (18 shorter events, 0.1 us)
Async XLA Ops:
  2.2 10.1 %all-to-all-start = ((f32[8,8,256]{2,1,0:T(8,128)}), f32[8,8,256]{2,1,0:T(8,128)S(1)}, u32[]{:S(2)}, u32[]{:S(2)}) async-start(f32[8,8,256]{2,1,0:T(8,128)} %shard_map.110), calls=%async_computation | async-start | bytes 131072 | tf_op jit(solution)/shard_map/all_to_all | solution.py:486
  6.9 0.7 copy-start.4
  6.9 0.7 copy-start.5
  6.9 0.7 copy-start.2
  6.9 0.7 copy-start.1
  6.9 0.7 copy-start.3
  7.6 1.1 %copy-start = (bf16[8,160,2,128]{3,2,1,0:T(2,128)(2,1)S(1)}, bf16[8,160,2,128]{3,2,1,0:T(2,128)(2,1)}, u32[]{:S(2)}) copy-start(bf16[8,160,2,128]{3,2,1,0:T(2,128)(2,1)} %param.11) | copy-start | bytes 1966084
  12.3 8.3 %copy-start.9 = (s32[1,32]{1,0:T(1,128)S(1)}, s32[1,32]{1,0:T(1,128)}, u32[]{:S(2)}) copy-start(s32[1,32]{1,0:T(1,128)} %param.17) | copy-start | bytes 388
  12.3 8.4 %copy-start.8 = (s32[1,32,32]{2,1,0:T(8,128)S(1)}, s32[1,32,32]{2,1,0:T(8,128)}, u32[]{:S(2)}) copy-start(s32[1,32,32]{2,1,0:T(8,128)} %param.16) | copy-start | bytes 12292
  12.3 12.1 %collective-permute-start.1 = (f32[80,256]{1,0:T(8,128)S(1)}, f32[80,256]{1,0:T(8,128)S(1)}, u32[]{:S(2)}, u32[]{:S(2)}) collective-permute-start(f32[80,256]{1,0:T(8,128)S(1)} %pad_maximum_fusion.own.co_ref), channel_id=1, source_target_pairs={{1,2},{2,1},{3,4},{4,3},{5,6},{6,5},{7,8},{8,7},{9,10},{10,9},{11,... | collective-permute-start | bytes 245768 | tf_op jit(solution)/shard_map/ppermute | solution.py:446
  18.6 6.3 %collective-permute-start = (f32[80,256]{1,0:T(8,128)S(1)}, f32[80,256]{1,0:T(8,128)S(1)}, u32[]{:S(2)}, u32[]{:S(2)}) collective-permute-start(f32[80,256]{1,0:T(8,128)S(1)} %pad_maximum_fusion.own.co_ref), channel_id=1, source_target_pairs={{0,1},{1,0},{2,3},{3,2},{4,5},{5,4},{6,7},{7,6},{8,9},{9,8},{10,11... | collective-permute-start | bytes 245768 | tf_op jit(solution)/shard_map/ppermute | solution.py:446
  20.8 15.2 %all-to-all-start.1 = ((bf16[8,320,128]{2,1,0:T(8,128)(2,1)}), bf16[8,320,128]{2,1,0:T(8,128)(2,1)S(1)}, u32[]{:S(2)}, u32[]{:S(2)}) async-start(bf16[8,320,128]{2,1,0:T(8,128)(2,1)} %get-tuple-element.20), calls=%async_computation.1 | async-start | bytes 1310720 | tf_op jit(solution)/shard_map/all_to_all | solution.py:501
  52.5 21.5 %copy-start.6 = (f32[2,128]{1,0:T(2,128)S(1)}, f32[2,128]{1,0:T(2,128)}, u32[]{:S(2)}) copy-start(f32[2,128]{1,0:T(2,128)} %surf_ref.1) | copy-start | bytes 3076
  52.6 21.5 %copy-start.7 = (f32[40]{0:T(128)S(1)}, f32[40]{0:T(128)}, u32[]{:S(2)}) copy-start(f32[40]{0:T(128)} %param.20) | copy-start | bytes 484
  52.6 21.5 %collective-permute-start.3 = (bf16[2,8,160,128]{3,2,1,0:T(8,128)(2,1)S(1)}, bf16[2,8,160,128]{3,2,1,0:T(8,128)(2,1)S(1)}, u32[]{:S(2)}, u32[]{:S(2)}) collective-permute-start(bf16[2,8,160,128]{3,2,1,0:T(8,128)(2,1)S(1)} %shard_map.113.own_ref), channel_id=1, source_target_pairs={{1,2},{2,1},{3,4},{4,3},{5,6},{6,5},{7,8},{8,7},{9,10},{10,9},{11,... | collective-permute-start | bytes 1966088 | tf_op jit(solution)/shard_map/ppermute | solution.py:446
  55.8 18.2 %collective-permute-start.2 = (bf16[2,8,160,128]{3,2,1,0:T(8,128)(2,1)S(1)}, bf16[2,8,160,128]{3,2,1,0:T(8,128)(2,1)S(1)}, u32[]{:S(2)}, u32[]{:S(2)}) collective-permute-start(bf16[2,8,160,128]{3,2,1,0:T(8,128)(2,1)S(1)} %shard_map.113.own_ref), channel_id=1, source_target_pairs={{0,1},{1,0},{2,3},{3,2},{4,5},{5,4},{6,7},{7,6},{8,9},{9,8},{10,11... | collective-permute-start | bytes 1966088 | tf_op jit(solution)/shard_map/ppermute | solution.py:446

commit v7 on v5

--- a/solution.py
+++ b/solution.py
@@ -395,7 +395,7 @@
 
 
 def first_side_kernel(odd, side_ref, own_ref, side_wind, own_wind, o_ref):
-    is_high = odd[0, 0] == 0
+    is_high = odd[0, 0] == 1
     coeffs = side_coeffs(is_high, own_wind[72:80], side_wind[72:80])
     shift = shift_matrix()
     for m, f in all_units(own_ref):
@@ -405,7 +405,7 @@
         o_ref[1, m, f : f + PART] = outs[1]
 
 
-def advect_kernel(odd, b_ref, own_ref, a_mid, ca_ref, co_ref, cb_ref, dep_ref, surf_ref, *refs):
+def advect_kernel(odd, a_ref, own_ref, b_mid, ca_ref, co_ref, cb_ref, dep_ref, surf_ref, *refs):
     o_ref, fac, flat, ready, sems = refs
     members, fields = own_ref.shape[1], own_ref.shape[2]
     span = 2 * fields
@@ -420,8 +420,9 @@
     units = all_units(own_ref)
 
     def first(m, f):
-        planes = side_rows(is_odd, b_ref, own_ref, m, f, coeffs_b)
-        return columns_step(planes, [c[1] for c in coeffs_b], shift)
+        high = jnp.logical_not(is_odd)
+        planes = side_rows(high, a_ref, own_ref, m, f, coeffs_a)
+        return columns_step(planes, [c[1] for c in coeffs_a], shift)
 
     ahead = 2
     mids = {u: first(*units[u]) for u in range(ahead)}
@@ -429,8 +430,8 @@
     for u, (m, f) in enumerate(units):
         if u + ahead < len(units):
             mids[u + ahead] = first(*units[u + ahead])
-        own_b, out_b = mids.pop(u)
-        own_a, out_a = a_mid[0, m, f : f + PART], a_mid[1, m, f : f + PART]
+        own_a, out_a = mids.pop(u)
+        own_b, out_b = b_mid[0, m, f : f + PART], b_mid[1, m, f : f + PART]
         planes = [
             rows_step(own_b, own_a, out_a, coeffs_a[0][0]),
             rows_step(own_a, own_b, out_b, coeffs_b[0][0]),
@@ -561,13 +562,14 @@
     planes = call(
         relayout_kernel, [jax.ShapeDtypeStruct(plane_shape, BF16)], flops=10**8
     )(returned)[0]
-    side_a, side_b = swap(planes, 0), swap(planes, 1)
-    a_mid = call(
+    side_b = swap(planes, 1)
+    side_a = swap(planes, 0)
+    b_mid = call(
         first_side_kernel,
         jax.ShapeDtypeStruct(plane_shape, F32),
         flops=10**8,
         specs=[smem] + [VMEM] * 4,
-    )(odd, side_a, planes, near_a, packed)
+    )(odd, side_b, planes, near_b, packed)
     done = pl.pallas_call(
         advect_kernel,
         out_shape=jax.ShapeDtypeStruct(flat.shape, BF16),
@@ -582,7 +584,7 @@
         compiler_params=params(),
         cost_estimate=cost(10**9),
     )(
-        odd, side_b, planes, a_mid, near_a, packed, near_b,
+        odd, side_a, planes, b_mid, near_a, packed, near_b,
         dep_velocity.reshape(1, -1), surface_factor,
     )
     return done.reshape(local, fields, tile_rows, columns)

time: 82.8 us -> 80 us (0.966)
  waiting for transfers between devices: 22 us -> 20.2 us
  starting transfers between devices: 24.3 us -> 23.4 us
    ppermute x4, waiting for transfers between devices: 17.5 us -> 15.6 us  [swap(): return lax.ppermute(x, 'space', pairs)]
    ppermute x4, starting transfers between devices: 15 us -> 14.1 us  [swap(): return lax.ppermute(x, 'space', pairs)]
  transfers between devices with their start and end apart: 6 -> 6, of which waited for: 3 -> 2; matrix products, arithmetic and copies ran while one was open for 1% -> 1% of each run, Pallas kernels for 11% -> 12%
where the time goes in v7:
time: 80 us; the launch traced here: 79.4 us
  starting transfers between devices  23.4 us (29%)
  waiting for transfers between devices  20.2 us (25%)
  Pallas kernels  16.6 us (21%)
  blocking collectives  14.2 us (18%)
  local copies, waits for them, and re-layouts  4.83 us (6%)
    ppermute x4, waiting for transfers between devices, swap(): return lax.ppermute(x, 'space', pairs)  15.6 us
    all_to_all x1, blocking collectives, shards(): returned = lax.all_to_all(back, 'mem', 0, 0, tiled=True)  14.2 us
    ppermute x4, starting transfers between devices, swap(): return lax.ppermute(x, 'space', pairs)  14.1 us
    pallas_call x1, Pallas kernels, shards(): call(weights_kernel, [jax.ShapeDtypeStruct((groups, 64, 256), BF16)] * 2,...  7.19 us
    all_to_all x1, starting transfers between devices, shards(): state = lax.all_to_all(payload, 'mem', 0, 0, tiled=True)  4.81 us
    all_to_all x1, waiting for transfers between devices, shards(): state = lax.all_to_all(payload, 'mem', 0, 0, tiled=True)  4.52 us
    unnamed x20, local copies, waits for them, and re-layouts  4.51 us
    all_to_all x1, starting transfers between devices, shards(): everywhere = lax.all_to_all(equiv, 'mem', 0, 0, tiled=True)  4.47 us
  transfers between devices with their start and end apart: 6, of which 2 were waited for; matrix products, arithmetic and copies ran while one was open for 1% of the time, Pallas kernels for 12%

profile of v7, /device:TPU:384, one launch (start us, length us, event | category | flops | bytes accessed | tf_op | source)
XLA Modules:
  0.0 79.4 jit_solution(5839256615427569320)
XLA Ops:
  0.0 2.2 %shard_map.110 = f32[8,8,256]{2,1,0:T(8,128)} custom-call(bf16[8,40,4,2,128]{4,3,2,1,0:T(2,128)(2,1)} %bitcast.7, s32[1,256]{1,0:T(1,128)} %cell.3, s32[1,256]{1,0:T(1,128)} %kind.1), custom_call_target="tpu_custom_call" | custom-call | flops 100000000 | bytes 1000000 | tf_op jit(solution)/shard_map/pallas_call | solution.py:501
  2.2 4.5 %all-to-all-start = ((f32[8,8,256]{2,1,0:T(8,128)}), f32[8,8,256]{2,1,0:T(8,128)S(1)}, u32[]{:S(2)}, u32[]{:S(2)}) async-start(f32[8,8,256]{2,1,0:T(8,128)} %shard_map.110), calls=%async_computation | async-start | bytes 131072 | tf_op jit(solution)/shard_map/all_to_all | solution.py:515
  6.7 0.1 broadcast_in_dim.12
  6.7 0.1 reshape.203
  6.9 0.0 copy-start
  6.9 1.1 %copy-done = bf16[8,160,2,128]{3,2,1,0:T(2,128)(2,1)S(1)} copy-done((bf16[8,160,2,128]{3,2,1,0:T(2,128)(2,1)S(1)}, bf16[8,160,2,128]{3,2,1,0:T(2,128)(2,1)}, u32[]{:S(2)}) %copy-start) | copy-done | bytes 655384
  8.0 0.7 copy-done.1
  8.7 0.7 copy-done.2
  9.4 0.7 copy-done.3
  10.1 0.7 copy-done.4
  10.7 0.7 copy-done.5
  11.4 1.4 %shard_map.109 = (bf16[8,320,128]{2,1,0:T(8,128)(2,1)}, f32[16,256]{1,0:T(8,128)S(1)}) custom-call(bf16[2560,128]{1,0:T(8,128)(2,1)S(1)} %bitcast.8, s32[1,256]{1,0:T(1,128)S(1)} %copy-done.3, f32[1,256]{1,0:T(1,128)S(1)} %copy-done.4, f32[1,256]{1,0:T(1,128)S(1)} %copy-done.5, f32[4,2,128]{2,1,0:T(2,128)S(1)} %copy-done.1, f32[4,2,128]{2,1,0:T(2,128)S(1)} %copy-done.2), custom_call_target="tpu_custom_call" | custom-call | flops 100000000 | bytes 1000000 | tf_op jit(solution)/shard_map/pallas_call | solution.py:516
  12.8 6.3 %collective-permute-start.1 = (f32[80,256]{1,0:T(8,128)S(1)}, f32[80,256]{1,0:T(8,128)S(1)}, u32[]{:S(2)}, u32[]{:S(2)}) collective-permute-start(f32[80,256]{1,0:T(8,128)S(1)} %pad_maximum_fusion.own.own_wind.co_ref), channel_id=1, source_target_pairs={{1,2},{2,1},{3,4},{4,3},{5,6},{6,5},{7,8},{8,7},{9,10},{10,9},{11,... | collective-permute-start | bytes 245768 | tf_op jit(solution)/shard_map/ppermute | solution.py:476
  19.1 1.9 %collective-permute-start = (f32[80,256]{1,0:T(8,128)S(1)}, f32[80,256]{1,0:T(8,128)S(1)}, u32[]{:S(2)}, u32[]{:S(2)}) collective-permute-start(f32[80,256]{1,0:T(8,128)S(1)} %pad_maximum_fusion.own.own_wind.co_ref), channel_id=1, source_target_pairs={{0,1},{1,0},{2,3},{3,2},{4,5},{5,4},{6,7},{7,6},{8,9},{9,8},{10,11... | collective-permute-start | bytes 245768 | tf_op jit(solution)/shard_map/ppermute | solution.py:476
  21.0 0.1 iota_compare_fusion
  21.1 0.1 lt.42
  21.2 0.1 squeeze.3
  21.3 4.8 %all-to-all-start.1 = ((bf16[8,320,128]{2,1,0:T(8,128)(2,1)}), bf16[8,320,128]{2,1,0:T(8,128)(2,1)S(1)}, u32[]{:S(2)}, u32[]{:S(2)}) async-start(bf16[8,320,128]{2,1,0:T(8,128)(2,1)} %get-tuple-element.20), calls=%async_computation.1 | async-start | bytes 1310720 | tf_op jit(solution)/shard_map/all_to_all | solution.py:530
  26.1 0.0 collective-permute-done.1.near_b.side_wind.cb_ref
  26.1 0.0 collective-permute-done.near_a.ca_ref
  26.1 7.2 %shard_map.111 = (bf16[8,64,256]{2,1,0:T(8,128)(2,1)S(1)}, bf16[8,64,256]{2,1,0:T(8,128)(2,1)S(1)}) custom-call(s32[1,1]{1,0:T(1,128)} %bitcast.odd, f32[80,256]{1,0:T(8,128)S(1)} %collective-permute-done.near_a.ca_ref, f32[80,256]{1,0:T(8,128)S(1)} %pad_maximum_fusion.own.own_wind.co_ref, f32[80,256]{1,0:T(8,128)S(1)} %collective-permute-done.1.near_b.side_wind.cb_ref, ...), custom_call_target="tpu_custom_call" | custom-call | flops 10000000000 | bytes 1000000 | tf_op jit(solution)/shard_map/pallas_call | solution.py:541
  33.3 4.5 %all-to-all-done.1.x_ref = bf16[8,320,128]{2,1,0:T(8,128)(2,1)S(1)} async-done(((bf16[8,320,128]{2,1,0:T(8,128)(2,1)}), bf16[8,320,128]{2,1,0:T(8,128)(2,1)S(1)}, u32[]{:S(2)}, u32[]{:S(2)}) %all-to-all-start.1) | async-done | bytes 655392 | tf_op jit(solution)/shard_map/all_to_all | solution.py:530
  37.9 1.8 %shard_map.112 = bf16[8,8,40,128]{3,2,1,0:T(8,128)(2,1)S(1)} custom-call(bf16[8,64,256]{2,1,0:T(8,128)(2,1)S(1)} %get-tuple-element.18.hi_ref, bf16[8,64,256]{2,1,0:T(8,128)(2,1)S(1)} %get-tuple-element.19.lo_ref, bf16[8,320,128]{2,1,0:T(8,128)(2,1)S(1)} %all-to-all-done.1.x_ref), custom_call_target="tpu_custom_call" | custom-call | flops 1000000000 | bytes 1000000 | tf_op jit(solution)/shard_map/pallas_call | solution.py:554
  39.7 14.2 %all_to_all.15.x_ref = bf16[8,8,40,128]{3,2,1,0:T(8,128)(2,1)S(1)} all-to-all(bf16[8,8,40,128]{3,2,1,0:T(8,128)(2,1)S(1)} %shard_map.112), channel_id=1, replica_groups=mesh['mem'=8,'space'=64] {'mem'}, dimensions={0} | all-to-all | bytes 1310720 | tf_op jit(solution)/shard_map/all_to_all | solution.py:560
  53.9 0.5 shard_map.113.own_ref
  54.4 0.0 copy-start.6
  54.4 0.0 copy-start.7
  54.4 3.3 %collective-permute-start.3 = (bf16[2,8,160,128]{3,2,1,0:T(8,128)(2,1)S(1)}, bf16[2,8,160,128]{3,2,1,0:T(8,128)(2,1)S(1)}, u32[]{:S(2)}, u32[]{:S(2)}) collective-permute-start(bf16[2,8,160,128]{3,2,1,0:T(8,128)(2,1)S(1)} %shard_map.113.own_ref), channel_id=1, source_target_pairs={{1,2},{2,1},{3,4},{4,3},{5,6},{6,5},{7,8},{8,7},{9,10},{10,9},{11,... | collective-permute-start | bytes 1966088 | tf_op jit(solution)/shard_map/ppermute | solution.py:476
  57.7 2.6 %collective-permute-start.2 = (bf16[2,8,160,128]{3,2,1,0:T(8,128)(2,1)S(1)}, bf16[2,8,160,128]{3,2,1,0:T(8,128)(2,1)S(1)}, u32[]{:S(2)}, u32[]{:S(2)}) collective-permute-start(bf16[2,8,160,128]{3,2,1,0:T(8,128)(2,1)S(1)} %shard_map.113.own_ref), channel_id=1, source_target_pairs={{0,1},{1,0},{2,3},{3,2},{4,5},{5,4},{6,7},{7,6},{8,9},{9,8},{10,11... | collective-permute-start | bytes 1966088 | tf_op jit(solution)/shard_map/ppermute | solution.py:476
  60.3 15.6 %collective-permute-done.3.side_ref = bf16[2,8,160,128]{3,2,1,0:T(8,128)(2,1)S(1)} collective-permute-done((bf16[2,8,160,128]{3,2,1,0:T(8,128)(2,1)S(1)}, bf16[2,8,160,128]{3,2,1,0:T(8,128)(2,1)S(1)}, u32[]{:S(2)}, u32[]{:S(2)}) %collective-permute-start.3) | collective-permute-done | bytes 655392 | tf_op jit(solution)/shard_map/ppermute | solution.py:476
  75.9 0.9 %shard_map.114.b_mid = f32[2,8,160,128]{3,2,1,0:T(8,128)S(1)} custom-call(s32[1,1]{1,0:T(1,128)} %bitcast.odd, bf16[2,8,160,128]{3,2,1,0:T(8,128)(2,1)S(1)} %collective-permute-done.3.side_ref, bf16[2,8,160,128]{3,2,1,0:T(8,128)(2,1)S(1)} %shard_map.113.own_ref, f32[80,256]{1,0:T(8,128)S(1)} %collective-permute-done.1.near_b.side_wind.cb_ref, ...), custom_call_target="tpu_custom_call" | custom-call | flops 100000000 | bytes 1000000 | tf_op jit(solution)/shard_map/pallas_call | solution.py:567
  76.8 2.6 %shard_map.115 = bf16[2560,128]{1,0:T(8,128)(2,1)} custom-call(s32[1,1]{1,0:T(1,128)} %bitcast.odd, bf16[2,8,160,128]{3,2,1,0:T(8,128)(2,1)S(1)} %collective-permute-done.2.a_ref, bf16[2,8,160,128]{3,2,1,0:T(8,128)(2,1)S(1)} %shard_map.113.own_ref, f32[2,8,160,128]{3,2,1,0:T(8,128)S(1)} %shard_map.114.b_mid, ...), custom_call_target="tpu_custom_call" | custom-call | flops 1000000000 | bytes 1000000 | tf_op jit(solution)/shard_map/pallas_call | solution.py:573
  (19 shorter events, 0.1 us)
Async XLA Ops:
  0.0 21.0 %copy-start.9 = (s32[1,32]{1,0:T(1,128)S(1)}, s32[1,32]{1,0:T(1,128)}, u32[]{:S(2)}) copy-start(s32[1,32]{1,0:T(1,128)} %param.17) | copy-start | bytes 388
  0.0 21.2 %copy-start.8 = (s32[1,32,32]{2,1,0:T(8,128)S(1)}, s32[1,32,32]{2,1,0:T(8,128)}, u32[]{:S(2)}) copy-start(s32[1,32,32]{2,1,0:T(8,128)} %param.16) | copy-start | bytes 12292
  2.2 10.6 %all-to-all-start = ((f32[8,8,256]{2,1,0:T(8,128)}), f32[8,8,256]{2,1,0:T(8,128)S(1)}, u32[]{:S(2)}, u32[]{:S(2)}) async-start(f32[8,8,256]{2,1,0:T(8,128)} %shard_map.110), calls=%async_computation | async-start | bytes 131072 | tf_op jit(solution)/shard_map/all_to_all | solution.py:515
  6.9 1.1 %copy-start = (bf16[8,160,2,128]{3,2,1,0:T(2,128)(2,1)S(1)}, bf16[8,160,2,128]{3,2,1,0:T(2,128)(2,1)}, u32[]{:S(2)}) copy-start(bf16[8,160,2,128]{3,2,1,0:T(2,128)(2,1)} %param.11) | copy-start | bytes 1966084
  8.0 0.7 copy-start.1
  8.7 0.7 copy-start.2
  9.4 0.7 copy-start.3
  10.0 0.7 copy-start.4
  10.7 0.7 copy-start.5
  12.8 13.3 %collective-permute-start.1 = (f32[80,256]{1,0:T(8,128)S(1)}, f32[80,256]{1,0:T(8,128)S(1)}, u32[]{:S(2)}, u32[]{:S(2)}) collective-permute-start(f32[80,256]{1,0:T(8,128)S(1)} %pad_maximum_fusion.own.own_wind.co_ref), channel_id=1, source_target_pairs={{1,2},{2,1},{3,4},{4,3},{5,6},{6,5},{7,8},{8,7},{9,10},{10,9},{11,... | collective-permute-start | bytes 245768 | tf_op jit(solution)/shard_map/ppermute | solution.py:476
  19.1 7.0 %collective-permute-start = (f32[80,256]{1,0:T(8,128)S(1)}, f32[80,256]{1,0:T(8,128)S(1)}, u32[]{:S(2)}, u32[]{:S(2)}) collective-permute-start(f32[80,256]{1,0:T(8,128)S(1)} %pad_maximum_fusion.own.own_wind.co_ref), channel_id=1, source_target_pairs={{0,1},{1,0},{2,3},{3,2},{4,5},{5,4},{6,7},{7,6},{8,9},{9,8},{10,11... | collective-permute-start | bytes 245768 | tf_op jit(solution)/shard_map/ppermute | solution.py:476
  21.3 16.6 %all-to-all-start.1 = ((bf16[8,320,128]{2,1,0:T(8,128)(2,1)}), bf16[8,320,128]{2,1,0:T(8,128)(2,1)S(1)}, u32[]{:S(2)}, u32[]{:S(2)}) async-start(bf16[8,320,128]{2,1,0:T(8,128)(2,1)} %get-tuple-element.20), calls=%async_computation.1 | async-start | bytes 1310720 | tf_op jit(solution)/shard_map/all_to_all | solution.py:530
  54.4 22.4 %copy-start.6 = (f32[2,128]{1,0:T(2,128)S(1)}, f32[2,128]{1,0:T(2,128)}, u32[]{:S(2)}) copy-start(f32[2,128]{1,0:T(2,128)} %surf_ref.1) | copy-start | bytes 3076
  54.4 22.4 %copy-start.7 = (f32[40]{0:T(128)S(1)}, f32[40]{0:T(128)}, u32[]{:S(2)}) copy-start(f32[40]{0:T(128)} %param.20) | copy-start | bytes 484
  54.4 21.5 %collective-permute-start.3 = (bf16[2,8,160,128]{3,2,1,0:T(8,128)(2,1)S(1)}, bf16[2,8,160,128]{3,2,1,0:T(8,128)(2,1)S(1)}, u32[]{:S(2)}, u32[]{:S(2)}) collective-permute-start(bf16[2,8,160,128]{3,2,1,0:T(8,128)(2,1)S(1)} %shard_map.113.own_ref), channel_id=1, source_target_pairs={{1,2},{2,1},{3,4},{4,3},{5,6},{6,5},{7,8},{8,7},{9,10},{10,9},{11,... | collective-permute-start | bytes 1966088 | tf_op jit(solution)/shard_map/ppermute | solution.py:476
  57.7 19.1 %collective-permute-start.2 = (bf16[2,8,160,128]{3,2,1,0:T(8,128)(2,1)S(1)}, bf16[2,8,160,128]{3,2,1,0:T(8,128)(2,1)S(1)}, u32[]{:S(2)}, u32[]{:S(2)}) collective-permute-start(bf16[2,8,160,128]{3,2,1,0:T(8,128)(2,1)S(1)} %shard_map.113.own_ref), channel_id=1, source_target_pairs={{0,1},{1,0},{2,3},{3,2},{4,5},{5,4},{6,7},{7,6},{8,9},{9,8},{10,11... | collective-permute-start | bytes 1966088 | tf_op jit(solution)/shard_map/ppermute | solution.py:476

commit v8 on v6

--- a/solution.py
+++ b/solution.py
@@ -363,7 +363,7 @@
         ((shift_out < 128) & (shift_in == shift_out - 1))
         | ((shift_out >= 128) & (shift_in == shift_out - 127))
     ).astype(F32).astype(BF16)
-    part = 80
+    part = 160
 
     def scale(c, q):
         return (q.reshape(part // 8, 8, 128) * c[None]).reshape(part, 128)
@@ -396,7 +396,7 @@
         q = [x.astype(F32) for x in q]
         return cols([rows(q[i], q[i + 1], q[i + 2], i) for i in range(4)], 0)
 
-    ahead = 2
+    ahead = 1
     mids = {u: first(*units[u]) for u in range(ahead)}
     copies = []
     for u, (m, f) in enumerate(units):

time: 77.9 us -> 77.9 us (level)
  no operation moved by 1% of the time
where the time goes in v8:
time: 77.9 us; the launch traced here: 77.3 us
  waiting for transfers between devices  22.3 us (29%)
  starting transfers between devices  22.1 us (28%)
  Pallas kernels  16.2 us (21%)
  blocking collectives  14.2 us (18%)
  local copies, waits for them, and re-layouts  2.13 us (3%)
    ppermute x4, waiting for transfers between devices, swap(): return lax.ppermute(x, 'space', pairs)  16.2 us
    all_to_all x1, blocking collectives, shards(): returned = lax.all_to_all(back, 'mem', 0, 0, tiled=True)  14.2 us
    ppermute x4, starting transfers between devices, swap(): return lax.ppermute(x, 'space', pairs)  14.1 us
    pallas_call x1, Pallas kernels, shards(): call(weights_kernel, [jax.ShapeDtypeStruct((groups, 64, 256), BF16)] * 2,...  7.18 us
    all_to_all x1, starting transfers between devices, shards(): everywhere = lax.all_to_all(equiv, 'mem', 0, 0, tiled=True)  4.49 us
    all_to_all x1, waiting for transfers between devices, shards(): state = lax.all_to_all(payload, 'mem', 0, 0, tiled=True)  3.88 us
    all_to_all x1, starting transfers between devices, shards(): state = lax.all_to_all(payload, 'mem', 0, 0, tiled=True)  3.55 us
    pallas_call x1, Pallas kernels, shards(): pl.pallas_call(functools.partial(advect_kernel, start), out_shape=jax.Sha...  3.23 us
  transfers between devices with their start and end apart: 6, of which 4 were waited for; matrix products, arithmetic and copies ran while one was open for 1% of the time, Pallas kernels for 11%

profile of v8, /device:TPU:384, one launch (start us, length us, event | category | flops | bytes accessed | tf_op | source)
XLA Modules:
  0.0 77.3 jit_solution(17964161260924595875)
XLA Ops:
  0.0 2.1 %shard_map.110 = f32[8,8,256]{2,1,0:T(8,128)} custom-call(bf16[8,40,4,2,128]{4,3,2,1,0:T(2,128)(2,1)} %bitcast.7, s32[1,256]{1,0:T(1,128)} %cell.3, s32[1,256]{1,0:T(1,128)} %kind.1), custom_call_target="tpu_custom_call" | custom-call | flops 100000000 | bytes 1000000 | tf_op jit(solution)/shard_map/pallas_call | solution.py:472
  2.2 4.5 %all-to-all-start = ((f32[8,8,256]{2,1,0:T(8,128)}), f32[8,8,256]{2,1,0:T(8,128)S(1)}, u32[]{:S(2)}, u32[]{:S(2)}) async-start(f32[8,8,256]{2,1,0:T(8,128)} %shard_map.110), calls=%async_computation | async-start | bytes 131072 | tf_op jit(solution)/shard_map/all_to_all | solution.py:486
  6.7 0.1 broadcast_in_dim.12
  6.7 0.1 reshape.203
  6.9 0.0 copy-start.4
  6.9 0.0 copy-start.5
  6.9 0.0 copy-start.2
  6.9 0.6 copy-done.4
  7.6 0.0 copy-done.5
  7.6 0.0 copy-done.2
  7.6 0.0 copy-done.1
  7.6 0.0 copy-done.3
  7.6 1.1 %copy-done = bf16[8,160,2,128]{3,2,1,0:T(2,128)(2,1)S(1)} copy-done((bf16[8,160,2,128]{3,2,1,0:T(2,128)(2,1)S(1)}, bf16[8,160,2,128]{3,2,1,0:T(2,128)(2,1)}, u32[]{:S(2)}) %copy-start) | copy-done | bytes 655384
  8.7 1.4 %shard_map.109 = (bf16[8,320,128]{2,1,0:T(8,128)(2,1)}, f32[16,256]{1,0:T(8,128)S(1)}) custom-call(bf16[2560,128]{1,0:T(8,128)(2,1)S(1)} %bitcast.8, s32[1,256]{1,0:T(1,128)S(1)} %copy-done.3, f32[1,256]{1,0:T(1,128)S(1)} %copy-done.4, f32[1,256]{1,0:T(1,128)S(1)} %copy-done.5, f32[4,2,128]{2,1,0:T(2,128)S(1)} %copy-done.1, f32[4,2,128]{2,1,0:T(2,128)S(1)} %copy-done.2), custom_call_target="tpu_custom_call" | custom-call | flops 100000000 | bytes 1000000 | tf_op jit(solution)/shard_map/pallas_call | solution.py:487
  10.1 2.2 %all-to-all-done = f32[8,8,256]{2,1,0:T(8,128)S(1)} async-done(((f32[8,8,256]{2,1,0:T(8,128)}), f32[8,8,256]{2,1,0:T(8,128)S(1)}, u32[]{:S(2)}, u32[]{:S(2)}) %all-to-all-start) | async-done | bytes 65568 | tf_op jit(solution)/shard_map/all_to_all | solution.py:486
  12.3 0.0 copy-start.8
  12.3 6.3 %collective-permute-start.1 = (f32[80,256]{1,0:T(8,128)S(1)}, f32[80,256]{1,0:T(8,128)S(1)}, u32[]{:S(2)}, u32[]{:S(2)}) collective-permute-start(f32[80,256]{1,0:T(8,128)S(1)} %pad_maximum_fusion.own.co_ref), channel_id=1, source_target_pairs={{1,2},{2,1},{3,4},{4,3},{5,6},{6,5},{7,8},{8,7},{9,10},{10,9},{11,... | collective-permute-start | bytes 245768 | tf_op jit(solution)/shard_map/ppermute | solution.py:446
  18.6 1.9 %collective-permute-start = (f32[80,256]{1,0:T(8,128)S(1)}, f32[80,256]{1,0:T(8,128)S(1)}, u32[]{:S(2)}, u32[]{:S(2)}) collective-permute-start(f32[80,256]{1,0:T(8,128)S(1)} %pad_maximum_fusion.own.co_ref), channel_id=1, source_target_pairs={{0,1},{1,0},{2,3},{3,2},{4,5},{5,4},{6,7},{7,6},{8,9},{9,8},{10,11... | collective-permute-start | bytes 245768 | tf_op jit(solution)/shard_map/ppermute | solution.py:446
  20.6 0.1 iota_compare_fusion
  20.6 0.1 lt.42
  20.7 0.1 squeeze.3
  20.8 3.5 %all-to-all-start.1 = ((bf16[8,320,128]{2,1,0:T(8,128)(2,1)}), bf16[8,320,128]{2,1,0:T(8,128)(2,1)S(1)}, u32[]{:S(2)}, u32[]{:S(2)}) async-start(bf16[8,320,128]{2,1,0:T(8,128)(2,1)} %get-tuple-element.20), calls=%async_computation.1 | async-start | bytes 1310720 | tf_op jit(solution)/shard_map/all_to_all | solution.py:501
  24.4 0.6 collective-permute-done.near_a.ca_ref
  24.9 7.2 %shard_map.111 = (bf16[8,64,256]{2,1,0:T(8,128)(2,1)S(1)}, bf16[8,64,256]{2,1,0:T(8,128)(2,1)S(1)}) custom-call(s32[1,1]{1,0:T(1,128)} %bitcast.odd, f32[80,256]{1,0:T(8,128)S(1)} %collective-permute-done.near_a.ca_ref, f32[80,256]{1,0:T(8,128)S(1)} %pad_maximum_fusion.own.co_ref, f32[80,256]{1,0:T(8,128)S(1)} %collective-permute-done.1.near_b.cb_ref, ...), custom_call_target="tpu_custom_call" | custom-call | flops 10000000000 | bytes 1000000 | tf_op jit(solution)/shard_map/pallas_call | solution.py:512
  32.1 3.9 %all-to-all-done.1.x_ref = bf16[8,320,128]{2,1,0:T(8,128)(2,1)S(1)} async-done(((bf16[8,320,128]{2,1,0:T(8,128)(2,1)}), bf16[8,320,128]{2,1,0:T(8,128)(2,1)S(1)}, u32[]{:S(2)}, u32[]{:S(2)}) %all-to-all-start.1) | async-done | bytes 655392 | tf_op jit(solution)/shard_map/all_to_all | solution.py:501
  36.0 1.8 %shard_map.112 = bf16[8,8,40,128]{3,2,1,0:T(8,128)(2,1)S(1)} custom-call(bf16[8,64,256]{2,1,0:T(8,128)(2,1)S(1)} %get-tuple-element.18.hi_ref, bf16[8,64,256]{2,1,0:T(8,128)(2,1)S(1)} %get-tuple-element.19.lo_ref, bf16[8,320,128]{2,1,0:T(8,128)(2,1)S(1)} %all-to-all-done.1.x_ref), custom_call_target="tpu_custom_call" | custom-call | flops 1000000000 | bytes 1000000 | tf_op jit(solution)/shard_map/pallas_call | solution.py:525
  37.8 14.2 %all_to_all.15.x_ref = bf16[8,8,40,128]{3,2,1,0:T(8,128)(2,1)S(1)} all-to-all(bf16[8,8,40,128]{3,2,1,0:T(8,128)(2,1)S(1)} %shard_map.112), channel_id=1, replica_groups=mesh['mem'=8,'space'=64] {'mem'}, dimensions={0} | all-to-all | bytes 1310720 | tf_op jit(solution)/shard_map/all_to_all | solution.py:531
  52.0 0.5 shard_map.113.own_ref
  52.6 3.3 %collective-permute-start.3 = (bf16[2,8,160,128]{3,2,1,0:T(8,128)(2,1)S(1)}, bf16[2,8,160,128]{3,2,1,0:T(8,128)(2,1)S(1)}, u32[]{:S(2)}, u32[]{:S(2)}) collective-permute-start(bf16[2,8,160,128]{3,2,1,0:T(8,128)(2,1)S(1)} %shard_map.113.own_ref), channel_id=1, source_target_pairs={{1,2},{2,1},{3,4},{4,3},{5,6},{6,5},{7,8},{8,7},{9,10},{10,9},{11,... | collective-permute-start | bytes 1966088 | tf_op jit(solution)/shard_map/ppermute | solution.py:446
  55.8 2.6 %collective-permute-start.2 = (bf16[2,8,160,128]{3,2,1,0:T(8,128)(2,1)S(1)}, bf16[2,8,160,128]{3,2,1,0:T(8,128)(2,1)S(1)}, u32[]{:S(2)}, u32[]{:S(2)}) collective-permute-start(bf16[2,8,160,128]{3,2,1,0:T(8,128)(2,1)S(1)} %shard_map.113.own_ref), channel_id=1, source_target_pairs={{0,1},{1,0},{2,3},{3,2},{4,5},{5,4},{6,7},{7,6},{8,9},{9,8},{10,11... | collective-permute-start | bytes 1966088 | tf_op jit(solution)/shard_map/ppermute | solution.py:446
  58.4 15.6 %collective-permute-done.3.b_ref = bf16[2,8,160,128]{3,2,1,0:T(8,128)(2,1)S(1)} collective-permute-done((bf16[2,8,160,128]{3,2,1,0:T(8,128)(2,1)S(1)}, bf16[2,8,160,128]{3,2,1,0:T(8,128)(2,1)S(1)}, u32[]{:S(2)}, u32[]{:S(2)}) %collective-permute-start.3) | collective-permute-done | bytes 655392 | tf_op jit(solution)/shard_map/ppermute | solution.py:446
  74.1 3.2 %shard_map.114 = bf16[2560,128]{1,0:T(8,128)(2,1)} custom-call(s32[1,1]{1,0:T(1,128)} %bitcast.odd, bf16[2,8,160,128]{3,2,1,0:T(8,128)(2,1)S(1)} %collective-permute-done.2.a_ref, bf16[2,8,160,128]{3,2,1,0:T(8,128)(2,1)S(1)} %shard_map.113.own_ref, bf16[2,8,160,128]{3,2,1,0:T(8,128)(2,1)S(1)} %collective-permute-done.3.b_ref, ...), custom_call_target="tpu_custom_call" | custom-call | flops 1000000000 | bytes 1000000 | tf_op jit(solution)/shard_map/pallas_call | solution.py:548
  (18 shorter events, 0.1 us)
Async XLA Ops:
  2.2 10.1 %all-to-all-start = ((f32[8,8,256]{2,1,0:T(8,128)}), f32[8,8,256]{2,1,0:T(8,128)S(1)}, u32[]{:S(2)}, u32[]{:S(2)}) async-start(f32[8,8,256]{2,1,0:T(8,128)} %shard_map.110), calls=%async_computation | async-start | bytes 131072 | tf_op jit(solution)/shard_map/all_to_all | solution.py:486
  6.9 0.7 copy-start.4
  6.9 0.7 copy-start.5
  6.9 0.7 copy-start.2
  6.9 0.7 copy-start.1
  6.9 0.7 copy-start.3
  7.6 1.1 %copy-start = (bf16[8,160,2,128]{3,2,1,0:T(2,128)(2,1)S(1)}, bf16[8,160,2,128]{3,2,1,0:T(2,128)(2,1)}, u32[]{:S(2)}) copy-start(bf16[8,160,2,128]{3,2,1,0:T(2,128)(2,1)} %param.11) | copy-start | bytes 1966084
  12.3 8.3 %copy-start.9 = (s32[1,32]{1,0:T(1,128)S(1)}, s32[1,32]{1,0:T(1,128)}, u32[]{:S(2)}) copy-start(s32[1,32]{1,0:T(1,128)} %param.17) | copy-start | bytes 388
  12.3 8.4 %copy-start.8 = (s32[1,32,32]{2,1,0:T(8,128)S(1)}, s32[1,32,32]{2,1,0:T(8,128)}, u32[]{:S(2)}) copy-start(s32[1,32,32]{2,1,0:T(8,128)} %param.16) | copy-start | bytes 12292
  12.3 12.1 %collective-permute-start.1 = (f32[80,256]{1,0:T(8,128)S(1)}, f32[80,256]{1,0:T(8,128)S(1)}, u32[]{:S(2)}, u32[]{:S(2)}) collective-permute-start(f32[80,256]{1,0:T(8,128)S(1)} %pad_maximum_fusion.own.co_ref), channel_id=1, source_target_pairs={{1,2},{2,1},{3,4},{4,3},{5,6},{6,5},{7,8},{8,7},{9,10},{10,9},{11,... | collective-permute-start | bytes 245768 | tf_op jit(solution)/shard_map/ppermute | solution.py:446
  18.6 6.3 %collective-permute-start = (f32[80,256]{1,0:T(8,128)S(1)}, f32[80,256]{1,0:T(8,128)S(1)}, u32[]{:S(2)}, u32[]{:S(2)}) collective-permute-start(f32[80,256]{1,0:T(8,128)S(1)} %pad_maximum_fusion.own.co_ref), channel_id=1, source_target_pairs={{0,1},{1,0},{2,3},{3,2},{4,5},{5,4},{6,7},{7,6},{8,9},{9,8},{10,11... | collective-permute-start | bytes 245768 | tf_op jit(solution)/shard_map/ppermute | solution.py:446
  20.8 15.2 %all-to-all-start.1 = ((bf16[8,320,128]{2,1,0:T(8,128)(2,1)}), bf16[8,320,128]{2,1,0:T(8,128)(2,1)S(1)}, u32[]{:S(2)}, u32[]{:S(2)}) async-start(bf16[8,320,128]{2,1,0:T(8,128)(2,1)} %get-tuple-element.20), calls=%async_computation.1 | async-start | bytes 1310720 | tf_op jit(solution)/shard_map/all_to_all | solution.py:501
  52.5 21.5 %copy-start.6 = (f32[2,128]{1,0:T(2,128)S(1)}, f32[2,128]{1,0:T(2,128)}, u32[]{:S(2)}) copy-start(f32[2,128]{1,0:T(2,128)} %surf_ref.1) | copy-start | bytes 3076
  52.6 21.5 %copy-start.7 = (f32[40]{0:T(128)S(1)}, f32[40]{0:T(128)}, u32[]{:S(2)}) copy-start(f32[40]{0:T(128)} %param.20) | copy-start | bytes 484
  52.6 21.5 %collective-permute-start.3 = (bf16[2,8,160,128]{3,2,1,0:T(8,128)(2,1)S(1)}, bf16[2,8,160,128]{3,2,1,0:T(8,128)(2,1)S(1)}, u32[]{:S(2)}, u32[]{:S(2)}) collective-permute-start(bf16[2,8,160,128]{3,2,1,0:T(8,128)(2,1)S(1)} %shard_map.113.own_ref), channel_id=1, source_target_pairs={{1,2},{2,1},{3,4},{4,3},{5,6},{6,5},{7,8},{8,7},{9,10},{10,9},{11,... | collective-permute-start | bytes 1966088 | tf_op jit(solution)/shard_map/ppermute | solution.py:446
  55.8 18.2 %collective-permute-start.2 = (bf16[2,8,160,128]{3,2,1,0:T(8,128)(2,1)S(1)}, bf16[2,8,160,128]{3,2,1,0:T(8,128)(2,1)S(1)}, u32[]{:S(2)}, u32[]{:S(2)}) collective-permute-start(bf16[2,8,160,128]{3,2,1,0:T(8,128)(2,1)S(1)} %shard_map.113.own_ref), channel_id=1, source_target_pairs={{0,1},{1,0},{2,3},{3,2},{4,5},{5,4},{6,7},{7,6},{8,9},{9,8},{10,11... | collective-permute-start | bytes 1966088 | tf_op jit(solution)/shard_map/ppermute | solution.py:446
